TPU v7x, 32 devices: a whole 2x2x4 slice. The times are simulated.
32 devices in a mesh: rep: 8 (over y, x, core), shard: 4 (over z).
Axes of the slice: x: 2, y: 2, z: 4, core: 2. Of those that a mesh axis runs over, the one named last changes fastest.
Arguments:
- block_input: bfloat16 [32, 384, 576], P(('rep', 'shard')), may hold values from -6 to 6
- segment_ids: int32 [32, 384], P(('rep', 'shard')), may hold values from 0 to 383, as said below
- positions: int32 [32, 384], P(('rep', 'shard')), may hold values from 0 to 383, as said below
- query_weight: bfloat16 [576, 576], P('shard'), may hold values from -0.25 to 0.25
- key_weight: bfloat16 [576, 192], P('shard'), may hold values from -0.25 to 0.25
- value_weight: bfloat16 [576, 192], P('shard'), may hold values from -0.25 to 0.25
- output_weight: bfloat16 [576, 576], P('shard'), may hold values from -0.75 to 0.75
- gate_weight: bfloat16 [576, 1536], P('shard'), may hold values from -0.25 to 0.25
- up_weight: bfloat16 [576, 1536], P('shard'), may hold values from -0.25 to 0.25
- down_weight: bfloat16 [1536, 576], P('shard'), may hold values from -0.15625 to 0.15625
- gain_attn: bfloat16 [576], P('shard'), may hold values from 0.5 to 1.5
- gain_mlp: bfloat16 [576], P('shard'), may hold values from 0.5 to 1.5
- layer_output_cotangent: bfloat16 [32, 384, 576], P(('rep', 'shard')), may hold values from -6 to 6
Outputs:
- block_output: bfloat16 [32, 384, 576], P(('rep', 'shard'))
- input_grad: float32 [32, 384, 576], P(('rep', 'shard'))
- grad_query: float32 [576, 576], P('shard')
- grad_key: float32 [576, 192], P('shard')
- grad_value: float32 [576, 192], P('shard')
- grad_output: float32 [576, 576], P('shard')
- grad_gate: float32 [576, 1536], P('shard')
- grad_up: float32 [576, 1536], P('shard')
- grad_down: float32 [1536, 576], P('shard')
- grad_gain_attn: float32 [576], P('shard')
- grad_gain_mlp: float32 [576], P('shard')
Inputs may be any that keep to these rules, and one draw needn't show every extreme that they name: `segment_ids`: in each row the ids start at 0, never fall and rise by at most one from token to token. `positions`: 0 at the first token of a segment, rising by one within it.
All inputs are finite; a program needn't handle non-finite values.
Results may differ from a plain program's by a relative error of at most 0.012.
The roundings to bfloat16 on the way count: a program that leaves them out, or rounds other values in their place, can miss the bound.
Values may be sent and summed in bfloat16 or wider, within the bound.
No kernel may reach another device: no remote copies, remote signals or barrier semaphores. Data moves between devices by JAX's collectives and lax.ppermute only.
A program may use at most 128 MiB of HBM per device.

v0:
```python
import jax
import jax.numpy as jnp
from jax import lax
from jax.experimental import pallas as pl
from jax.experimental.pallas import tpu as pltpu
from jax.sharding import PartitionSpec as P

QUERY_HEADS = 9
KEY_VALUE_HEADS = 3
HEAD_WIDTH = 64


EPSILON = 1e-05
ROPE_BASE = 100000.0


def product_term(pattern, left_op, right_op):
    return jnp.einsum(pattern, left_op, right_op, preferred_element_type=jnp.float32)


def norm_stats(values):
    inverse = lax.rsqrt(jnp.mean(values * values, axis=-1, keepdims=True) + EPSILON)
    return (inverse, values * inverse)


def rope_tables(positions):
    half_dim = HEAD_WIDTH // 2
    frequency = ROPE_BASE ** (-(jnp.arange(half_dim, dtype=jnp.float32) * 2.0 / HEAD_WIDTH))
    angles = positions.astype(jnp.float32)[:, :, None] * frequency
    return (jnp.cos(angles)[:, :, None, :], jnp.sin(angles)[:, :, None, :])


def rotate(tensor, cosine_table, sine_table, direction):
    half_dim = HEAD_WIDTH // 2
    first_half = tensor[..., :half_dim]
    second_half = tensor[..., half_dim:]
    return jnp.concatenate(
        [
            first_half * cosine_table - direction * second_half * sine_table,
            second_half * cosine_table + direction * first_half * sine_table,
        ],
        axis=-1,
    )


def attention_mask(segment_ids):
    indices = jnp.arange(segment_ids.shape[1])
    causal = indices[:, None] >= indices[None, :]
    same_doc = segment_ids[:, :, None] == segment_ids[:, None, :]
    return (causal[None] & same_doc)[:, None, None]


def score_block(q_rot, k_rot, allowed):
    scores = product_term("sqgrh,skgh->sgrqk", q_rot, k_rot) * HEAD_WIDTH ** (-0.5)
    return jnp.where(allowed, scores, -1e30)


def forward_pass(weights, block_input, segment_ids, positions):
    (
        query_weight,
        key_weight,
        value_weight,
        output_weight,
        gate_weight,
        up_weight,
        down_weight,
        gain_attn,
        gain_mlp,
    ) = weights
    sequence_count, sequence_length, width = block_input.shape
    group_size = QUERY_HEADS // KEY_VALUE_HEADS
    q_width = QUERY_HEADS * HEAD_WIDTH
    residual_input = block_input.astype(jnp.float32)
    inv_attn, unit_attn = norm_stats(residual_input)
    attention_normalized = (unit_attn * gain_attn.astype(jnp.float32)).astype(jnp.bfloat16)
    cosine_table, sine_table = rope_tables(positions)
    query_projected = product_term("ifw,wq->ifq", attention_normalized, query_weight).reshape(
        sequence_count, sequence_length, QUERY_HEADS, HEAD_WIDTH
    )
    key_projected = product_term("ifw,wq->ifq", attention_normalized, key_weight).reshape(
        sequence_count, sequence_length, KEY_VALUE_HEADS, HEAD_WIDTH
    )
    value_projected = product_term("ifw,wq->ifq", attention_normalized, value_weight).reshape(
        sequence_count, sequence_length, KEY_VALUE_HEADS, HEAD_WIDTH
    )
    q_rot = rotate(query_projected, cosine_table, sine_table, 1.0).astype(jnp.bfloat16)
    q_rot = q_rot.reshape(sequence_count, sequence_length, KEY_VALUE_HEADS, group_size, HEAD_WIDTH)
    k_rot = rotate(key_projected, cosine_table, sine_table, 1.0).astype(jnp.bfloat16)
    value_b = value_projected.astype(jnp.bfloat16)
    allowed = attention_mask(segment_ids)
    scores = score_block(q_rot, k_rot, allowed)
    row_max = jnp.max(scores, axis=-1, keepdims=True)
    log_total = row_max + jnp.log(jnp.sum(jnp.exp(scores - row_max), axis=-1, keepdims=True))
    attn_probs = jnp.exp(scores - log_total).astype(jnp.bfloat16)
    attention_merged = (
        product_term("sgrqk,skgh->sqgrh", attn_probs, value_b)
        .reshape(sequence_count, sequence_length, q_width)
        .astype(jnp.bfloat16)
    )
    residual_middle = residual_input + product_term("gwb,ba->gwa", attention_merged, output_weight)
    inv_mlp, unit_mlp = norm_stats(residual_middle)
    feedforward_normalized = (unit_mlp * gain_mlp.astype(jnp.float32)).astype(jnp.bfloat16)
    gate_projected = product_term("qbg,gh->qbh", feedforward_normalized, gate_weight)
    up_projected = product_term("qbg,gh->qbh", feedforward_normalized, up_weight)
    hidden_state = (jax.nn.silu(gate_projected) * up_projected).astype(jnp.bfloat16)
    layer_result = residual_middle + product_term("jbw,wg->jbg", hidden_state, down_weight)
    stored = (
        inv_attn,
        unit_attn,
        attention_normalized,
        q_rot,
        k_rot,
        value_b,
        log_total,
        attention_merged,
        inv_mlp,
        unit_mlp,
        feedforward_normalized,
        gate_projected,
        up_projected,
        hidden_state,
    )
    return (layer_result, stored)


def backward_mlp(weights, layer_output_cotangent, stored):
    (
        query_weight,
        key_weight,
        value_weight,
        output_weight,
        gate_weight,
        up_weight,
        down_weight,
        gain_attn,
        gain_mlp,
    ) = weights
    inv_mlp, unit_mlp, feedforward_normalized, gate_projected, up_projected, hidden_state = stored[
        8:
    ]
    grad_out = layer_output_cotangent.astype(jnp.float32)
    activation_cotangent = product_term("zeo,ho->zeh", layer_output_cotangent, down_weight)
    down_weight_gradient = product_term("bux,bue->xe", layer_output_cotangent, hidden_state)
    gate_sigmoid = jax.nn.sigmoid(gate_projected)
    gate_cotangent = (
        activation_cotangent
        * up_projected
        * gate_sigmoid
        * (1.0 + gate_projected * (1.0 - gate_sigmoid))
    ).astype(jnp.bfloat16)
    up_cotangent = (activation_cotangent * gate_projected * gate_sigmoid).astype(jnp.bfloat16)
    gate_weight_gradient = product_term("avq,avc->qc", feedforward_normalized, gate_cotangent)
    up_weight_gradient = product_term("avq,avc->qc", feedforward_normalized, up_cotangent)
    normalized_cotangent = product_term("abo,mo->abm", gate_cotangent, gate_weight) + product_term(
        "abo,mo->abm", up_cotangent, up_weight
    )
    g_gain = jnp.sum(normalized_cotangent * unit_mlp, axis=(0, 1))
    d_unit = normalized_cotangent * gain_mlp.astype(jnp.float32)
    grad_mid = grad_out + inv_mlp * (
        d_unit - unit_mlp * jnp.mean(d_unit * unit_mlp, axis=-1, keepdims=True)
    )
    return (grad_mid, (gate_weight_gradient, up_weight_gradient, down_weight_gradient, g_gain))


def backward_attention(weights, segment_ids, positions, stored, grad_mid):
    (
        query_weight,
        key_weight,
        value_weight,
        output_weight,
        gate_weight,
        up_weight,
        down_weight,
        gain_attn,
        gain_mlp,
    ) = weights
    (
        inv_attn,
        unit_attn,
        attention_normalized,
        q_rot,
        k_rot,
        value_b,
        log_total,
        attention_merged,
    ) = stored[:8]
    sequence_count, sequence_length, width = grad_mid.shape
    group_size = QUERY_HEADS // KEY_VALUE_HEADS
    q_width = QUERY_HEADS * HEAD_WIDTH
    kv_width = KEY_VALUE_HEADS * HEAD_WIDTH
    block_gradient = grad_mid.astype(jnp.bfloat16)
    output_weight_gradient = product_term("uvc,uvn->cn", attention_merged, block_gradient)
    merged_cotangent = product_term("nuw,vw->nuv", block_gradient, output_weight).astype(
        jnp.bfloat16
    )
    merged_cotangent = merged_cotangent.reshape(
        sequence_count, sequence_length, KEY_VALUE_HEADS, group_size, HEAD_WIDTH
    )
    allowed = attention_mask(segment_ids)
    scores = score_block(q_rot, k_rot, allowed)
    attn_probs = jnp.exp(scores - log_total)
    d_value = product_term("sgrqk,sqgrh->skgh", attn_probs.astype(jnp.bfloat16), merged_cotangent)
    d_prob = product_term("sqgrh,skgh->sgrqk", merged_cotangent, value_b)
    mixed_heads = attention_merged.reshape(
        sequence_count, sequence_length, KEY_VALUE_HEADS, group_size, HEAD_WIDTH
    )
    row_delta = jnp.sum(
        merged_cotangent.astype(jnp.float32) * mixed_heads.astype(jnp.float32), axis=-1
    )
    row_delta = jnp.transpose(row_delta, (0, 2, 3, 1))[..., None]
    d_score = (attn_probs * (d_prob - row_delta) * HEAD_WIDTH ** (-0.5)).astype(jnp.bfloat16)
    d_query = product_term("sgrqk,skgh->sqgrh", d_score, k_rot).reshape(
        sequence_count, sequence_length, QUERY_HEADS, HEAD_WIDTH
    )
    d_key = product_term("sgrqk,sqgrh->skgh", d_score, q_rot)
    cosine_table, sine_table = rope_tables(positions)
    query_block_cotangent = (
        rotate(d_query, cosine_table, sine_table, -1.0)
        .astype(jnp.bfloat16)
        .reshape(sequence_count, sequence_length, q_width)
    )
    key_block_cotangent = (
        rotate(d_key, cosine_table, sine_table, -1.0)
        .astype(jnp.bfloat16)
        .reshape(sequence_count, sequence_length, kv_width)
    )
    value_block_cotangent = d_value.astype(jnp.bfloat16).reshape(
        sequence_count, sequence_length, kv_width
    )
    query_weight_gradient = product_term("uxj,uxc->jc", attention_normalized, query_block_cotangent)
    key_weight_gradient = product_term("uxj,uxc->jc", attention_normalized, key_block_cotangent)
    value_weight_gradient = product_term("uxj,uxc->jc", attention_normalized, value_block_cotangent)
    normalized_cotangent = (
        product_term("vcm,tm->vct", query_block_cotangent, query_weight)
        + product_term("vcm,tm->vct", key_block_cotangent, key_weight)
        + product_term("vcm,tm->vct", value_block_cotangent, value_weight)
    )
    g_gain = jnp.sum(normalized_cotangent * unit_attn, axis=(0, 1))
    d_unit = normalized_cotangent * gain_attn.astype(jnp.float32)
    grad_in = grad_mid + inv_attn * (
        d_unit - unit_attn * jnp.mean(d_unit * unit_attn, axis=-1, keepdims=True)
    )
    return (
        grad_in,
        (
            query_weight_gradient,
            key_weight_gradient,
            value_weight_gradient,
            output_weight_gradient,
            g_gain,
        ),
    )


def shifted(values, steps):
    size = lax.axis_size("shard")
    return lax.ppermute(values, "shard", [(i, (i + steps) % size) for i in range(size)])


def piece_of(block):
    copies = lax.axis_size("rep")
    me = lax.axis_index("rep")
    rows, columns = block.shape[0] // 2, block.shape[1] // (copies // 2)
    return lax.dynamic_slice(block, ((me % 2) * rows, (me // 2) * columns), (rows, columns))


def row_piece_of(block):
    copies = lax.axis_size("rep")
    rows = block.shape[0] // copies
    return lax.dynamic_slice_in_dim(block, lax.axis_index("rep") * rows, rows, 0)


def fetch_others(piece):
    size = lax.axis_size("shard")
    return jnp.stack([shifted(piece, k) for k in range(1, size)])


def place_blocks(own, others):
    size = lax.axis_size("shard")
    me = lax.axis_index("shard")
    full = jnp.zeros((size,) + own.shape, own.dtype)
    full = lax.dynamic_update_index_in_dim(full, own, me, 0)
    for k in range(1, size):
        full = lax.dynamic_update_index_in_dim(full, others[k - 1], (me - k) % size, 0)
    return full.reshape((size * own.shape[0],) + own.shape[1:])


def join_pieces(gathered):
    copies = gathered.shape[0]
    lead, rows, columns = gathered.shape[1:]
    parts = gathered.reshape(copies // 2, 2, lead, rows, columns)
    return jnp.transpose(parts, (2, 1, 3, 0, 4)).reshape(lead, 2 * rows, copies // 2 * columns)


def split_pieces(full):
    size = lax.axis_size("shard")
    copies = lax.axis_size("rep")
    rows, columns = full.shape[0] // size // 2, full.shape[1] // (copies // 2)
    parts = full.astype(jnp.bfloat16).reshape(size, 2, rows, copies // 2, columns)
    return jnp.transpose(parts, (3, 1, 0, 2, 4)).reshape(copies, size, rows, columns)


def sum_over_shard(parts):
    size = lax.axis_size("shard")
    me = lax.axis_index("shard")
    total = lax.dynamic_index_in_dim(parts, me, 0, keepdims=False).astype(jnp.float32)
    for k in range(1, size):
        block = lax.dynamic_index_in_dim(parts, (me + k) % size, 0, keepdims=False)
        total = total + shifted(block, k).astype(jnp.float32)
    return total


def gather_weights(q, k, v, o, gate, up, down, gain_attn, gain_mlp):
    rows = q.shape[0]
    attn = jnp.concatenate([q, k, v, o], axis=1)
    attn_piece = piece_of(attn)
    gains = jnp.stack([gain_attn, gain_mlp])
    gains_pad = jnp.pad(gains, ((0, 6), (0, attn_piece.shape[1] - rows)))
    attn_others = fetch_others(jnp.concatenate([attn_piece, gains_pad]))
    half = attn_piece.shape[0]
    gains_full = place_blocks(gains, attn_others[:, half : half + 2, :rows])
    size = lax.axis_size("shard")
    gains_full = jnp.transpose(gains_full.reshape(size, 2, rows), (1, 0, 2)).reshape(2, size * rows)
    attn_gathered = lax.all_gather(attn_others[:, :half], "rep")
    attn_full = place_blocks(attn, join_pieces(attn_gathered))
    gate_piece = piece_of(gate)
    tall = jnp.transpose(down)
    tall_piece = row_piece_of(tall).reshape(gate_piece.shape)
    wide = jnp.stack([gate_piece, piece_of(up), tall_piece])
    wide_gathered = lax.all_gather(fetch_others(wide), "rep")
    gate_full = place_blocks(gate, join_pieces(wide_gathered[:, :, 0]))
    up_full = place_blocks(up, join_pieces(wide_gathered[:, :, 1]))
    tall_rows = jnp.transpose(wide_gathered[:, :, 2], (1, 0, 2, 3)).reshape((-1,) + tall.shape)
    down_full = jnp.transpose(place_blocks(down, jnp.transpose(tall_rows, (0, 2, 1))), (0, 1))
    a, b, c = q.shape[1], k.shape[1], v.shape[1]
    return (
        attn_full[:, :a],
        attn_full[:, a : a + b],
        attn_full[:, a + b : a + b + c],
        attn_full[:, a + b + c :],
        gate_full,
        up_full,
        down_full,
        gains_full[0],
        gains_full[1],
    )


def spread_pieces(piece):
    gathered = lax.all_gather(piece.astype(jnp.bfloat16), "rep")
    return join_pieces(gathered[:, None])[0].astype(jnp.float32)


def reduce_mlp(gate, up, tall):
    size = lax.axis_size("shard")
    copies = lax.axis_size("rep")
    gate_parts = split_pieces(gate)
    tall_parts = tall.astype(jnp.bfloat16).reshape(copies, tall.shape[0] // copies, size, -1)
    tall_parts = jnp.transpose(tall_parts, (0, 2, 1, 3))
    rows, columns = tall_parts.shape[2:]
    wide = jnp.stack([gate_parts, split_pieces(up), tall_parts.reshape(gate_parts.shape)], axis=2)
    shape = wide.shape[1:]
    wide = lax.psum_scatter(wide.reshape(-1, columns), "rep", scatter_dimension=0, tiled=True)
    wide = wide.reshape(shape)
    wide = sum_over_shard(wide).astype(jnp.bfloat16)
    wide = lax.all_gather(wide, "rep").astype(jnp.float32)
    tall_total = wide[:, 2].reshape(copies * rows, columns)
    return (
        join_pieces(wide[:, None, 0])[0],
        join_pieces(wide[:, None, 1])[0],
        jnp.transpose(tall_total),
    )


def reduce_attn(q, k, v, o, gain_attn, gain_mlp):
    size = lax.axis_size("shard")
    copies = lax.axis_size("rep")
    parts = split_pieces(jnp.concatenate([q, k, v, o], axis=1))
    half, columns = parts.shape[2:]
    gains = jnp.stack([gain_attn, gain_mlp]).reshape(2, size, -1).astype(jnp.bfloat16)
    rows = gains.shape[2]
    gains = jnp.pad(jnp.transpose(gains, (1, 0, 2)), ((0, 0), (0, 6), (0, columns - rows)))
    gains = jnp.broadcast_to(gains[None], (copies,) + gains.shape)
    parts = lax.psum_scatter(jnp.concatenate([parts, gains], axis=2), "rep", scatter_dimension=0)
    total = sum_over_shard(parts)
    full = spread_pieces(total[:half])
    a, b, c = q.shape[1], k.shape[1], v.shape[1]
    return (
        full[:, :a],
        full[:, a : a + b],
        full[:, a + b : a + b + c],
        full[:, a + b + c :],
        total[half, :rows],
        total[half + 1, :rows],
    )


def on_device_generic(
    block_input,
    segment_ids,
    positions,
    query_weight,
    key_weight,
    value_weight,
    output_weight,
    gate_weight,
    up_weight,
    down_weight,
    gain_attn,
    gain_mlp,
    layer_output_cotangent,
):
    weights = gather_weights(
        query_weight,
        key_weight,
        value_weight,
        output_weight,
        gate_weight,
        up_weight,
        down_weight,
        gain_attn,
        gain_mlp,
    )
    layer_result, stored = forward_pass(weights, block_input, segment_ids, positions)
    grad_mid, mlp_grads = backward_mlp(weights, layer_output_cotangent, stored)
    gate_total, up_total, down_total = reduce_mlp(*mlp_grads[:3])
    grad_in, attn_grads = backward_attention(weights, segment_ids, positions, stored, grad_mid)
    q_total, k_total, v_total, o_total, gain_attn_total, gain_mlp_total = reduce_attn(
        *attn_grads, mlp_grads[3]
    )
    return (
        layer_result.astype(jnp.bfloat16),
        grad_in,
        q_total,
        k_total,
        v_total,
        o_total,
        gate_total,
        up_total,
        down_total,
        gain_attn_total,
        gain_mlp_total,
    )


TOKENS = 384
CHUNK = 384
GROUPS = KEY_VALUE_HEADS
SHARE = QUERY_HEADS // KEY_VALUE_HEADS
VMEM_LIMIT = 56 * 1024 * 1024


def dot(left, right, left_dim=1, right_dim=0):
    return lax.dot_general(
        left, right, (((left_dim,), (right_dim,)), ((), ())), preferred_element_type=jnp.float32
    )


def widen(values):
    return values.astype(jnp.float32)


def narrow(values):
    return values.astype(jnp.bfloat16)


def mask_bias(seg_col, seg_row):
    shape = (TOKENS, TOKENS)
    key_at = lax.broadcasted_iota(jnp.int32, shape, 0)
    query_at = lax.broadcasted_iota(jnp.int32, shape, 1)
    allowed = (key_at <= query_at) & (seg_col == seg_row)
    return jnp.where(allowed, 0.0, -1e30)


def turn(values, cosine, sine):
    half = HEAD_WIDTH // 2
    first, second = values[:half], values[half:]
    return jnp.concatenate(
        [first * cosine - second * sine, second * cosine + first * sine], axis=0
    )


def attention_forward_kernel(
    shards, z_ref, x_ref, col_ref, row_ref, cos_ref, sin_ref, own_ref, gain_own_ref, others_ref,
    w_ref, gain_ref, x2_ref, q_ref, k_ref, v_ref, o_ref, lse_ref, bias_ref,
):
    z = z_ref[0]
    rows = own_ref.shape[0]
    half = rows // 2
    width = x_ref.shape[1]
    own_at = pl.multiple_of(z * rows, 16)
    w_ref[pl.ds(own_at, rows), :] = own_ref[...]
    gains = widen(gain_own_ref[...])
    for k in range(1, shards):
        at = pl.multiple_of(lax.rem(z + shards - k, shards) * rows, 16)
        gains = gains + widen(others_ref[0, k - 1, half:])
        for c in range(own_ref.shape[1] // CHUNK):
            pieces = [widen(others_ref[2 * c + h, k - 1, :half]) for h in range(2)]
            w_ref[pl.ds(at, rows), c * CHUNK : (c + 1) * CHUNK] = narrow(
                jnp.concatenate(pieces, axis=0)
            )
    tail = width - CHUNK
    gain_attn = jnp.concatenate([gains[0:1], gains[1:2, :tail]], axis=1)
    gain_mlp = jnp.concatenate([gains[2:3], gains[3:4, :tail]], axis=1)
    gain_ref[0:1, :] = gain_attn
    gain_ref[1:2, :] = gain_mlp
    x = widen(x_ref[...])
    inverse = lax.rsqrt(jnp.mean(x * x, axis=-1, keepdims=True) + EPSILON)
    h1 = narrow(x * inverse * gain_attn)
    kv = jnp.transpose(dot(h1, w_ref[:, :CHUNK]))
    q = jnp.transpose(dot(h1, w_ref[:, 896:]))[HEAD_WIDTH:]
    cosine, sine = cos_ref[...], sin_ref[...]
    bias_ref[...] = mask_bias(col_ref[...], row_ref[...])
    for g in range(GROUPS):
        at = g * HEAD_WIDTH
        k_ref[g] = narrow(turn(kv[at : at + HEAD_WIDTH], cosine, sine))
        at = (GROUPS + g) * HEAD_WIDTH
        v_ref[g] = narrow(kv[at : at + HEAD_WIDTH])
        for r in range(SHARE):
            at = (g * SHARE + r) * HEAD_WIDTH
            q_ref[g, :, r * TOKENS : (r + 1) * TOKENS] = narrow(
                turn(q[at : at + HEAD_WIDTH], cosine, sine)
            )

    def one_group(g, carry):
        scores = dot(k_ref[g], q_ref[g], 0, 0) * HEAD_WIDTH ** (-0.5)
        bias = bias_ref[...]
        scores = scores + jnp.concatenate([bias] * SHARE, axis=1)
        top = jnp.max(scores, axis=0, keepdims=True)
        weight = jnp.exp(scores - top)
        total = jnp.sum(weight, axis=0, keepdims=True)
        lse_ref[g] = top + jnp.log(total)
        probs = narrow(weight * (1.0 / total))
        o_ref[g] = narrow(dot(v_ref[g], probs))
        return carry

    lax.fori_loop(0, GROUPS, one_group, 0)
    x2_ref[...] = x + dot(joined_heads(o_ref), w_ref[:, CHUNK : CHUNK + width], 0, 0)


def joined_heads(ref):
    return jnp.concatenate(
        [
            ref[g, :, r * TOKENS : (r + 1) * TOKENS]
            for g in range(GROUPS)
            for r in range(SHARE)
        ],
        axis=0,
    )


def attention_forward(z, x, col, row, cosine, sine, own, gain_own, others, shards):
    width = x.shape[1]
    cells = SHARE * TOKENS
    bf16, f32 = jnp.bfloat16, jnp.float32

    def kernel(*refs):
        attention_forward_kernel(shards, *refs)

    return pl.pallas_call(
        kernel,
        grid_spec=pltpu.PrefetchScalarGridSpec(
            num_scalar_prefetch=1,
            grid=(),
            in_specs=[pl.BlockSpec(memory_space=pltpu.VMEM)] * 8,
            out_specs=[pl.BlockSpec(memory_space=pltpu.VMEM)] * 8,
            scratch_shapes=[pltpu.VMEM((TOKENS, TOKENS), f32)],
        ),
        out_shape=[
            jax.ShapeDtypeStruct((shards * own.shape[0], own.shape[1]), bf16),
            jax.ShapeDtypeStruct((8, width), f32),
            jax.ShapeDtypeStruct((TOKENS, width), f32),
            jax.ShapeDtypeStruct((GROUPS, HEAD_WIDTH, cells), bf16),
            jax.ShapeDtypeStruct((GROUPS, HEAD_WIDTH, TOKENS), bf16),
            jax.ShapeDtypeStruct((GROUPS, HEAD_WIDTH, TOKENS), bf16),
            jax.ShapeDtypeStruct((GROUPS, HEAD_WIDTH, cells), bf16),
            jax.ShapeDtypeStruct((GROUPS, 1, cells), f32),
        ],
        compiler_params=pltpu.CompilerParams(vmem_limit_bytes=VMEM_LIMIT),
        cost_estimate=pl.CostEstimate(
            flops=int(1.5e9), bytes_accessed=8000000, transcendentals=2000000
        ),
        name="attention_forward",
    )(z, x, col, row, cosine, sine, own, gain_own, others)


def mlp_kernel(
    shards, z_ref, x2_ref, ct_ref, gain_ref, gate_ref, up_ref, tall_ref, wide_ref, tall_other_ref,
    out_ref, dx2_ref, gain_grad_ref, grad_ref,
    u2_ref, h2_ref, h2t_ref, ctt_ref, acc_ref, dh2_ref, wg_ref, wu_ref, wd_ref,
):
    z = z_ref[0]
    j = pl.program_id(0)
    rows = gate_ref.shape[0]
    half = rows // 2

    @pl.when(j == 0)
    def _():
        x2 = x2_ref[...]
        inverse = lax.rsqrt(jnp.mean(x2 * x2, axis=-1, keepdims=True) + EPSILON)
        u2 = x2 * inverse
        u2_ref[...] = u2
        h2 = narrow(u2 * gain_ref[1:2, :])
        h2_ref[...] = h2
        h2t_ref[...] = narrow(jnp.transpose(widen(h2)))
        ctt_ref[...] = narrow(jnp.transpose(widen(ct_ref[...])))
        acc_ref[...] = x2
        dh2_ref[...] = jnp.zeros_like(dh2_ref)

    own_at = pl.multiple_of(z * rows, 16)
    wg_ref[pl.ds(own_at, rows), :] = gate_ref[...]
    wu_ref[pl.ds(own_at, rows), :] = up_ref[...]
    for k in range(1, shards):
        at = pl.multiple_of(lax.rem(z + shards - k, shards) * rows, 16)
        for m, ref in ((0, wg_ref), (1, wu_ref)):
            pieces = [widen(wide_ref[h, k - 1, m]) for h in range(2)]
            ref[pl.ds(at, rows), :] = narrow(jnp.concatenate(pieces, axis=0))

    @pl.when(j == z)
    def _():
        wd_ref[...] = tall_ref[...]

    @pl.when(j != z)
    def _():
        pieces = [widen(tall_other_ref[r, 0, 0]) for r in range(tall_other_ref.shape[0])]
        wd_ref[...] = narrow(jnp.concatenate(pieces, axis=0))

    h2, ct = h2_ref[...], ct_ref[...]
    wg, wu, wd = wg_ref[...], wu_ref[...], wd_ref[...]
    gate, up = dot(h2, wg), dot(h2, wu)
    da = dot(ct, wd)
    sigmoid = 1.0 / (1.0 + jnp.exp(-gate))
    silu = gate * sigmoid
    act = narrow(silu * up)
    dg = narrow(da * up * sigmoid * (1.0 + gate * (1.0 - sigmoid)))
    du = narrow(da * silu)
    acc_ref[...] += dot(act, wd, 1, 1)
    dh2_ref[...] += dot(dg, wg, 1, 1) + dot(du, wu, 1, 1)
    for m, grad in ((0, dot(h2t_ref[...], dg)), (1, dot(h2t_ref[...], du))):
        for b in range(shards):
            for h in range(2):
                at = b * rows + h * half
                grad_ref[2 * j + h, b, m] = narrow(grad[at : at + half])
    grad = dot(ctt_ref[...], act)
    for r in range(2 * shards):
        grad_ref[r, j, 2] = narrow(grad[r * half : (r + 1) * half])

    @pl.when(j == pl.num_programs(0) - 1)
    def _():
        out_ref[...] = narrow(acc_ref[...])
        dh2, u2, x2 = dh2_ref[...], u2_ref[...], x2_ref[...]
        inverse = lax.rsqrt(jnp.mean(x2 * x2, axis=-1, keepdims=True) + EPSILON)
        gain_grad_ref[0:1, :] = jnp.sum(dh2 * u2, axis=0, keepdims=True)
        n2 = dh2 * gain_ref[1:2, :]
        mean = jnp.mean(n2 * u2, axis=-1, keepdims=True)
        dx2_ref[...] = widen(ct_ref[...]) + inverse * (n2 - u2 * mean)


def mlp(z, x2, ct, gains, gate, up, tall, gathered, shards):
    width = x2.shape[1]
    copies = gathered.shape[0]
    rows, ff = gate.shape
    half = rows // 2
    bf16, f32 = jnp.bfloat16, jnp.float32

    def kernel(*refs):
        mlp_kernel(shards, *refs)

    def tall_block(j, z_ref):
        return (0, jnp.maximum(lax.rem(z_ref[0] + shards - j, shards) - 1, 0), 2, 0, 0)

    whole = lambda shape: pl.BlockSpec(shape, lambda j, z_ref: (0,) * len(shape))
    return pl.pallas_call(
        kernel,
        grid_spec=pltpu.PrefetchScalarGridSpec(
            num_scalar_prefetch=1,
            grid=(ff // CHUNK,),
            in_specs=[
                whole((TOKENS, width)),
                whole((TOKENS, width)),
                whole((8, width)),
                pl.BlockSpec((rows, CHUNK), lambda j, z_ref: (0, j)),
                pl.BlockSpec((rows, CHUNK), lambda j, z_ref: (0, j)),
                whole((width, CHUNK)),
                pl.BlockSpec((2, shards - 1, 2, half, CHUNK), lambda j, z_ref: (j, 0, 0, 0, 0)),
                pl.BlockSpec((copies, 1, 1, half, CHUNK), tall_block),
            ],
            out_specs=[
                whole((TOKENS, width)),
                whole((TOKENS, width)),
                whole((8, width)),
                whole((copies, shards, 3, half, CHUNK)),
            ],
            scratch_shapes=[
                pltpu.VMEM((TOKENS, width), f32),
                pltpu.VMEM((TOKENS, width), bf16),
                pltpu.VMEM((width, TOKENS), bf16),
                pltpu.VMEM((width, TOKENS), bf16),
                pltpu.VMEM((TOKENS, width), f32),
                pltpu.VMEM((TOKENS, width), f32),
                pltpu.VMEM((width, CHUNK), bf16),
                pltpu.VMEM((width, CHUNK), bf16),
                pltpu.VMEM((width, CHUNK), bf16),
            ],
        ),
        out_shape=[
            jax.ShapeDtypeStruct((TOKENS, width), bf16),
            jax.ShapeDtypeStruct((TOKENS, width), f32),
            jax.ShapeDtypeStruct((8, width), f32),
            jax.ShapeDtypeStruct((copies, shards, 3, half, CHUNK), bf16),
        ],
        compiler_params=pltpu.CompilerParams(
            vmem_limit_bytes=VMEM_LIMIT, dimension_semantics=("arbitrary",)
        ),
        cost_estimate=pl.CostEstimate(
            flops=int(6.2e9), bytes_accessed=14000000, transcendentals=1200000
        ),
        name="mlp",
    )(z, x2, ct, gains, gate, up, tall, gathered, gathered)


def attention_backward_kernel(
    shards, x_ref, dx2_ref, col_ref, row_ref, cos_ref, sin_ref, w_ref, gain_ref, q_ref, k_ref,
    v_ref, o_ref, lse_ref, gain_grad_ref,
    dx_ref, grad_ref,
    bias_ref, do_ref, dq_ref, dk_ref, dv_ref,
):
    width = x_ref.shape[1]
    rows = width // shards
    half = rows // 2
    x = widen(x_ref[...])
    inverse = lax.rsqrt(jnp.mean(x * x, axis=-1, keepdims=True) + EPSILON)
    u1 = x * inverse
    gain_attn = gain_ref[0:1, :]
    h1t = narrow(jnp.transpose(u1 * gain_attn))
    gx = narrow(dx2_ref[...])
    cosine, sine = cos_ref[...], sin_ref[...]
    bias_ref[...] = mask_bias(col_ref[...], row_ref[...])
    do = narrow(dot(w_ref[:, CHUNK : CHUNK + width], gx, 1, 1))
    for g in range(GROUPS):
        for r in range(SHARE):
            at = (g * SHARE + r) * HEAD_WIDTH
            do_ref[g, :, r * TOKENS : (r + 1) * TOKENS] = do[at : at + HEAD_WIDTH]

    def one_group(g, carry):
        bias = bias_ref[...]
        scores = dot(k_ref[g], q_ref[g], 0, 0) * HEAD_WIDTH ** (-0.5)
        scores = scores + jnp.concatenate([bias] * SHARE, axis=1)
        probs = jnp.exp(scores - lse_ref[g])
        do_g = do_ref[g]
        dv_ref[g] = jnp.transpose(dot(narrow(probs), do_g, 1, 1))
        delta = jnp.sum(widen(do_g) * widen(o_ref[g]), axis=0, keepdims=True)
        dp = dot(v_ref[g], do_g, 0, 0)
        ds = narrow(probs * (dp - delta) * HEAD_WIDTH ** (-0.5))
        dq_ref[g] = dot(k_ref[g], ds)
        dk_ref[g] = jnp.transpose(dot(ds, q_ref[g], 1, 1))
        return carry

    lax.fori_loop(0, GROUPS, one_group, 0)
    dkv = [narrow(turn(dk_ref[g], cosine, -sine)) for g in range(GROUPS)]
    dkv = jnp.concatenate(dkv + [narrow(dv_ref[g]) for g in range(GROUPS)], axis=0)
    dq = [
        narrow(turn(dq_ref[g, :, r * TOKENS : (r + 1) * TOKENS], cosine, -sine))
        for g in range(GROUPS)
        for r in range(SHARE)
    ]
    zeros = jnp.zeros((HEAD_WIDTH, TOKENS), jnp.bfloat16)
    dq_padded = jnp.concatenate([zeros] + dq, axis=0)
    dq = jnp.concatenate(dq, axis=0)
    dh1 = jnp.transpose(dot(w_ref[:, :CHUNK], dkv) + dot(w_ref[:, 896:], dq_padded))
    gain_grad = jnp.sum(dh1 * u1, axis=0, keepdims=True)
    n1 = dh1 * gain_attn
    mean = jnp.mean(n1 * u1, axis=-1, keepdims=True)
    dx_ref[...] = dx2_ref[...] + inverse * (n1 - u1 * mean)
    gain_mlp_grad = gain_grad_ref[0:1, :]
    tail = width - CHUNK
    blank = jnp.zeros((1, CHUNK - tail), jnp.float32)
    extra = jnp.concatenate(
        [
            gain_grad[:, :CHUNK],
            jnp.concatenate([gain_grad[:, CHUNK:], blank], axis=1),
            gain_mlp_grad[:, :CHUNK],
            jnp.concatenate([gain_mlp_grad[:, CHUNK:], blank], axis=1),
            jnp.zeros((4, CHUNK), jnp.float32),
        ],
        axis=0,
    )
    o = joined_heads(o_ref)
    for c in range(4):
        if c == 0:
            grad = dot(h1t, dkv, 1, 1)
        elif c == 1:
            grad = dot(o, gx[:, :CHUNK])
        elif c == 2:
            grad = jnp.concatenate(
                [dot(o, gx[:, CHUNK:]), dot(h1t, dq[: CHUNK - tail], 1, 1)], axis=1
            )
        else:
            grad = dot(h1t, dq[CHUNK - tail :], 1, 1)
        for b in range(shards):
            for h in range(2):
                at = b * rows + h * half
                grad_ref[2 * c + h, b] = narrow(
                    jnp.concatenate([grad[at : at + half], extra], axis=0)
                )


def attention_backward(args, shards, copies):
    x = args[0]
    width = x.shape[1]
    half = width // shards // 2
    cells = SHARE * TOKENS
    bf16, f32 = jnp.bfloat16, jnp.float32

    def kernel(*refs):
        attention_backward_kernel(shards, *refs)

    return pl.pallas_call(
        kernel,
        in_specs=[pl.BlockSpec(memory_space=pltpu.VMEM)] * len(args),
        out_specs=[pl.BlockSpec(memory_space=pltpu.VMEM)] * 2,
        out_shape=[
            jax.ShapeDtypeStruct((TOKENS, width), f32),
            jax.ShapeDtypeStruct((copies, shards, half + 8, CHUNK), bf16),
        ],
        scratch_shapes=[
            pltpu.VMEM((TOKENS, TOKENS), f32),
            pltpu.VMEM((GROUPS, HEAD_WIDTH, cells), bf16),
            pltpu.VMEM((GROUPS, HEAD_WIDTH, cells), f32),
            pltpu.VMEM((GROUPS, HEAD_WIDTH, TOKENS), f32),
            pltpu.VMEM((GROUPS, HEAD_WIDTH, TOKENS), f32),
        ],
        compiler_params=pltpu.CompilerParams(vmem_limit_bytes=VMEM_LIMIT),
        cost_estimate=pl.CostEstimate(
            flops=int(3e9), bytes_accessed=9000000, transcendentals=1400000
        ),
        name="attention_backward",
    )(*args)


def unpack_attn_kernel(piece_ref, q_ref, k_ref, v_ref, o_ref):
    half = piece_ref.shape[1]
    columns = []
    for c in range(piece_ref.shape[0] // 2):
        columns.append(
            jnp.concatenate([widen(piece_ref[2 * c]), widen(piece_ref[2 * c + 1])], axis=0)
        )
    full = jnp.concatenate(columns, axis=1)
    kvw, width = k_ref.shape[1], o_ref.shape[1]
    k_ref[...] = full[:, :kvw]
    v_ref[...] = full[:, kvw : 2 * kvw]
    o_ref[...] = full[:, 2 * kvw : 2 * kvw + width]
    q_ref[...] = full[:, 2 * kvw + width :]


def unpack_attn(pieces, shapes):
    return pl.pallas_call(
        unpack_attn_kernel,
        out_shape=[jax.ShapeDtypeStruct(shape, jnp.float32) for shape in shapes],
        name="unpack_attn",
    )(pieces)


def unpack_mlp_kernel(piece_ref, gate_ref, up_ref, down_ref):
    half = piece_ref.shape[2]
    for c in range(piece_ref.shape[0] // 2):
        for h in range(2):
            for m, ref in ((0, gate_ref), (1, up_ref)):
                ref[h * half : (h + 1) * half, c * CHUNK : (c + 1) * CHUNK] = widen(
                    piece_ref[2 * c + h, m]
                )
    tall = [widen(piece_ref[r, 2]) for r in range(piece_ref.shape[0])]
    down_ref[...] = jnp.transpose(jnp.concatenate(tall, axis=0))


def unpack_mlp(pieces, shapes):
    return pl.pallas_call(
        unpack_mlp_kernel,
        out_shape=[jax.ShapeDtypeStruct(shape, jnp.float32) for shape in shapes],
        name="unpack_mlp",
    )(pieces)


def fits_kernels(block_input, query_weight, key_weight, gate_weight, down_weight):
    return (
        lax.axis_size("rep") == 8
        and lax.axis_size("shard") == 4
        and block_input.shape == (1, TOKENS, 576)
        and query_weight.shape == (144, 576)
        and key_weight.shape == (144, 192)
        and gate_weight.shape == (144, 1536)
        and down_weight.shape == (384, 576)
    )


def gain_rows(gain_attn, gain_mlp):
    rows = gain_attn.shape[0]
    size = lax.axis_size("shard")
    both = jnp.zeros((2, 2 * CHUNK), jnp.bfloat16)
    both = lax.dynamic_update_slice(
        both, jnp.stack([gain_attn, gain_mlp]), (0, lax.axis_index("shard") * rows)
    )
    return jnp.pad(both.reshape(4, CHUNK), ((0, 4), (0, 0)))


def on_device(
    block_input,
    segment_ids,
    positions,
    query_weight,
    key_weight,
    value_weight,
    output_weight,
    gate_weight,
    up_weight,
    down_weight,
    gain_attn,
    gain_mlp,
    layer_output_cotangent,
):
    if not fits_kernels(block_input, query_weight, key_weight, gate_weight, down_weight):
        return on_device_generic(
            block_input,
            segment_ids,
            positions,
            query_weight,
            key_weight,
            value_weight,
            output_weight,
            gate_weight,
            up_weight,
            down_weight,
            gain_attn,
            gain_mlp,
            layer_output_cotangent,
        )
    shards, copies = lax.axis_size("shard"), lax.axis_size("rep")
    z = lax.axis_index("shard").astype(jnp.int32).reshape(1)
    own = jnp.concatenate([key_weight, value_weight, output_weight, query_weight], axis=1)
    gains_own = gain_rows(gain_attn, gain_mlp)
    attn_others = fetch_others(jnp.concatenate([piece_of(own), gains_own]))
    attn_pieces = lax.all_gather(attn_others, "rep")
    tall = jnp.transpose(down_weight)
    wide = jnp.stack([piece_of(gate_weight), piece_of(up_weight), row_piece_of(tall)])
    wide_pieces = lax.all_gather(fetch_others(wide), "rep")

    half_dim = HEAD_WIDTH // 2
    frequency = ROPE_BASE ** (-(jnp.arange(half_dim, dtype=jnp.float32) * 2.0 / HEAD_WIDTH))
    angles = frequency[:, None] * positions.astype(jnp.float32)
    cosine, sine = jnp.cos(angles), jnp.sin(angles)
    row = segment_ids
    col = segment_ids.reshape(-1, 1)
    x = block_input[0]
    ct = layer_output_cotangent[0]

    w, gains, x2, q, k, v, o, lse = attention_forward(
        z, x, col, row, cosine, sine, own, gains_own, attn_pieces, shards
    )
    out, dx2, gain_mlp_grad, wide_grad = mlp(
        z, x2, ct, gains, gate_weight, up_weight, tall, wide_pieces, shards
    )
    half = gate_weight.shape[0] // 2
    wide_part = lax.psum_scatter(
        wide_grad.reshape(-1, CHUNK), "rep", scatter_dimension=0, tiled=True
    ).reshape(shards, 3, half, CHUNK)
    dx, attn_grad = attention_backward(
        (x, dx2, col, row, cosine, sine, w, gains, q, k, v, o, lse, gain_mlp_grad),
        shards,
        copies,
    )
    attn_part = lax.psum_scatter(
        attn_grad.reshape(-1, CHUNK), "rep", scatter_dimension=0, tiled=True
    ).reshape(shards, half + 8, CHUNK)
    wide_total = narrow(sum_over_shard(wide_part))
    gate_grad, up_grad, down_grad = unpack_mlp(
        lax.all_gather(wide_total, "rep"),
        (gate_weight.shape, up_weight.shape, down_weight.shape),
    )
    attn_total = sum_over_shard(attn_part)
    q_grad, k_grad, v_grad, o_grad = unpack_attn(
        lax.all_gather(narrow(attn_total[:half]), "rep"),
        (query_weight.shape, key_weight.shape, value_weight.shape, output_weight.shape),
    )
    both = attn_total[half : half + 4].reshape(2, 2 * CHUNK)
    rows = gain_attn.shape[0]
    both = lax.dynamic_slice(both, (0, lax.axis_index("shard") * rows), (2, rows))
    return (
        out[None],
        dx[None],
        q_grad,
        k_grad,
        v_grad,
        o_grad,
        gate_grad,
        up_grad,
        down_grad,
        both[0],
        both[1],
    )


def solution(mesh):
    placed = (
        P(("rep", "shard"), None, None),
        P(("rep", "shard"), None),
        P(("rep", "shard"), None),
        P("shard", None),
        P("shard", None),
        P("shard", None),
        P("shard", None),
        P("shard", None),
        P("shard", None),
        P("shard", None),
        P("shard"),
        P("shard"),
        P(("rep", "shard"), None, None),
    )
    return jax.shard_map(
        on_device,
        mesh=mesh,
        in_specs=placed,
        out_specs=(
            P(("rep", "shard"), None, None),
            P(("rep", "shard"), None, None),
            P("shard", None),
            P("shard", None),
            P("shard", None),
            P("shard", None),
            P("shard", None),
            P("shard", None),
            P("shard", None),
            P("shard"),
            P("shard"),
        ),
        check_vma=False,
    )
```

profile of v0, /device:TPU:0, one launch (start us, length us, event | category | flops | bytes accessed | tf_op | source)
XLA Modules:
  0.0 243.4 jit_solution(4380084656036900647)
XLA Ops:
  10.3 3.2 %collective-permute-start = (bf16[80,384]{1,0:T(8,128)(2,1)S(1)}, bf16[80,384]{1,0:T(8,128)(2,1)S(1)}, u32[]{:S(2)}, u32[]{:S(2)}) collective-permute-start(bf16[80,384]{1,0:T(8,128)(2,1)S(1)} %pad_maximum_fusion.3), channel_id=1, source_target_pairs={{0,1},{1,2},{2,3},{3,0},{4,5},{5,6},{6,7},{7,4},{8,9},{9,10},{10,1... | collective-permute-start | bytes 184328 | tf_op jit(solution)/shard_map/ppermute | solution.py:257
  13.5 2.6 %collective-permute-start.1 = (bf16[80,384]{1,0:T(8,128)(2,1)S(1)}, bf16[80,384]{1,0:T(8,128)(2,1)S(1)}, u32[]{:S(2)}, u32[]{:S(2)}) collective-permute-start(bf16[80,384]{1,0:T(8,128)(2,1)S(1)} %pad_maximum_fusion.3), channel_id=1, source_target_pairs={{0,2},{1,3},{2,0},{3,1},{4,6},{5,7},{6,4},{7,5},{8,10},{9,11},{10,... | collective-permute-start | bytes 184328 | tf_op jit(solution)/shard_map/ppermute | solution.py:257
  17.9 2.4 collective-permute-done.1
  24.6 2.1 collective-permute-start.4
  27.0 5.3 %collective-permute-done.3 = bf16[3,72,384]{2,1,0:T(8,128)(2,1)S(1)} collective-permute-done((bf16[3,72,384]{2,1,0:T(8,128)(2,1)S(1)}, bf16[3,72,384]{2,1,0:T(8,128)(2,1)S(1)}, u32[]{:S(2)}, u32[]{:S(2)}) %collective-permute-start.3) | collective-permute-done | bytes 165920 | tf_op jit(solution)/shard_map/ppermute | solution.py:257
  32.3 5.5 %collective-permute-done.4 = bf16[3,72,384]{2,1,0:T(8,128)(2,1)S(1)} collective-permute-done((bf16[3,72,384]{2,1,0:T(8,128)(2,1)S(1)}, bf16[3,72,384]{2,1,0:T(8,128)(2,1)S(1)}, u32[]{:S(2)}, u32[]{:S(2)}) %collective-permute-start.4) | collective-permute-done | bytes 165920 | tf_op jit(solution)/shard_map/ppermute | solution.py:257
  42.5 4.8 %all-gather.8.cloned.1.call-done = bf16[24,80,384]{2,1,0:T(8,128)(2,1)} async-done(((bf16[3,80,384]{2,1,0:T(8,128)(2,1)}), bf16[24,80,384]{2,1,0:T(8,128)(2,1)}) %all-gather.8.cloned.1.call-update) | async-done | bytes 1474576 | tf_op jit(solution)/shard_map/all_gather | solution.py:942
  47.3 7.6 %attention_forward.1 = (bf16[576,1536]{1,0:T(8,128)(2,1)}, f32[8,576]{1,0:T(8,128)}, f32[384,576]{1,0:T(8,128)}, bf16[3,64,1152]{2,1,0:T(8,128)(2,1)}, bf16[3,64...) custom-call(s32[1]{0:T(128)} %bitcast.refs_0_, ...), custom_call_target="tpu_custom_call" | custom-call | flops 1500000000 | bytes 8000000 | tf_op jit(solution)/shard_map/attention_forward/pallas_call | solution.py:560
  54.9 30.8 %all-gather.10.cloned.1.call-done = bf16[24,3,72,384]{3,2,1,0:T(8,128)(2,1)} async-done(((bf16[3,3,72,384]{3,2,1,0:T(8,128)(2,1)}), bf16[24,3,72,384]{3,2,1,0:T(8,128)(2,1)}) %all-gather.10.cloned.1.call-update) | async-done | bytes 3981328 | tf_op jit(solution)/shard_map/all_gather | solution.py:945
  85.6 17.4 %mlp.1 = (bf16[384,576]{1,0:T(8,128)(2,1)}, f32[384,576]{1,0:T(8,128)}, f32[8,576]{1,0:T(8,128)}, bf16[8,4,3,72,384]{4,3,2,1,0:T(8,128)(2,1)}) custom-call(s32[1]{0:T(128)} %bitcast.refs_0_, f32[384,576]{1,0:T(8,128)} %get-tuple-element.32.refs_1_, bf16[384,576]{1,0:T(8,128)(2,1)} %bitcast.59, f32[8,576]{1,0:T(8,128)} %get-tuple-element.33.refs_3_.refs_7_, ...), custom_call_target="tpu_custom_call" | custom-call | flops 6200000000 | bytes 14000000 | tf_op jit(solution)/shard_map/mlp/pallas_call | solution.py:673
  103.3 11.4 %attention_backward.1 = (f32[384,576]{1,0:T(8,128)}, bf16[8,4,80,384]{3,2,1,0:T(8,128)(2,1)}) custom-call(bf16[384,576]{1,0:T(8,128)(2,1)} %bitcast.58, f32[384,576]{1,0:T(8,128)} %get-tuple-element.35.refs_1_, s32[384,1]{1,0:T(8,128)} %copy.37.refs_2_, s32[1,384]{1,0:T(1,128)} %refs_3_.3, f32[32,384]{1,0:T(8,128)} %get-tuple-element.95.refs_4_, ...), custom_call_target="tpu_custom_call" | custom-call | flops 3000000000 | bytes 9000000 | tf_op jit(solution)/shard_map/attention_backward/pallas_call | solution.py:818
  114.7 45.4 %reduce-scatter.5.cloned.1.call-done = bf16[864,384]{1,0:T(8,128)(2,1)} async-done(((bf16[6912,384]{1,0:T(8,128)(2,1)}), bf16[864,384]{1,0:T(8,128)(2,1)}) %reduce-scatter.5.cloned.1.call-update) | async-done | bytes 663568 | tf_op jit(solution)/shard_map/reduce_scatter | solution.py:963
  161.3 2.5 %collective-permute-start.10 = (bf16[3,72,384]{2,1,0:T(8,128)(2,1)S(1)}, bf16[3,72,384]{2,1,0:T(8,128)(2,1)S(1)}, u32[]{:S(2)}, u32[]{:S(2)}) collective-permute-start(bf16[3,72,384]{2,1,0:T(8,128)(2,1)S(1)} %get-tuple-element.88), channel_id=1, source_target_pairs={{0,2},{1,3},{2,0},{3,1},{4,6},{5,7},{6,4},{7,5},{8,10},{9,11},{10,... | collective-permute-start | bytes 497672 | tf_op jit(solution)/shard_map/ppermute | solution.py:257
  165.8 8.1 %collective-permute-done.10 = bf16[3,72,384]{2,1,0:T(8,128)(2,1)S(1)} collective-permute-done((bf16[3,72,384]{2,1,0:T(8,128)(2,1)S(1)}, bf16[3,72,384]{2,1,0:T(8,128)(2,1)S(1)}, u32[]{:S(2)}, u32[]{:S(2)}) %collective-permute-start.10) | collective-permute-done | bytes 165920 | tf_op jit(solution)/shard_map/ppermute | solution.py:257
  173.9 2.5 %collective-permute-done.9 = bf16[3,72,384]{2,1,0:T(8,128)(2,1)S(1)} collective-permute-done((bf16[3,72,384]{2,1,0:T(8,128)(2,1)S(1)}, bf16[3,72,384]{2,1,0:T(8,128)(2,1)S(1)}, u32[]{:S(2)}, u32[]{:S(2)}) %collective-permute-start.9) | collective-permute-done | bytes 165920 | tf_op jit(solution)/shard_map/ppermute | solution.py:257
  176.4 1.7 fusion.2
  178.1 25.9 %reduce-scatter.3.cloned.1.call-done = bf16[320,384]{1,0:T(8,128)(2,1)} async-done(((bf16[2560,384]{1,0:T(8,128)(2,1)}), bf16[320,384]{1,0:T(8,128)(2,1)}) %reduce-scatter.3.cloned.1.call-update) | async-done | bytes 245776 | tf_op jit(solution)/shard_map/reduce_scatter | solution.py:971
  205.0 1.5 collective-permute-start.6
  206.5 2.4 collective-permute-start.7
  214.6 10.7 %all-gather.2 = bf16[576,384]{1,0:T(8,128)(2,1)} all-gather(bf16[72,384]{1,0:T(8,128)(2,1)S(1)} %slice.20), channel_id=4, replica_groups=mesh['rep'=8,'shard'=4] {'rep'}, dimensions={0}, use_global_device_ids=true | all-gather | bytes 497664 | tf_op jit(solution)/shard_map/all_gather | solution.py:981
  225.4 2.0 unpack_attn.1
  228.0 3.3 %all-gather.12.cloned.1.call-done = bf16[24,72,384]{2,1,0:T(8,128)(2,1)} async-done(((bf16[3,72,384]{2,1,0:T(8,128)(2,1)}), bf16[24,72,384]{2,1,0:T(8,128)(2,1)}) %all-gather.12.cloned.1.call-update) | async-done | bytes 1327120 | tf_op jit(solution)/shard_map/all_gather | solution.py:976
  231.4 3.1 %unpack_mlp.1 = (f32[144,1536]{1,0:T(8,128)}, f32[144,1536]{1,0:T(8,128)}, f32[384,576]{1,0:T(8,128)}) custom-call(bf16[8,3,72,384]{3,2,1,0:T(8,128)(2,1)} %bitcast.52), custom_call_target="tpu_custom_call" | custom-call | tf_op jit(solution)/shard_map/unpack_mlp/pallas_call | solution.py:877
  234.4 2.4 copy.42
  (69 shorter events, 24.9 us)
Async XLA Ops:
  7.2 40.2 %all-gather.8.cloned.1.call-start = ((), (), s32[]{:S(2)}) async-start(), calls=%async_computation.4 | async-start | bytes 1658880 | tf_op jit(solution)/shard_map/all_gather | solution.py:942
  8.8 29.9 %copy-start.5 = (bf16[8,384]{1,0:T(8,128)(2,1)}, bf16[8,384]{1,0:T(8,128)(2,1)S(1)}, u32[]{:S(2)}) copy-start(bf16[8,384]{1,0:T(8,128)(2,1)S(1)} %pad.4.refs_7_) | copy-start | bytes 18436
  8.8 29.9 %copy-start.3 = (bf16[1,384,576]{1,2,0:T(8,128)(2,1)S(1)}, bf16[1,384,576]{1,2,0:T(8,128)(2,1)}, u32[]{:S(2)}) copy-start(bf16[1,384,576]{1,2,0:T(8,128)(2,1)} %param.13) | copy-start | bytes 1327108
  10.2 30.4 %copy-start.1 = (bf16[144,1536]{1,0:T(8,128)(2,1)}, bf16[144,1536]{1,0:T(8,128)(2,1)S(1)}, u32[]{:S(2)}) copy-start(bf16[144,1536]{1,0:T(8,128)(2,1)S(1)} %concatenate.6.refs_6_) | copy-start | bytes 1327108
  10.2 29.6 %copy-start.6 = (s32[1,384]{1,0:T(1,128)S(1)}, s32[1,384]{1,0:T(1,128)}, u32[]{:S(2)}) copy-start(s32[1,384]{1,0:T(1,128)} %refs_3_.3) | copy-start | bytes 4612
  10.3 30.3 %copy-start.4 = (bf16[1,384,576]{1,2,0:T(8,128)(2,1)S(1)}, bf16[1,384,576]{1,2,0:T(8,128)(2,1)}, u32[]{:S(2)}) copy-start(bf16[1,384,576]{1,2,0:T(8,128)(2,1)} %param.25) | copy-start | bytes 1327108
  10.3 7.7 %collective-permute-start = (bf16[80,384]{1,0:T(8,128)(2,1)S(1)}, bf16[80,384]{1,0:T(8,128)(2,1)S(1)}, u32[]{:S(2)}, u32[]{:S(2)}) collective-permute-start(bf16[80,384]{1,0:T(8,128)(2,1)S(1)} %pad_maximum_fusion.3), channel_id=1, source_target_pairs={{0,1},{1,2},{2,3},{3,0},{4,5},{5,6},{6,7},{7,4},{8,9},{9,10},{10,1... | collective-permute-start | bytes 184328 | tf_op jit(solution)/shard_map/ppermute | solution.py:257
  13.5 6.9 %collective-permute-start.1 = (bf16[80,384]{1,0:T(8,128)(2,1)S(1)}, bf16[80,384]{1,0:T(8,128)(2,1)S(1)}, u32[]{:S(2)}, u32[]{:S(2)}) collective-permute-start(bf16[80,384]{1,0:T(8,128)(2,1)S(1)} %pad_maximum_fusion.3), channel_id=1, source_target_pairs={{0,2},{1,3},{2,0},{3,1},{4,6},{5,7},{6,4},{7,5},{8,10},{9,11},{10,... | collective-permute-start | bytes 184328 | tf_op jit(solution)/shard_map/ppermute | solution.py:257
  16.1 4.6 %collective-permute-start.2 = (bf16[80,384]{1,0:T(8,128)(2,1)S(1)}, bf16[80,384]{1,0:T(8,128)(2,1)S(1)}, u32[]{:S(2)}, u32[]{:S(2)}) collective-permute-start(bf16[80,384]{1,0:T(8,128)(2,1)S(1)} %pad_maximum_fusion.3), channel_id=1, source_target_pairs={{0,3},{1,0},{2,1},{3,2},{4,7},{5,4},{6,5},{7,6},{8,11},{9,8},{10,9... | collective-permute-start | bytes 184328 | tf_op jit(solution)/shard_map/ppermute | solution.py:257
  21.4 64.3 %all-gather.10.cloned.1.call-start = ((), (), s32[]{:S(2)}) async-start(), calls=%async_computation.5 | async-start | bytes 4478976 | tf_op jit(solution)/shard_map/all_gather | solution.py:945
  23.2 9.2 %collective-permute-start.3 = (bf16[3,72,384]{2,1,0:T(8,128)(2,1)S(1)}, bf16[3,72,384]{2,1,0:T(8,128)(2,1)S(1)}, u32[]{:S(2)}, u32[]{:S(2)}) collective-permute-start(bf16[3,72,384]{2,1,0:T(8,128)(2,1)S(1)} %pad_maximum_fusion.2), channel_id=1, source_target_pairs={{0,1},{1,2},{2,3},{3,0},{4,5},{5,6},{6,7},{7,4},{8,9},{9,10},{10,1... | collective-permute-start | bytes 497672 | tf_op jit(solution)/shard_map/ppermute | solution.py:257
  24.6 13.2 %collective-permute-start.4 = (bf16[3,72,384]{2,1,0:T(8,128)(2,1)S(1)}, bf16[3,72,384]{2,1,0:T(8,128)(2,1)S(1)}, u32[]{:S(2)}, u32[]{:S(2)}) collective-permute-start(bf16[3,72,384]{2,1,0:T(8,128)(2,1)S(1)} %pad_maximum_fusion.2), channel_id=1, source_target_pairs={{0,2},{1,3},{2,0},{3,1},{4,6},{5,7},{6,4},{7,5},{8,10},{9,11},{10,... | collective-permute-start | bytes 497672 | tf_op jit(solution)/shard_map/ppermute | solution.py:257
  26.6 11.2 %collective-permute-start.5 = (bf16[3,72,384]{2,1,0:T(8,128)(2,1)S(1)}, bf16[3,72,384]{2,1,0:T(8,128)(2,1)S(1)}, u32[]{:S(2)}, u32[]{:S(2)}) collective-permute-start(bf16[3,72,384]{2,1,0:T(8,128)(2,1)S(1)} %pad_maximum_fusion.2), channel_id=1, source_target_pairs={{0,3},{1,0},{2,1},{3,2},{4,7},{5,4},{6,5},{7,6},{8,11},{9,8},{10,9... | collective-permute-start | bytes 497672 | tf_op jit(solution)/shard_map/ppermute | solution.py:257
  38.7 121.4 %reduce-scatter.5.cloned.1.call-start = ((), (), s32[]{:S(2)}) async-start(), calls=%async_computation.3 | async-start | bytes 5971968 | tf_op jit(solution)/shard_map/reduce_scatter | solution.py:963
  103.0 101.0 %reduce-scatter.3.cloned.1.call-start = ((), (), s32[]{:S(2)}) async-start(), calls=%async_computation.2 | async-start | bytes 2211840 | tf_op jit(solution)/shard_map/reduce_scatter | solution.py:971
  114.6 95.7 %copy-start = (f32[384,576]{1,0:T(8,128)S(1)}, f32[384,576]{1,0:T(8,128)}, u32[]{:S(2)}) copy-start(f32[384,576]{1,0:T(8,128)} %get-tuple-element.43) | copy-start | bytes 2654212
  114.7 116.7 %all-gather.12.cloned.1.call-start = ((), (), s32[]{:S(2)}) async-start(), calls=%async_computation.6 | async-start | bytes 1492992 | tf_op jit(solution)/shard_map/all_gather | solution.py:976
  160.1 51.5 %copy-start.2 = (bf16[384,576]{1,0:T(8,128)(2,1)S(1)}, bf16[384,576]{1,0:T(8,128)(2,1)}, u32[]{:S(2)}) copy-start(bf16[384,576]{1,0:T(8,128)(2,1)} %get-tuple-element.34) | copy-start | bytes 1327108
  161.3 12.7 %collective-permute-start.10 = (bf16[3,72,384]{2,1,0:T(8,128)(2,1)S(1)}, bf16[3,72,384]{2,1,0:T(8,128)(2,1)S(1)}, u32[]{:S(2)}, u32[]{:S(2)}) collective-permute-start(bf16[3,72,384]{2,1,0:T(8,128)(2,1)S(1)} %get-tuple-element.88), channel_id=1, source_target_pairs={{0,2},{1,3},{2,0},{3,1},{4,6},{5,7},{6,4},{7,5},{8,10},{9,11},{10,... | collective-permute-start | bytes 497672 | tf_op jit(solution)/shard_map/ppermute | solution.py:257
  163.8 10.2 %collective-permute-start.11 = (bf16[3,72,384]{2,1,0:T(8,128)(2,1)S(1)}, bf16[3,72,384]{2,1,0:T(8,128)(2,1)S(1)}, u32[]{:S(2)}, u32[]{:S(2)}) collective-permute-start(bf16[3,72,384]{2,1,0:T(8,128)(2,1)S(1)} %get-tuple-element.87), channel_id=1, source_target_pairs={{0,3},{1,0},{2,1},{3,2},{4,7},{5,4},{6,5},{7,6},{8,11},{9,8},{10,9... | collective-permute-start | bytes 497672 | tf_op jit(solution)/shard_map/ppermute | solution.py:257
  165.2 11.2 %collective-permute-start.9 = (bf16[3,72,384]{2,1,0:T(8,128)(2,1)S(1)}, bf16[3,72,384]{2,1,0:T(8,128)(2,1)S(1)}, u32[]{:S(2)}, u32[]{:S(2)}) collective-permute-start(bf16[3,72,384]{2,1,0:T(8,128)(2,1)S(1)} %get-tuple-element.86), channel_id=1, source_target_pairs={{0,1},{1,2},{2,3},{3,0},{4,5},{5,6},{6,7},{7,4},{8,9},{9,10},{10,1... | collective-permute-start | bytes 497672 | tf_op jit(solution)/shard_map/ppermute | solution.py:257
  205.0 7.6 %collective-permute-start.6 = (bf16[80,384]{1,0:T(8,128)(2,1)S(1)}, bf16[80,384]{1,0:T(8,128)(2,1)S(1)}, u32[]{:S(2)}, u32[]{:S(2)}) collective-permute-start(bf16[80,384]{1,0:T(8,128)(2,1)S(1)} %get-tuple-element.89), channel_id=1, source_target_pairs={{0,1},{1,2},{2,3},{3,0},{4,5},{5,6},{6,7},{7,4},{8,9},{9,10},{10,1... | collective-permute-start | bytes 184328 | tf_op jit(solution)/shard_map/ppermute | solution.py:257
  206.5 7.2 %collective-permute-start.7 = (bf16[80,384]{1,0:T(8,128)(2,1)S(1)}, bf16[80,384]{1,0:T(8,128)(2,1)S(1)}, u32[]{:S(2)}, u32[]{:S(2)}) collective-permute-start(bf16[80,384]{1,0:T(8,128)(2,1)S(1)} %get-tuple-element.91), channel_id=1, source_target_pairs={{0,2},{1,3},{2,0},{3,1},{4,6},{5,7},{6,4},{7,5},{8,10},{9,11},{10,... | collective-permute-start | bytes 184328 | tf_op jit(solution)/shard_map/ppermute | solution.py:257
  208.9 4.8 %collective-permute-start.8 = (bf16[80,384]{1,0:T(8,128)(2,1)S(1)}, bf16[80,384]{1,0:T(8,128)(2,1)S(1)}, u32[]{:S(2)}, u32[]{:S(2)}) collective-permute-start(bf16[80,384]{1,0:T(8,128)(2,1)S(1)} %get-tuple-element.90), channel_id=1, source_target_pairs={{0,3},{1,0},{2,1},{3,2},{4,7},{5,4},{6,5},{7,6},{8,11},{9,8},{10,9... | collective-permute-start | bytes 184328 | tf_op jit(solution)/shard_map/ppermute | solution.py:257
  (1 other events, 18.5 us)
Sparse Core Ops, SparseCore 0:
  21.5 25.7 all-gather.7
  49.8 35.8 all-gather.9
  103.2 56.9 reduce-scatter.4
  163.7 40.2 reduce-scatter.2
  206.4 24.9 all-gather.11
where the time goes:
time: 244 us; the launch traced here: 243 us
  waiting for transfers between devices  136 us (56%)
  Pallas kernels  41.3 us (17%)
  starting transfers between devices  21.3 us (9%)
  local copies, waits for them, and re-layouts  14.8 us (6%)
  between operations  14 us (6%)
  blocking collectives  10.7 us (4%)
  other arithmetic  5.09 us (2%)
    reduce_scatter x1, waiting for transfers between devices, on_device(): lax.psum_scatter(wide_grad.reshape(-1, CHUNK), 'rep', scatter_dimension=0...  45.4 us
    all_gather x1, waiting for transfers between devices, on_device(): wide_pieces = lax.all_gather(fetch_others(wide), 'rep')  30.8 us
    reduce_scatter x1, waiting for transfers between devices, on_device(): lax.psum_scatter(attn_grad.reshape(-1, CHUNK), 'rep', scatter_dimension=0...  25.9 us
    ppermute x12, waiting for transfers between devices, shifted(): lax.ppermute(values, 'shard', [(i, (i + steps) % size) for i in range(siz...  25.8 us
    ppermute x12, starting transfers between devices, shifted(): lax.ppermute(values, 'shard', [(i, (i + steps) % size) for i in range(siz...  20.9 us
    pallas_call x1, Pallas kernels, mlp(): pl.pallas_call(kernel, grid_spec=pltpu.PrefetchScalarGridSpec(num_scalar_...  17.4 us
    pallas_call x1, Pallas kernels, attention_backward(): pl.pallas_call(kernel, in_specs=[pl.BlockSpec(memory_space=pltpu.VMEM)] *...  11.4 us
    all_gather x1, blocking collectives, on_device(): lax.all_gather(narrow(attn_total[:half]), 'rep')  10.7 us
  transfers between devices with their start and end apart: 17, of which 13 were waited for; matrix products, arithmetic and copies ran while one was open for 6% of the time, Pallas kernels for 9%

commit v1 on v0

--- a/solution.py
+++ b/solution.py
@@ -481,10 +481,11 @@
 
 
 def attention_forward_kernel(
-    shards, z_ref, x_ref, col_ref, row_ref, cos_ref, sin_ref, own_ref, gain_own_ref, others_ref,
-    w_ref, gain_ref, x2_ref, q_ref, k_ref, v_ref, o_ref, lse_ref, bias_ref,
+    shards, at_ref, x_ref, col_ref, row_ref, cos_ref, sin_ref, own_ref, gain_own_ref, mine_ref,
+    pair_ref, w_ref, gain_ref, x2_ref, q_ref, k_ref, v_ref, o_ref, lse_ref, bias_ref,
 ):
-    z = z_ref[0]
+    z = at_ref[0]
+    first_core = at_ref[2] == 0
     rows = own_ref.shape[0]
     half = rows // 2
     width = x_ref.shape[1]
@@ -493,15 +494,13 @@
     gains = widen(gain_own_ref[...])
     for k in range(1, shards):
         at = pl.multiple_of(lax.rem(z + shards - k, shards) * rows, 16)
-        gains = gains + widen(others_ref[0, k - 1, half:])
-        for c in range(own_ref.shape[1] // CHUNK):
-            pieces = [widen(others_ref[2 * c + h, k - 1, :half]) for h in range(2)]
-            w_ref[pl.ds(at, rows), c * CHUNK : (c + 1) * CHUNK] = narrow(
-                jnp.concatenate(pieces, axis=0)
-            )
-    tail = width - CHUNK
-    gain_attn = jnp.concatenate([gains[0:1], gains[1:2, :tail]], axis=1)
-    gain_mlp = jnp.concatenate([gains[2:3], gains[3:4, :tail]], axis=1)
+        gains = gains + widen(mine_ref[k - 1, half:])
+        mine, pair = widen(mine_ref[k - 1, :half]), widen(pair_ref[k - 1, :half])
+        upper = jnp.where(first_core, mine, pair)
+        lower = jnp.where(first_core, pair, mine)
+        w_ref[pl.ds(at, rows), :] = narrow(jnp.concatenate([upper, lower], axis=0))
+    gain_attn = gains[0:1, :width]
+    gain_mlp = gains[1:2, :width]
     gain_ref[0:1, :] = gain_attn
     gain_ref[1:2, :] = gain_mlp
     x = widen(x_ref[...])
@@ -549,7 +548,7 @@
     )
 
 
-def attention_forward(z, x, col, row, cosine, sine, own, gain_own, others, shards):
+def attention_forward(at, x, col, row, cosine, sine, own, gain_own, mine, pair, shards):
     width = x.shape[1]
     cells = SHARE * TOKENS
     bf16, f32 = jnp.bfloat16, jnp.float32
@@ -562,7 +561,7 @@
         grid_spec=pltpu.PrefetchScalarGridSpec(
             num_scalar_prefetch=1,
             grid=(),
-            in_specs=[pl.BlockSpec(memory_space=pltpu.VMEM)] * 8,
+            in_specs=[pl.BlockSpec(memory_space=pltpu.VMEM)] * 9,
             out_specs=[pl.BlockSpec(memory_space=pltpu.VMEM)] * 8,
             scratch_shapes=[pltpu.VMEM((TOKENS, TOKENS), f32)],
         ),
@@ -581,15 +580,16 @@
             flops=int(1.5e9), bytes_accessed=8000000, transcendentals=2000000
         ),
         name="attention_forward",
-    )(z, x, col, row, cosine, sine, own, gain_own, others)
+    )(at, x, col, row, cosine, sine, own, gain_own, mine, pair)
 
 
 def mlp_kernel(
-    shards, z_ref, x2_ref, ct_ref, gain_ref, gate_ref, up_ref, tall_ref, wide_ref, tall_other_ref,
-    out_ref, dx2_ref, gain_grad_ref, grad_ref,
+    shards, at_ref, x2_ref, ct_ref, gain_ref, gate_ref, up_ref, tall_ref, wide_ref, tall_other_ref,
+    out_ref, dx2_ref, gain_grad_ref, keep_ref, send_ref,
     u2_ref, h2_ref, h2t_ref, ctt_ref, acc_ref, dh2_ref, wg_ref, wu_ref, wd_ref,
+    gg_ref, gu_ref, gd_ref,
 ):
-    z = z_ref[0]
+    z, chip, core = at_ref[0], at_ref[1], at_ref[2]
     j = pl.program_id(0)
     rows = gate_ref.shape[0]
     half = rows // 2
@@ -636,14 +636,22 @@
     du = narrow(da * silu)
     acc_ref[...] += dot(act, wd, 1, 1)
     dh2_ref[...] += dot(dg, wg, 1, 1) + dot(du, wu, 1, 1)
-    for m, grad in ((0, dot(h2t_ref[...], dg)), (1, dot(h2t_ref[...], du))):
-        for b in range(shards):
-            for h in range(2):
-                at = b * rows + h * half
-                grad_ref[2 * j + h, b, m] = narrow(grad[at : at + half])
-    grad = dot(ctt_ref[...], act)
-    for r in range(2 * shards):
-        grad_ref[r, j, 2] = narrow(grad[r * half : (r + 1) * half])
+    gg_ref[...] = dot(h2t_ref[...], dg)
+    gu_ref[...] = dot(h2t_ref[...], du)
+    gd_ref[...] = dot(ctt_ref[...], act)
+    to_chip = lax.bitwise_xor(j, chip)
+    to_shard = lax.rem(j + shards - z, shards)
+    for rel, ref in ((0, keep_ref), (1, send_ref)):
+        to_core = lax.bitwise_xor(core, rel)
+        for k in range(shards):
+            at = lax.rem(z + k, shards) * rows + to_core * half
+            at = pl.multiple_of(at, 8)
+            ref[to_chip, k, 0] = narrow(gg_ref[pl.ds(at, half), :])
+            ref[to_chip, k, 1] = narrow(gu_ref[pl.ds(at, half), :])
+        for c in range(4):
+            at = (2 * lax.bitwise_xor(chip, c) + to_core) * half
+            at = pl.multiple_of(at, 8)
+            ref[c, to_shard, 2] = narrow(gd_ref[pl.ds(at, half), :])
 
     @pl.when(j == pl.num_programs(0) - 1)
     def _():
@@ -656,7 +664,7 @@
         dx2_ref[...] = widen(ct_ref[...]) + inverse * (n2 - u2 * mean)
 
 
-def mlp(z, x2, ct, gains, gate, up, tall, gathered, shards):
+def mlp(at, x2, ct, gains, gate, up, tall, gathered, shards):
     width = x2.shape[1]
     copies = gathered.shape[0]
     rows, ff = gate.shape
@@ -666,10 +674,10 @@
     def kernel(*refs):
         mlp_kernel(shards, *refs)
 
-    def tall_block(j, z_ref):
-        return (0, jnp.maximum(lax.rem(z_ref[0] + shards - j, shards) - 1, 0), 2, 0, 0)
-
-    whole = lambda shape: pl.BlockSpec(shape, lambda j, z_ref: (0,) * len(shape))
+    def tall_block(j, at_ref):
+        return (0, jnp.maximum(lax.rem(at_ref[0] + shards - j, shards) - 1, 0), 2, 0, 0)
+
+    whole = lambda shape: pl.BlockSpec(shape, lambda j, at_ref: (0,) * len(shape))
     return pl.pallas_call(
         kernel,
         grid_spec=pltpu.PrefetchScalarGridSpec(
@@ -679,17 +687,18 @@
                 whole((TOKENS, width)),
                 whole((TOKENS, width)),
                 whole((8, width)),
-                pl.BlockSpec((rows, CHUNK), lambda j, z_ref: (0, j)),
-                pl.BlockSpec((rows, CHUNK), lambda j, z_ref: (0, j)),
+                pl.BlockSpec((rows, CHUNK), lambda j, at_ref: (0, j)),
+                pl.BlockSpec((rows, CHUNK), lambda j, at_ref: (0, j)),
                 whole((width, CHUNK)),
-                pl.BlockSpec((2, shards - 1, 2, half, CHUNK), lambda j, z_ref: (j, 0, 0, 0, 0)),
+                pl.BlockSpec((2, shards - 1, 2, half, CHUNK), lambda j, at_ref: (j, 0, 0, 0, 0)),
                 pl.BlockSpec((copies, 1, 1, half, CHUNK), tall_block),
             ],
             out_specs=[
                 whole((TOKENS, width)),
                 whole((TOKENS, width)),
                 whole((8, width)),
-                whole((copies, shards, 3, half, CHUNK)),
+                whole((copies // 2, shards, 3, half, CHUNK)),
+                whole((copies // 2, shards, 3, half, CHUNK)),
             ],
             scratch_shapes=[
                 pltpu.VMEM((TOKENS, width), f32),
@@ -701,13 +710,17 @@
                 pltpu.VMEM((width, CHUNK), bf16),
                 pltpu.VMEM((width, CHUNK), bf16),
                 pltpu.VMEM((width, CHUNK), bf16),
+                pltpu.VMEM((width, CHUNK), f32),
+                pltpu.VMEM((width, CHUNK), f32),
+                pltpu.VMEM((width, CHUNK), f32),
             ],
         ),
         out_shape=[
             jax.ShapeDtypeStruct((TOKENS, width), bf16),
             jax.ShapeDtypeStruct((TOKENS, width), f32),
             jax.ShapeDtypeStruct((8, width), f32),
-            jax.ShapeDtypeStruct((copies, shards, 3, half, CHUNK), bf16),
+            jax.ShapeDtypeStruct((copies // 2, shards, 3, half, CHUNK), bf16),
+            jax.ShapeDtypeStruct((copies // 2, shards, 3, half, CHUNK), bf16),
         ],
         compiler_params=pltpu.CompilerParams(
             vmem_limit_bytes=VMEM_LIMIT, dimension_semantics=("arbitrary",)
@@ -716,15 +729,16 @@
             flops=int(6.2e9), bytes_accessed=14000000, transcendentals=1200000
         ),
         name="mlp",
-    )(z, x2, ct, gains, gate, up, tall, gathered, gathered)
+    )(at, x2, ct, gains, gate, up, tall, gathered, gathered)
 
 
 def attention_backward_kernel(
-    shards, x_ref, dx2_ref, col_ref, row_ref, cos_ref, sin_ref, w_ref, gain_ref, q_ref, k_ref,
-    v_ref, o_ref, lse_ref, gain_grad_ref,
-    dx_ref, grad_ref,
-    bias_ref, do_ref, dq_ref, dk_ref, dv_ref,
+    shards, at_ref, x_ref, dx2_ref, col_ref, row_ref, cos_ref, sin_ref, w_ref, gain_ref, q_ref,
+    k_ref, v_ref, o_ref, lse_ref, gain_grad_ref,
+    dx_ref, keep_ref, send_ref,
+    bias_ref, do_ref, dq_ref, dk_ref, dv_ref, grad_ref,
 ):
+    z, chip, core = at_ref[0], at_ref[1], at_ref[2]
     width = x_ref.shape[1]
     rows = width // shards
     half = rows // 2
@@ -797,15 +811,18 @@
             )
         else:
             grad = dot(h1t, dq[CHUNK - tail :], 1, 1)
-        for b in range(shards):
-            for h in range(2):
-                at = b * rows + h * half
-                grad_ref[2 * c + h, b] = narrow(
-                    jnp.concatenate([grad[at : at + half], extra], axis=0)
+        grad_ref[...] = grad
+        to_chip = lax.bitwise_xor(chip, c)
+        for rel, ref in ((0, keep_ref), (1, send_ref)):
+            for k in range(shards):
+                at = lax.rem(z + k, shards) * rows + lax.bitwise_xor(core, rel) * half
+                at = pl.multiple_of(at, 8)
+                ref[to_chip, k] = narrow(
+                    jnp.concatenate([grad_ref[pl.ds(at, half), :], extra], axis=0)
                 )
 
 
-def attention_backward(args, shards, copies):
+def attention_backward(at, args, shards, copies):
     x = args[0]
     width = x.shape[1]
     half = width // shards // 2
@@ -817,25 +834,31 @@
 
     return pl.pallas_call(
         kernel,
-        in_specs=[pl.BlockSpec(memory_space=pltpu.VMEM)] * len(args),
-        out_specs=[pl.BlockSpec(memory_space=pltpu.VMEM)] * 2,
+        grid_spec=pltpu.PrefetchScalarGridSpec(
+            num_scalar_prefetch=1,
+            grid=(),
+            in_specs=[pl.BlockSpec(memory_space=pltpu.VMEM)] * len(args),
+            out_specs=[pl.BlockSpec(memory_space=pltpu.VMEM)] * 3,
+            scratch_shapes=[
+                pltpu.VMEM((TOKENS, TOKENS), f32),
+                pltpu.VMEM((GROUPS, HEAD_WIDTH, cells), bf16),
+                pltpu.VMEM((GROUPS, HEAD_WIDTH, cells), f32),
+                pltpu.VMEM((GROUPS, HEAD_WIDTH, TOKENS), f32),
+                pltpu.VMEM((GROUPS, HEAD_WIDTH, TOKENS), f32),
+                pltpu.VMEM((width, CHUNK), f32),
+            ],
+        ),
         out_shape=[
             jax.ShapeDtypeStruct((TOKENS, width), f32),
-            jax.ShapeDtypeStruct((copies, shards, half + 8, CHUNK), bf16),
-        ],
-        scratch_shapes=[
-            pltpu.VMEM((TOKENS, TOKENS), f32),
-            pltpu.VMEM((GROUPS, HEAD_WIDTH, cells), bf16),
-            pltpu.VMEM((GROUPS, HEAD_WIDTH, cells), f32),
-            pltpu.VMEM((GROUPS, HEAD_WIDTH, TOKENS), f32),
-            pltpu.VMEM((GROUPS, HEAD_WIDTH, TOKENS), f32),
+            jax.ShapeDtypeStruct((copies // 2, shards, half + 8, CHUNK), bf16),
+            jax.ShapeDtypeStruct((copies // 2, shards, half + 8, CHUNK), bf16),
         ],
         compiler_params=pltpu.CompilerParams(vmem_limit_bytes=VMEM_LIMIT),
         cost_estimate=pl.CostEstimate(
             flops=int(3e9), bytes_accessed=9000000, transcendentals=1400000
         ),
         name="attention_backward",
-    )(*args)
+    )(at, *args)
 
 
 def unpack_attn_kernel(piece_ref, q_ref, k_ref, v_ref, o_ref):
@@ -893,14 +916,44 @@
     )
 
 
-def gain_rows(gain_attn, gain_mlp):
-    rows = gain_attn.shape[0]
-    size = lax.axis_size("shard")
-    both = jnp.zeros((2, 2 * CHUNK), jnp.bfloat16)
-    both = lax.dynamic_update_slice(
-        both, jnp.stack([gain_attn, gain_mlp]), (0, lax.axis_index("shard") * rows)
-    )
-    return jnp.pad(both.reshape(4, CHUNK), ((0, 4), (0, 0)))
+def gain_rows(gain_attn, gain_mlp, columns):
+    both = jnp.zeros((8, columns), jnp.bfloat16)
+    at = lax.axis_index("shard") * gain_attn.shape[0]
+    return lax.dynamic_update_slice(both, jnp.stack([gain_attn, gain_mlp]), (0, at))
+
+
+def swapped(values, bit):
+    size = lax.axis_size("rep")
+    return lax.ppermute(values, "rep", [(i, i ^ bit) for i in range(size)])
+
+
+def plus(left, right):
+    return narrow(widen(left) + widen(right))
+
+
+def sum_in_plane(keep, came):
+    tail = keep.shape[1:]
+    mid = tail[0] // 2
+    keep = keep.reshape((2, 2) + tail)
+    came = came.reshape((2, 2) + tail)
+    a_came = swapped(plus(keep[:, 1, :mid], came[:, 1, :mid]), 2)
+    b_came = swapped(plus(keep[1, :, mid:], came[1, :, mid:]), 4)
+    a_keep = plus(keep[:, 0, :mid], came[:, 0, :mid])
+    b_keep = plus(keep[0, :, mid:], came[0, :, mid:])
+    a_last = swapped(plus(a_keep[1], a_came[1]), 4)
+    b_last = swapped(plus(b_keep[1], b_came[1]), 2)
+    a = widen(a_keep[0]) + widen(a_came[0]) + widen(a_last)
+    b = widen(b_keep[0]) + widen(b_came[0]) + widen(b_last)
+    return a, b
+
+
+def sum_along_shard(a, b):
+    blocks = [a[i] for i in range(a.shape[0])] + [b[i] for i in range(b.shape[0])]
+    came = [shifted(narrow(blocks[k]), k) for k in range(1, len(blocks))]
+    total = blocks[0]
+    for value in came:
+        total = total + widen(value)
+    return total
 
 
 def on_device(
@@ -935,14 +988,20 @@
             layer_output_cotangent,
         )
     shards, copies = lax.axis_size("shard"), lax.axis_size("rep")
-    z = lax.axis_index("shard").astype(jnp.int32).reshape(1)
-    own = jnp.concatenate([key_weight, value_weight, output_weight, query_weight], axis=1)
-    gains_own = gain_rows(gain_attn, gain_mlp)
-    attn_others = fetch_others(jnp.concatenate([piece_of(own), gains_own]))
-    attn_pieces = lax.all_gather(attn_others, "rep")
+    rank = lax.axis_index("rep")
+    at = jnp.stack([lax.axis_index("shard"), rank // 2, rank % 2]).astype(jnp.int32)
     tall = jnp.transpose(down_weight)
     wide = jnp.stack([piece_of(gate_weight), piece_of(up_weight), row_piece_of(tall)])
-    wide_pieces = lax.all_gather(fetch_others(wide), "rep")
+    wide_others = fetch_others(wide)
+    wide_pieces = lax.all_gather(wide_others, "rep")
+    own = jnp.concatenate([key_weight, value_weight, output_weight, query_weight], axis=1)
+    gains_own = gain_rows(gain_attn, gain_mlp, own.shape[1])
+    rows = own.shape[0]
+    own_half = lax.dynamic_slice_in_dim(own, (rank % 2) * (rows // 2), rows // 2, 0)
+    own_half = jnp.concatenate([own_half, gains_own])
+    own_half, _ = lax.optimization_barrier((own_half, wide_others))
+    mine = fetch_others(own_half)
+    pair = swapped(mine, 1)
 
     half_dim = HEAD_WIDTH // 2
     frequency = ROPE_BASE ** (-(jnp.arange(half_dim, dtype=jnp.float32) * 2.0 / HEAD_WIDTH))
@@ -954,35 +1013,30 @@
     ct = layer_output_cotangent[0]
 
     w, gains, x2, q, k, v, o, lse = attention_forward(
-        z, x, col, row, cosine, sine, own, gains_own, attn_pieces, shards
-    )
-    out, dx2, gain_mlp_grad, wide_grad = mlp(
-        z, x2, ct, gains, gate_weight, up_weight, tall, wide_pieces, shards
-    )
-    half = gate_weight.shape[0] // 2
-    wide_part = lax.psum_scatter(
-        wide_grad.reshape(-1, CHUNK), "rep", scatter_dimension=0, tiled=True
-    ).reshape(shards, 3, half, CHUNK)
-    dx, attn_grad = attention_backward(
+        at, x, col, row, cosine, sine, own, gains_own, mine, pair, shards
+    )
+    out, dx2, gain_mlp_grad, wide_keep, wide_send = mlp(
+        at, x2, ct, gains, gate_weight, up_weight, tall, wide_pieces, shards
+    )
+    wide_came = swapped(wide_send, 1)
+    dx, attn_keep, attn_send = attention_backward(
+        at,
         (x, dx2, col, row, cosine, sine, w, gains, q, k, v, o, lse, gain_mlp_grad),
         shards,
         copies,
     )
-    attn_part = lax.psum_scatter(
-        attn_grad.reshape(-1, CHUNK), "rep", scatter_dimension=0, tiled=True
-    ).reshape(shards, half + 8, CHUNK)
-    wide_total = narrow(sum_over_shard(wide_part))
+    wide_total = narrow(sum_along_shard(*sum_in_plane(wide_keep, wide_came)))
     gate_grad, up_grad, down_grad = unpack_mlp(
         lax.all_gather(wide_total, "rep"),
         (gate_weight.shape, up_weight.shape, down_weight.shape),
     )
-    attn_total = sum_over_shard(attn_part)
+    attn_total = sum_along_shard(*sum_in_plane(attn_keep, swapped(attn_send, 1)))
+    half = rows // 2
     q_grad, k_grad, v_grad, o_grad = unpack_attn(
         lax.all_gather(narrow(attn_total[:half]), "rep"),
         (query_weight.shape, key_weight.shape, value_weight.shape, output_weight.shape),
     )
     both = attn_total[half : half + 4].reshape(2, 2 * CHUNK)
-    rows = gain_attn.shape[0]
     both = lax.dynamic_slice(both, (0, lax.axis_index("shard") * rows), (2, rows))
     return (
         out[None],

time: 244 us -> 192 us (0.79)
  waiting for transfers between devices: 136 us -> 79.2 us
  starting transfers between devices: 21.3 us -> 25.1 us
  local copies, waits for them, and re-layouts: 14.8 us -> 11.6 us
  Pallas kernels: 41.3 us -> 44.2 us
    reduce_scatter x2 -> x0, waiting for transfers between devices: 71.3 us -> none  [the longest x1 45.4 us: on_device(): lax.psum_scatter(wide_grad.reshape(-1, CHUNK), 'rep', scatter_dimension=0...]
    ppermute x0 -> x11, waiting for transfers between devices: none -> 36 us  [swapped(): return lax.ppermute(values, 'rep', [(i, i ^ bit) for i in range(size)])]
    all_gather x2 -> x1, waiting for transfers between devices: 35.6 us -> 0.02 us  [on_device(): wide_pieces = lax.all_gather(wide_others, 'rep')]
    ppermute x12, waiting for transfers between devices: 25.8 us -> 43.2 us  [shifted(): lax.ppermute(values, 'shard', [(i, (i + steps) % size) for i in range(siz...]
    ppermute x0 -> x11, starting transfers between devices: none -> 9.63 us  [swapped(): return lax.ppermute(values, 'rep', [(i, i ^ bit) for i in range(size)])]
    ppermute x12, starting transfers between devices: 20.9 us -> 15.4 us  [shifted(): lax.ppermute(values, 'shard', [(i, (i + steps) % size) for i in range(siz...]
    all_gather x1, waiting for transfers between devices: 3.34 us -> 0.01 us  [on_device(): lax.all_gather(wide_total, 'rep')]
    unnamed x21 -> x41, local copies, waits for them, and re-layouts: 6.67 us -> 7.59 us
  transfers between devices with their start and end apart: 17 -> 25, of which waited for: 13 -> 15; matrix products, arithmetic and copies ran while one was open for 6% -> 5% of each run, Pallas kernels for 9% -> 12%
where the time goes in v1:
time: 192 us; the launch traced here: 191 us
  waiting for transfers between devices  79.2 us (41%)
  Pallas kernels  44.2 us (23%)
  starting transfers between devices  25.1 us (13%)
  between operations  14.5 us (8%)
  local copies, waits for them, and re-layouts  11.6 us (6%)
  blocking collectives  10.5 us (5%)
  other arithmetic  6.28 us (3%)
    ppermute x12, waiting for transfers between devices, shifted(): lax.ppermute(values, 'shard', [(i, (i + steps) % size) for i in range(siz...  43.2 us
    ppermute x11, waiting for transfers between devices, swapped(): return lax.ppermute(values, 'rep', [(i, i ^ bit) for i in range(size)])  36 us
    pallas_call x1, Pallas kernels, mlp(): pl.pallas_call(kernel, grid_spec=pltpu.PrefetchScalarGridSpec(num_scalar_...  18.5 us
    ppermute x12, starting transfers between devices, shifted(): lax.ppermute(values, 'shard', [(i, (i + steps) % size) for i in range(siz...  15.4 us
    pallas_call x1, Pallas kernels, attention_backward(): pl.pallas_call(kernel, grid_spec=pltpu.PrefetchScalarGridSpec(num_scalar_...  12.2 us
    all_gather x1, blocking collectives, on_device(): lax.all_gather(narrow(attn_total[:half]), 'rep')  10.5 us
    ppermute x11, starting transfers between devices, swapped(): return lax.ppermute(values, 'rep', [(i, i ^ bit) for i in range(size)])  9.63 us
    pallas_call x1, Pallas kernels, attention_forward(): pl.pallas_call(kernel, grid_spec=pltpu.PrefetchScalarGridSpec(num_scalar_...  8.44 us
  transfers between devices with their start and end apart: 25, of which 15 were waited for; matrix products, arithmetic and copies ran while one was open for 5% of the time, Pallas kernels for 12%

profile of v1, /device:TPU:0, one launch (start us, length us, event | category | flops | bytes accessed | tf_op | source)
XLA Modules:
  0.0 191.5 jit_solution(5775890369777004458)
XLA Ops:
  9.2 5.1 %collective-permute-start.2 = (bf16[3,72,384]{2,1,0:T(8,128)(2,1)S(1)}, bf16[3,72,384]{2,1,0:T(8,128)(2,1)S(1)}, u32[]{:S(2)}, u32[]{:S(2)}) collective-permute-start(bf16[3,72,384]{2,1,0:T(8,128)(2,1)S(1)} %pad_maximum_fusion.3), channel_id=1, source_target_pairs={{0,3},{1,0},{2,1},{3,2},{4,7},{5,4},{6,5},{7,6},{8,11},{9,8},{10,9... | collective-permute-start | bytes 497672 | tf_op jit(solution)/shard_map/ppermute | solution.py:257
  15.3 3.7 %collective-permute-done.2 = bf16[3,72,384]{2,1,0:T(8,128)(2,1)S(1)} collective-permute-done((bf16[3,72,384]{2,1,0:T(8,128)(2,1)S(1)}, bf16[3,72,384]{2,1,0:T(8,128)(2,1)S(1)}, u32[]{:S(2)}, u32[]{:S(2)}) %collective-permute-start.2) | collective-permute-done | bytes 165920 | tf_op jit(solution)/shard_map/ppermute | solution.py:257
  19.0 9.4 %collective-permute-done.1 = bf16[3,72,384]{2,1,0:T(8,128)(2,1)S(1)} collective-permute-done((bf16[3,72,384]{2,1,0:T(8,128)(2,1)S(1)}, bf16[3,72,384]{2,1,0:T(8,128)(2,1)S(1)}, u32[]{:S(2)}, u32[]{:S(2)}) %collective-permute-start.1) | collective-permute-done | bytes 165920 | tf_op jit(solution)/shard_map/ppermute | solution.py:257
  31.5 1.9 collective-permute-start.4
  33.3 1.9 %collective-permute-start.3 = (bf16[80,1536]{1,0:T(8,128)(2,1)S(1)}, bf16[80,1536]{1,0:T(8,128)(2,1)S(1)}, u32[]{:S(2)}, u32[]{:S(2)}) collective-permute-start(bf16[80,1536]{1,0:T(8,128)(2,1)S(1)} %pad_maximum_fusion.2), channel_id=1, source_target_pairs={{0,1},{1,2},{2,3},{3,0},{4,5},{5,6},{6,7},{7,4},{8,9},{9,10},{10,1... | collective-permute-start | bytes 737288 | tf_op jit(solution)/shard_map/ppermute | solution.py:257
  35.3 2.8 %collective-permute-done.5 = bf16[80,1536]{1,0:T(8,128)(2,1)S(1)} collective-permute-done((bf16[80,1536]{1,0:T(8,128)(2,1)S(1)}, bf16[80,1536]{1,0:T(8,128)(2,1)S(1)}, u32[]{:S(2)}, u32[]{:S(2)}) %collective-permute-start.5) | collective-permute-done | bytes 245792 | tf_op jit(solution)/shard_map/ppermute | solution.py:257
  38.1 16.3 %collective-permute-done.4 = bf16[80,1536]{1,0:T(8,128)(2,1)S(1)} collective-permute-done((bf16[80,1536]{1,0:T(8,128)(2,1)S(1)}, bf16[80,1536]{1,0:T(8,128)(2,1)S(1)}, u32[]{:S(2)}, u32[]{:S(2)}) %collective-permute-start.4) | collective-permute-done | bytes 245792 | tf_op jit(solution)/shard_map/ppermute | solution.py:257
  59.9 8.4 %attention_forward.1 = (bf16[576,1536]{1,0:T(8,128)(2,1)}, f32[8,576]{1,0:T(8,128)}, f32[384,576]{1,0:T(8,128)}, bf16[3,64,1152]{2,1,0:T(8,128)(2,1)}, bf16[3,64...) custom-call(s32[3]{0:T(128)} %pad_add_fusion.refs_0_, ...), custom_call_target="tpu_custom_call" | custom-call | flops 1500000000 | bytes 8000000 | tf_op jit(solution)/shard_map/attention_forward/pallas_call | solution.py:559
  68.4 18.5 %mlp.1 = (bf16[384,576]{1,0:T(8,128)(2,1)}, f32[384,576]{1,0:T(8,128)}, f32[8,576]{1,0:T(8,128)}, bf16[4,4,3,72,384]{4,3,2,1,0:T(8,128)(2,1)}, bf16[4,4,3,72,384]{4,3,2,1,0:T(8,128)(2,1)}) custom-call(s32[3]{0:T(128)} %pad_add_fusion.refs_0_, f32[384,576]{1,0:T(8,128)} %get-tuple-element.36.refs_1_, bf16[384,576]{1,0:T(8,128)(2,1)} %bitcast.152, ...), custom_call_target="tpu_custom_call" | custom-call | flops 6200000000 | bytes 14000000 | tf_op jit(solution)/shard_map/mlp/pallas_call | solution.py:681
  87.4 4.8 %collective-permute-done.15 = bf16[4,4,3,72,384]{4,3,2,1,0:T(8,128)(2,1)S(1)} collective-permute-done((bf16[4,4,3,72,384]{4,3,2,1,0:T(8,128)(2,1)}, bf16[4,4,3,72,384]{4,3,2,1,0:T(8,128)(2,1)S(1)}, u32[]{:S(2)}, u32[]{:S(2)}) %collective-permute-start.15) | collective-permute-done | bytes 2654240 | tf_op jit(solution)/shard_map/ppermute | solution.py:927
  92.2 1.8 add_convert_fusion.1
  97.4 13.8 %collective-permute-done.19 = bf16[2,2,3,72,384]{4,3,2,1,0:T(8,128)(2,1)S(1)} collective-permute-done((bf16[2,2,3,72,384]{4,3,2,1,0:T(8,128)(2,1)S(1)}, bf16[2,2,3,72,384]{4,3,2,1,0:T(8,128)(2,1)S(1)}, u32[]{:S(2)}, u32[]{:S(2)}) %collective-permute-start.19) | collective-permute-done | bytes 663584 | tf_op jit(solution)/shard_map/ppermute | solution.py:927
  112.9 12.2 %attention_backward.1 = (f32[384,576]{1,0:T(8,128)}, bf16[4,4,80,384]{3,2,1,0:T(8,128)(2,1)}, bf16[4,4,80,384]{3,2,1,0:T(8,128)(2,1)}) custom-call(s32[3]{0:T(128)} %pad_add_fusion.refs_0_, bf16[384,576]{1,0:T(8,128)(2,1)} %bitcast.151, f32[384,576]{1,0:T(8,128)} %get-tuple-element.39.refs_2_, s32[384,1]{1,0:T(8,128)} %copy.37.refs_2_.refs_3_, ...), custom_call_target="tpu_custom_call" | custom-call | flops 3000000000 | bytes 9000000 | tf_op jit(solution)/shard_map/attention_backward/pallas_call | solution.py:835
  127.6 7.8 %collective-permute-done.17 = bf16[2,3,72,384]{3,2,1,0:T(8,128)(2,1)S(1)} collective-permute-done((bf16[2,3,72,384]{3,2,1,0:T(8,128)(2,1)S(1)}, bf16[2,3,72,384]{3,2,1,0:T(8,128)(2,1)S(1)}, u32[]{:S(2)}, u32[]{:S(2)}) %collective-permute-start.17) | collective-permute-done | bytes 331808 | tf_op jit(solution)/shard_map/ppermute | solution.py:927
  136.9 6.6 %collective-permute-done.18 = bf16[3,72,384]{2,1,0:T(8,128)(2,1)S(1)} collective-permute-done((bf16[3,72,384]{2,1,0:T(8,128)(2,1)S(1)}, bf16[3,72,384]{2,1,0:T(8,128)(2,1)S(1)}, u32[]{:S(2)}, u32[]{:S(2)}) %collective-permute-start.18) | collective-permute-done | bytes 165920 | tf_op jit(solution)/shard_map/ppermute | solution.py:257
  146.7 4.5 %collective-permute-done.11 = bf16[2,2,80,384]{3,2,1,0:T(8,128)(2,1)S(1)} collective-permute-done((bf16[2,2,80,384]{3,2,1,0:T(8,128)(2,1)S(1)}, bf16[2,2,80,384]{3,2,1,0:T(8,128)(2,1)S(1)}, u32[]{:S(2)}, u32[]{:S(2)}) %collective-permute-start.11) | collective-permute-done | bytes 245792 | tf_op jit(solution)/shard_map/ppermute | solution.py:927
  151.8 2.9 %collective-permute-done.8 = bf16[2,2,80,384]{3,2,1,0:T(8,128)(2,1)S(1)} collective-permute-done((bf16[2,2,80,384]{3,2,1,0:T(8,128)(2,1)S(1)}, bf16[2,2,80,384]{3,2,1,0:T(8,128)(2,1)S(1)}, u32[]{:S(2)}, u32[]{:S(2)}) %collective-permute-start.8) | collective-permute-done | bytes 245792 | tf_op jit(solution)/shard_map/ppermute | solution.py:927
  154.9 2.1 %collective-permute-done.12 = bf16[2,80,384]{2,1,0:T(8,128)(2,1)S(1)} collective-permute-done((bf16[2,80,384]{2,1,0:T(8,128)(2,1)S(1)}, bf16[2,80,384]{2,1,0:T(8,128)(2,1)S(1)}, u32[]{:S(2)}, u32[]{:S(2)}) %collective-permute-start.12) | collective-permute-done | bytes 122912 | tf_op jit(solution)/shard_map/ppermute | solution.py:927
  157.6 2.1 %collective-permute-start.14 = (bf16[80,384]{1,0:T(8,128)(2,1)S(1)}, bf16[80,384]{1,0:T(8,128)(2,1)S(1)}, u32[]{:S(2)}, u32[]{:S(2)}) collective-permute-start(bf16[80,384]{1,0:T(8,128)(2,1)S(1)} %get-tuple-element.103), channel_id=1, source_target_pairs={{0,3},{1,0},{2,1},{3,2},{4,7},{5,4},{6,5},{7,6},{8,11},{9,8},{10,9... | collective-permute-start | bytes 184328 | tf_op jit(solution)/shard_map/ppermute | solution.py:257
  163.2 2.7 %collective-permute-done.10 = bf16[80,384]{1,0:T(8,128)(2,1)S(1)} collective-permute-done((bf16[80,384]{1,0:T(8,128)(2,1)S(1)}, bf16[80,384]{1,0:T(8,128)(2,1)S(1)}, u32[]{:S(2)}, u32[]{:S(2)}) %collective-permute-start.10) | collective-permute-done | bytes 61472 | tf_op jit(solution)/shard_map/ppermute | solution.py:257
  166.0 10.5 %all-gather.1 = bf16[576,384]{1,0:T(8,128)(2,1)} all-gather(bf16[72,384]{1,0:T(8,128)(2,1)S(1)} %slice.308), channel_id=3, replica_groups=mesh['rep'=8,'shard'=4] {'rep'}, dimensions={0}, use_global_device_ids=true | all-gather | bytes 497664 | tf_op jit(solution)/shard_map/all_gather | solution.py:1036
  176.5 2.0 %unpack_attn.1 = (f32[144,576]{1,0:T(8,128)}, f32[144,192]{1,0:T(8,128)}, f32[144,192]{1,0:T(8,128)}, f32[144,576]{1,0:T(8,128)}) custom-call(bf16[8,72,384]{2,1,0:T(8,128)(2,1)} %bitcast.142), custom_call_target="tpu_custom_call" | custom-call | tf_op jit(solution)/shard_map/unpack_attn/pallas_call | solution.py:880
  179.1 3.1 %unpack_mlp.1 = (f32[144,1536]{1,0:T(8,128)}, f32[144,1536]{1,0:T(8,128)}, f32[384,576]{1,0:T(8,128)}) custom-call(bf16[8,3,72,384]{3,2,1,0:T(8,128)(2,1)} %bitcast.143), custom_call_target="tpu_custom_call" | custom-call | tf_op jit(solution)/shard_map/unpack_mlp/pallas_call | solution.py:900
  182.2 2.4 %copy.42 = f32[384,576]{0,1:T(8,128)} copy(f32[384,576]{1,0:T(8,128)} %get-tuple-element.89) | data formatting | bytes 1769472
  (115 shorter events, 29.7 us)
Async XLA Ops:
  7.2 61.1 %all-gather.6.cloned.1.call-start = ((), (), s32[]{:S(2)}) async-start(), calls=%async_computation | async-start | bytes 4478976 | tf_op jit(solution)/shard_map/all_gather | solution.py:996
  9.2 9.8 %collective-permute-start.2 = (bf16[3,72,384]{2,1,0:T(8,128)(2,1)S(1)}, bf16[3,72,384]{2,1,0:T(8,128)(2,1)S(1)}, u32[]{:S(2)}, u32[]{:S(2)}) collective-permute-start(bf16[3,72,384]{2,1,0:T(8,128)(2,1)S(1)} %pad_maximum_fusion.3), channel_id=1, source_target_pairs={{0,3},{1,0},{2,1},{3,2},{4,7},{5,4},{6,5},{7,6},{8,11},{9,8},{10,9... | collective-permute-start | bytes 497672 | tf_op jit(solution)/shard_map/ppermute | solution.py:257
  14.3 14.1 %collective-permute-start.1 = (bf16[3,72,384]{2,1,0:T(8,128)(2,1)S(1)}, bf16[3,72,384]{2,1,0:T(8,128)(2,1)S(1)}, u32[]{:S(2)}, u32[]{:S(2)}) collective-permute-start(bf16[3,72,384]{2,1,0:T(8,128)(2,1)S(1)} %pad_maximum_fusion.3), channel_id=1, source_target_pairs={{0,2},{1,3},{2,0},{3,1},{4,6},{5,7},{6,4},{7,5},{8,10},{9,11},{10,... | collective-permute-start | bytes 497672 | tf_op jit(solution)/shard_map/ppermute | solution.py:257
  14.3 14.1 %collective-permute-start = (bf16[3,72,384]{2,1,0:T(8,128)(2,1)S(1)}, bf16[3,72,384]{2,1,0:T(8,128)(2,1)S(1)}, u32[]{:S(2)}, u32[]{:S(2)}) collective-permute-start(bf16[3,72,384]{2,1,0:T(8,128)(2,1)S(1)} %pad_maximum_fusion.3), channel_id=1, source_target_pairs={{0,1},{1,2},{2,3},{3,0},{4,5},{5,6},{6,7},{7,4},{8,9},{9,10},{10,1... | collective-permute-start | bytes 497672 | tf_op jit(solution)/shard_map/ppermute | solution.py:257
  29.2 149.9 %all-gather.8.cloned.1.call-start = ((), (), s32[]{:S(2)}) async-start(), calls=%async_computation.1 | async-start | bytes 1492992 | tf_op jit(solution)/shard_map/all_gather | solution.py:1030
  30.1 8.0 %collective-permute-start.5 = (bf16[80,1536]{1,0:T(8,128)(2,1)S(1)}, bf16[80,1536]{1,0:T(8,128)(2,1)S(1)}, u32[]{:S(2)}, u32[]{:S(2)}) collective-permute-start(bf16[80,1536]{1,0:T(8,128)(2,1)S(1)} %pad_maximum_fusion.2), channel_id=1, source_target_pairs={{0,3},{1,0},{2,1},{3,2},{4,7},{5,4},{6,5},{7,6},{8,11},{9,8},{10,9... | collective-permute-start | bytes 737288 | tf_op jit(solution)/shard_map/ppermute | solution.py:257
  31.5 22.9 %collective-permute-start.4 = (bf16[80,1536]{1,0:T(8,128)(2,1)S(1)}, bf16[80,1536]{1,0:T(8,128)(2,1)S(1)}, u32[]{:S(2)}, u32[]{:S(2)}) collective-permute-start(bf16[80,1536]{1,0:T(8,128)(2,1)S(1)} %pad_maximum_fusion.2), channel_id=1, source_target_pairs={{0,2},{1,3},{2,0},{3,1},{4,6},{5,7},{6,4},{7,5},{8,10},{9,11},{10,... | collective-permute-start | bytes 737288 | tf_op jit(solution)/shard_map/ppermute | solution.py:257
  33.3 21.1 %collective-permute-start.3 = (bf16[80,1536]{1,0:T(8,128)(2,1)S(1)}, bf16[80,1536]{1,0:T(8,128)(2,1)S(1)}, u32[]{:S(2)}, u32[]{:S(2)}) collective-permute-start(bf16[80,1536]{1,0:T(8,128)(2,1)S(1)} %pad_maximum_fusion.2), channel_id=1, source_target_pairs={{0,1},{1,2},{2,3},{3,0},{4,5},{5,6},{6,7},{7,4},{8,9},{9,10},{10,1... | collective-permute-start | bytes 737288 | tf_op jit(solution)/shard_map/ppermute | solution.py:257
  86.9 5.3 %collective-permute-start.15 = (bf16[4,4,3,72,384]{4,3,2,1,0:T(8,128)(2,1)}, bf16[4,4,3,72,384]{4,3,2,1,0:T(8,128)(2,1)S(1)}, u32[]{:S(2)}, u32[]{:S(2)}) collective-permute-start(bf16[4,4,3,72,384]{4,3,2,1,0:T(8,128)(2,1)} %get-tuple-element.55), channel_id=1, source_target_pairs={{0,4},{4,0},{8,12},{12,8},{16,20},{20,16},{24,28},{28,24},{1,5},{5... | collective-permute-start | bytes 7962632 | tf_op jit(solution)/shard_map/ppermute | solution.py:927
  94.0 17.3 %collective-permute-start.19 = (bf16[2,2,3,72,384]{4,3,2,1,0:T(8,128)(2,1)S(1)}, bf16[2,2,3,72,384]{4,3,2,1,0:T(8,128)(2,1)S(1)}, u32[]{:S(2)}, u32[]{:S(2)}) collective-permute-start(bf16[2,2,3,72,384]{4,3,2,1,0:T(8,128)(2,1)S(1)} %get-tuple-element.93), channel_id=1, source_target_pairs={{0,16},{4,20},{8,24},{12,28},{16,0},{20,4},{24,8},{28,12},{1,17},{... | collective-permute-start | bytes 1990664 | tf_op jit(solution)/shard_map/ppermute | solution.py:927
  95.9 29.1 %collective-permute-start.16 = (bf16[2,2,3,72,384]{4,3,2,1,0:T(8,128)(2,1)S(1)}, bf16[2,2,3,72,384]{4,3,2,1,0:T(8,128)(2,1)S(1)}, u32[]{:S(2)}, u32[]{:S(2)}) collective-permute-start(bf16[2,2,3,72,384]{4,3,2,1,0:T(8,128)(2,1)S(1)} %get-tuple-element.95), channel_id=1, source_target_pairs={{0,8},{4,12},{8,0},{12,4},{16,24},{20,28},{24,16},{28,20},{1,9},{5... | collective-permute-start | bytes 1990664 | tf_op jit(solution)/shard_map/ppermute | solution.py:927
  111.3 15.4 %collective-permute-start.20 = (bf16[2,3,72,384]{3,2,1,0:T(8,128)(2,1)S(1)}, bf16[2,3,72,384]{3,2,1,0:T(8,128)(2,1)S(1)}, u32[]{:S(2)}, u32[]{:S(2)}) collective-permute-start(bf16[2,3,72,384]{3,2,1,0:T(8,128)(2,1)S(1)} %fusion.10), channel_id=1, source_target_pairs={{0,8},{4,12},{8,0},{12,4},{16,24},{20,28},{24,16},{28,20},{1,9},{5... | collective-permute-start | bytes 995336 | tf_op jit(solution)/shard_map/ppermute | solution.py:927
  125.0 19.2 %collective-permute-start.7 = (bf16[4,4,80,384]{3,2,1,0:T(8,128)(2,1)}, bf16[4,4,80,384]{3,2,1,0:T(8,128)(2,1)S(1)}, u32[]{:S(2)}, u32[]{:S(2)}) collective-permute-start(bf16[4,4,80,384]{3,2,1,0:T(8,128)(2,1)} %get-tuple-element.49), channel_id=1, source_target_pairs={{0,4},{4,0},{8,12},{12,8},{16,20},{20,16},{24,28},{28,24},{1,5},{5... | collective-permute-start | bytes 2949128 | tf_op jit(solution)/shard_map/ppermute | solution.py:927
  125.1 10.3 %collective-permute-start.17 = (bf16[2,3,72,384]{3,2,1,0:T(8,128)(2,1)S(1)}, bf16[2,3,72,384]{3,2,1,0:T(8,128)(2,1)S(1)}, u32[]{:S(2)}, u32[]{:S(2)}) collective-permute-start(bf16[2,3,72,384]{3,2,1,0:T(8,128)(2,1)S(1)} %fusion.9), channel_id=1, source_target_pairs={{0,16},{4,20},{8,24},{12,28},{16,0},{20,4},{24,8},{28,12},{1,17},{... | collective-permute-start | bytes 995336 | tf_op jit(solution)/shard_map/ppermute | solution.py:927
  126.9 9.0 %collective-permute-start.21 = (bf16[3,72,384]{2,1,0:T(8,128)(2,1)S(1)}, bf16[3,72,384]{2,1,0:T(8,128)(2,1)S(1)}, u32[]{:S(2)}, u32[]{:S(2)}) collective-permute-start(bf16[3,72,384]{2,1,0:T(8,128)(2,1)S(1)} %get-tuple-element.100), channel_id=1, source_target_pairs={{0,2},{1,3},{2,0},{3,1},{4,6},{5,7},{6,4},{7,5},{8,10},{9,11},{10,... | collective-permute-start | bytes 497672 | tf_op jit(solution)/shard_map/ppermute | solution.py:257
  127.1 9.8 %collective-permute-start.22 = (bf16[3,72,384]{2,1,0:T(8,128)(2,1)S(1)}, bf16[3,72,384]{2,1,0:T(8,128)(2,1)S(1)}, u32[]{:S(2)}, u32[]{:S(2)}) collective-permute-start(bf16[3,72,384]{2,1,0:T(8,128)(2,1)S(1)} %get-tuple-element.101), channel_id=1, source_target_pairs={{0,3},{1,0},{2,1},{3,2},{4,7},{5,4},{6,5},{7,6},{8,11},{9,8},{10,9... | collective-permute-start | bytes 497672 | tf_op jit(solution)/shard_map/ppermute | solution.py:257
  135.6 7.9 %collective-permute-start.18 = (bf16[3,72,384]{2,1,0:T(8,128)(2,1)S(1)}, bf16[3,72,384]{2,1,0:T(8,128)(2,1)S(1)}, u32[]{:S(2)}, u32[]{:S(2)}) collective-permute-start(bf16[3,72,384]{2,1,0:T(8,128)(2,1)S(1)} %fusion.24), channel_id=1, source_target_pairs={{0,1},{1,2},{2,3},{3,0},{4,5},{5,6},{6,7},{7,4},{8,9},{9,10},{10,1... | collective-permute-start | bytes 497672 | tf_op jit(solution)/shard_map/ppermute | solution.py:257
  144.4 6.8 %collective-permute-start.11 = (bf16[2,2,80,384]{3,2,1,0:T(8,128)(2,1)S(1)}, bf16[2,2,80,384]{3,2,1,0:T(8,128)(2,1)S(1)}, u32[]{:S(2)}, u32[]{:S(2)}) collective-permute-start(bf16[2,2,80,384]{3,2,1,0:T(8,128)(2,1)S(1)} %get-tuple-element.97), channel_id=1, source_target_pairs={{0,16},{4,20},{8,24},{12,28},{16,0},{20,4},{24,8},{28,12},{1,17},{... | collective-permute-start | bytes 737288 | tf_op jit(solution)/shard_map/ppermute | solution.py:927
  146.1 8.6 %collective-permute-start.8 = (bf16[2,2,80,384]{3,2,1,0:T(8,128)(2,1)S(1)}, bf16[2,2,80,384]{3,2,1,0:T(8,128)(2,1)S(1)}, u32[]{:S(2)}, u32[]{:S(2)}) collective-permute-start(bf16[2,2,80,384]{3,2,1,0:T(8,128)(2,1)S(1)} %get-tuple-element.99), channel_id=1, source_target_pairs={{0,8},{4,12},{8,0},{12,4},{16,24},{20,28},{24,16},{28,20},{1,9},{5... | collective-permute-start | bytes 737288 | tf_op jit(solution)/shard_map/ppermute | solution.py:927
  151.2 5.8 %collective-permute-start.12 = (bf16[2,80,384]{2,1,0:T(8,128)(2,1)S(1)}, bf16[2,80,384]{2,1,0:T(8,128)(2,1)S(1)}, u32[]{:S(2)}, u32[]{:S(2)}) collective-permute-start(bf16[2,80,384]{2,1,0:T(8,128)(2,1)S(1)} %fusion.26), channel_id=1, source_target_pairs={{0,8},{4,12},{8,0},{12,4},{16,24},{20,28},{24,16},{28,20},{1,9},{5... | collective-permute-start | bytes 368648 | tf_op jit(solution)/shard_map/ppermute | solution.py:927
  154.8 4.9 %collective-permute-start.9 = (bf16[2,80,384]{2,1,0:T(8,128)(2,1)S(1)}, bf16[2,80,384]{2,1,0:T(8,128)(2,1)S(1)}, u32[]{:S(2)}, u32[]{:S(2)}) collective-permute-start(bf16[2,80,384]{2,1,0:T(8,128)(2,1)S(1)} %fusion.25), channel_id=1, source_target_pairs={{0,16},{4,20},{8,24},{12,28},{16,0},{20,4},{24,8},{28,12},{1,17},{... | collective-permute-start | bytes 368648 | tf_op jit(solution)/shard_map/ppermute | solution.py:927
  157.1 6.1 %collective-permute-start.13 = (bf16[80,384]{1,0:T(8,128)(2,1)S(1)}, bf16[80,384]{1,0:T(8,128)(2,1)S(1)}, u32[]{:S(2)}, u32[]{:S(2)}) collective-permute-start(bf16[80,384]{1,0:T(8,128)(2,1)S(1)} %get-tuple-element.102), channel_id=1, source_target_pairs={{0,2},{1,3},{2,0},{3,1},{4,6},{5,7},{6,4},{7,5},{8,10},{9,11},{10,... | collective-permute-start | bytes 184328 | tf_op jit(solution)/shard_map/ppermute | solution.py:257
  157.6 5.6 %collective-permute-start.14 = (bf16[80,384]{1,0:T(8,128)(2,1)S(1)}, bf16[80,384]{1,0:T(8,128)(2,1)S(1)}, u32[]{:S(2)}, u32[]{:S(2)}) collective-permute-start(bf16[80,384]{1,0:T(8,128)(2,1)S(1)} %get-tuple-element.103), channel_id=1, source_target_pairs={{0,3},{1,0},{2,1},{3,2},{4,7},{5,4},{6,5},{7,6},{8,11},{9,8},{10,9... | collective-permute-start | bytes 184328 | tf_op jit(solution)/shard_map/ppermute | solution.py:257
  159.8 6.1 %collective-permute-start.10 = (bf16[80,384]{1,0:T(8,128)(2,1)S(1)}, bf16[80,384]{1,0:T(8,128)(2,1)S(1)}, u32[]{:S(2)}, u32[]{:S(2)}) collective-permute-start(bf16[80,384]{1,0:T(8,128)(2,1)S(1)} %fusion.30), channel_id=1, source_target_pairs={{0,1},{1,2},{2,3},{3,0},{4,5},{5,6},{6,7},{7,4},{8,9},{9,10},{10,1... | collective-permute-start | bytes 184328 | tf_op jit(solution)/shard_map/ppermute | solution.py:257
  (19 other events, 316.7 us)
Sparse Core Ops, SparseCore 0:
  29.3 36.2 all-gather.5
  144.4 23.3 all-gather.7

commit v2 on v1

--- a/solution.py
+++ b/solution.py
@@ -445,6 +445,7 @@
 
 TOKENS = 384
 CHUNK = 384
+LANES = 128
 GROUPS = KEY_VALUE_HEADS
 SHARE = QUERY_HEADS // KEY_VALUE_HEADS
 VMEM_LIMIT = 56 * 1024 * 1024
@@ -464,8 +465,9 @@
     return values.astype(jnp.bfloat16)
 
 
-def mask_bias(seg_col, seg_row):
+def mask_bias(seg_row):
     shape = (TOKENS, TOKENS)
+    seg_col = jnp.transpose(jnp.broadcast_to(seg_row, (LANES, TOKENS)))[:, 0:1]
     key_at = lax.broadcasted_iota(jnp.int32, shape, 0)
     query_at = lax.broadcasted_iota(jnp.int32, shape, 1)
     allowed = (key_at <= query_at) & (seg_col == seg_row)
@@ -481,14 +483,14 @@
 
 
 def attention_forward_kernel(
-    shards, at_ref, x_ref, col_ref, row_ref, cos_ref, sin_ref, own_ref, gain_own_ref, mine_ref,
+    shards, at_ref, x_ref, row_ref, cos_ref, sin_ref, own_ref, gain_own_ref, mine_ref,
     pair_ref, w_ref, gain_ref, x2_ref, q_ref, k_ref, v_ref, o_ref, lse_ref, bias_ref,
 ):
     z = at_ref[0]
     first_core = at_ref[2] == 0
     rows = own_ref.shape[0]
     half = rows // 2
-    width = x_ref.shape[1]
+    width = x_ref.shape[0]
     own_at = pl.multiple_of(z * rows, 16)
     w_ref[pl.ds(own_at, rows), :] = own_ref[...]
     gains = widen(gain_own_ref[...])
@@ -499,17 +501,15 @@
         upper = jnp.where(first_core, mine, pair)
         lower = jnp.where(first_core, pair, mine)
         w_ref[pl.ds(at, rows), :] = narrow(jnp.concatenate([upper, lower], axis=0))
-    gain_attn = gains[0:1, :width]
-    gain_mlp = gains[1:2, :width]
-    gain_ref[0:1, :] = gain_attn
-    gain_ref[1:2, :] = gain_mlp
+    turned = jnp.transpose(jnp.concatenate([gains[:, : 5 * LANES]] * (LANES // 8), axis=0))
+    gain_ref[...] = turned[:width]
     x = widen(x_ref[...])
-    inverse = lax.rsqrt(jnp.mean(x * x, axis=-1, keepdims=True) + EPSILON)
-    h1 = narrow(x * inverse * gain_attn)
-    kv = jnp.transpose(dot(h1, w_ref[:, :CHUNK]))
-    q = jnp.transpose(dot(h1, w_ref[:, 896:]))[HEAD_WIDTH:]
+    inverse = lax.rsqrt(jnp.mean(x * x, axis=0, keepdims=True) + EPSILON)
+    h1 = narrow(x * inverse * turned[:width, 0:1])
+    kv = dot(w_ref[:, :CHUNK], h1, 0, 0)
+    q = dot(w_ref[:, 896:], h1, 0, 0)[HEAD_WIDTH:]
     cosine, sine = cos_ref[...], sin_ref[...]
-    bias_ref[...] = mask_bias(col_ref[...], row_ref[...])
+    bias_ref[...] = mask_bias(row_ref[...])
     for g in range(GROUPS):
         at = g * HEAD_WIDTH
         k_ref[g] = narrow(turn(kv[at : at + HEAD_WIDTH], cosine, sine))
@@ -534,7 +534,7 @@
         return carry
 
     lax.fori_loop(0, GROUPS, one_group, 0)
-    x2_ref[...] = x + dot(joined_heads(o_ref), w_ref[:, CHUNK : CHUNK + width], 0, 0)
+    x2_ref[...] = x + dot(w_ref[:, CHUNK : CHUNK + width], joined_heads(o_ref), 0, 0)
 
 
 def joined_heads(ref):
@@ -548,8 +548,8 @@
     )
 
 
-def attention_forward(at, x, col, row, cosine, sine, own, gain_own, mine, pair, shards):
-    width = x.shape[1]
+def attention_forward(at, x, row, cosine, sine, own, gain_own, mine, pair, shards):
+    width = x.shape[0]
     cells = SHARE * TOKENS
     bf16, f32 = jnp.bfloat16, jnp.float32
 
@@ -561,14 +561,14 @@
         grid_spec=pltpu.PrefetchScalarGridSpec(
             num_scalar_prefetch=1,
             grid=(),
-            in_specs=[pl.BlockSpec(memory_space=pltpu.VMEM)] * 9,
+            in_specs=[pl.BlockSpec(memory_space=pltpu.VMEM)] * 8,
             out_specs=[pl.BlockSpec(memory_space=pltpu.VMEM)] * 8,
             scratch_shapes=[pltpu.VMEM((TOKENS, TOKENS), f32)],
         ),
         out_shape=[
             jax.ShapeDtypeStruct((shards * own.shape[0], own.shape[1]), bf16),
-            jax.ShapeDtypeStruct((8, width), f32),
-            jax.ShapeDtypeStruct((TOKENS, width), f32),
+            jax.ShapeDtypeStruct((width, LANES), f32),
+            jax.ShapeDtypeStruct((width, TOKENS), f32),
             jax.ShapeDtypeStruct((GROUPS, HEAD_WIDTH, cells), bf16),
             jax.ShapeDtypeStruct((GROUPS, HEAD_WIDTH, TOKENS), bf16),
             jax.ShapeDtypeStruct((GROUPS, HEAD_WIDTH, TOKENS), bf16),
@@ -580,13 +580,13 @@
             flops=int(1.5e9), bytes_accessed=8000000, transcendentals=2000000
         ),
         name="attention_forward",
-    )(at, x, col, row, cosine, sine, own, gain_own, mine, pair)
+    )(at, x, row, cosine, sine, own, gain_own, mine, pair)
 
 
 def mlp_kernel(
-    shards, at_ref, x2_ref, ct_ref, gain_ref, gate_ref, up_ref, tall_ref, wide_ref, tall_other_ref,
+    shards, at_ref, x2_ref, ctt_ref, gain_ref, gate_ref, up_ref, tall_ref, wide_ref, tall_other_ref,
     out_ref, dx2_ref, gain_grad_ref, keep_ref, send_ref,
-    u2_ref, h2_ref, h2t_ref, ctt_ref, acc_ref, dh2_ref, wg_ref, wu_ref, wd_ref,
+    h2_ref, h2t_ref, ct_ref, acc_ref, dh2_ref, wg_ref, wu_ref, wd_ref,
     gg_ref, gu_ref, gd_ref,
 ):
     z, chip, core = at_ref[0], at_ref[1], at_ref[2]
@@ -597,13 +597,11 @@
     @pl.when(j == 0)
     def _():
         x2 = x2_ref[...]
-        inverse = lax.rsqrt(jnp.mean(x2 * x2, axis=-1, keepdims=True) + EPSILON)
-        u2 = x2 * inverse
-        u2_ref[...] = u2
-        h2 = narrow(u2 * gain_ref[1:2, :])
-        h2_ref[...] = h2
-        h2t_ref[...] = narrow(jnp.transpose(widen(h2)))
-        ctt_ref[...] = narrow(jnp.transpose(widen(ct_ref[...])))
+        inverse = lax.rsqrt(jnp.mean(x2 * x2, axis=0, keepdims=True) + EPSILON)
+        h2t = x2 * inverse * gain_ref[:, 1:2]
+        h2t_ref[...] = narrow(h2t)
+        h2_ref[...] = narrow(jnp.transpose(h2t))
+        ct_ref[...] = narrow(jnp.transpose(widen(ctt_ref[...])))
         acc_ref[...] = x2
         dh2_ref[...] = jnp.zeros_like(dh2_ref)
 
@@ -634,8 +632,8 @@
     act = narrow(silu * up)
     dg = narrow(da * up * sigmoid * (1.0 + gate * (1.0 - sigmoid)))
     du = narrow(da * silu)
-    acc_ref[...] += dot(act, wd, 1, 1)
-    dh2_ref[...] += dot(dg, wg, 1, 1) + dot(du, wu, 1, 1)
+    acc_ref[...] += dot(wd, act, 1, 1)
+    dh2_ref[...] += dot(wg, dg, 1, 1) + dot(wu, du, 1, 1)
     gg_ref[...] = dot(h2t_ref[...], dg)
     gu_ref[...] = dot(h2t_ref[...], du)
     gd_ref[...] = dot(ctt_ref[...], act)
@@ -656,16 +654,18 @@
     @pl.when(j == pl.num_programs(0) - 1)
     def _():
         out_ref[...] = narrow(acc_ref[...])
-        dh2, u2, x2 = dh2_ref[...], u2_ref[...], x2_ref[...]
-        inverse = lax.rsqrt(jnp.mean(x2 * x2, axis=-1, keepdims=True) + EPSILON)
-        gain_grad_ref[0:1, :] = jnp.sum(dh2 * u2, axis=0, keepdims=True)
-        n2 = dh2 * gain_ref[1:2, :]
-        mean = jnp.mean(n2 * u2, axis=-1, keepdims=True)
-        dx2_ref[...] = widen(ct_ref[...]) + inverse * (n2 - u2 * mean)
+        dh2, x2 = dh2_ref[...], x2_ref[...]
+        inverse = lax.rsqrt(jnp.mean(x2 * x2, axis=0, keepdims=True) + EPSILON)
+        u2 = x2 * inverse
+        gain_grad = jnp.sum(dh2 * u2, axis=1, keepdims=True)
+        gain_grad_ref[...] = jnp.broadcast_to(gain_grad, gain_grad_ref.shape)
+        n2 = dh2 * gain_ref[:, 1:2]
+        mean = jnp.mean(n2 * u2, axis=0, keepdims=True)
+        dx2_ref[...] = widen(ctt_ref[...]) + inverse * (n2 - u2 * mean)
 
 
 def mlp(at, x2, ct, gains, gate, up, tall, gathered, shards):
-    width = x2.shape[1]
+    width = x2.shape[0]
     copies = gathered.shape[0]
     rows, ff = gate.shape
     half = rows // 2
@@ -684,9 +684,9 @@
             num_scalar_prefetch=1,
             grid=(ff // CHUNK,),
             in_specs=[
-                whole((TOKENS, width)),
-                whole((TOKENS, width)),
-                whole((8, width)),
+                whole((width, TOKENS)),
+                whole((width, TOKENS)),
+                whole((width, LANES)),
                 pl.BlockSpec((rows, CHUNK), lambda j, at_ref: (0, j)),
                 pl.BlockSpec((rows, CHUNK), lambda j, at_ref: (0, j)),
                 whole((width, CHUNK)),
@@ -694,19 +694,18 @@
                 pl.BlockSpec((copies, 1, 1, half, CHUNK), tall_block),
             ],
             out_specs=[
-                whole((TOKENS, width)),
-                whole((TOKENS, width)),
-                whole((8, width)),
+                whole((width, TOKENS)),
+                whole((width, TOKENS)),
+                whole((width, LANES)),
                 whole((copies // 2, shards, 3, half, CHUNK)),
                 whole((copies // 2, shards, 3, half, CHUNK)),
             ],
             scratch_shapes=[
-                pltpu.VMEM((TOKENS, width), f32),
                 pltpu.VMEM((TOKENS, width), bf16),
                 pltpu.VMEM((width, TOKENS), bf16),
-                pltpu.VMEM((width, TOKENS), bf16),
-                pltpu.VMEM((TOKENS, width), f32),
-                pltpu.VMEM((TOKENS, width), f32),
+                pltpu.VMEM((TOKENS, width), bf16),
+                pltpu.VMEM((width, TOKENS), f32),
+                pltpu.VMEM((width, TOKENS), f32),
                 pltpu.VMEM((width, CHUNK), bf16),
                 pltpu.VMEM((width, CHUNK), bf16),
                 pltpu.VMEM((width, CHUNK), bf16),
@@ -716,9 +715,9 @@
             ],
         ),
         out_shape=[
-            jax.ShapeDtypeStruct((TOKENS, width), bf16),
-            jax.ShapeDtypeStruct((TOKENS, width), f32),
-            jax.ShapeDtypeStruct((8, width), f32),
+            jax.ShapeDtypeStruct((width, TOKENS), bf16),
+            jax.ShapeDtypeStruct((width, TOKENS), f32),
+            jax.ShapeDtypeStruct((width, LANES), f32),
             jax.ShapeDtypeStruct((copies // 2, shards, 3, half, CHUNK), bf16),
             jax.ShapeDtypeStruct((copies // 2, shards, 3, half, CHUNK), bf16),
         ],
@@ -733,24 +732,24 @@
 
 
 def attention_backward_kernel(
-    shards, at_ref, x_ref, dx2_ref, col_ref, row_ref, cos_ref, sin_ref, w_ref, gain_ref, q_ref,
+    shards, at_ref, x_ref, dx2_ref, row_ref, cos_ref, sin_ref, w_ref, gain_ref, q_ref,
     k_ref, v_ref, o_ref, lse_ref, gain_grad_ref,
     dx_ref, keep_ref, send_ref,
     bias_ref, do_ref, dq_ref, dk_ref, dv_ref, grad_ref,
 ):
     z, chip, core = at_ref[0], at_ref[1], at_ref[2]
-    width = x_ref.shape[1]
+    width = x_ref.shape[0]
     rows = width // shards
     half = rows // 2
     x = widen(x_ref[...])
-    inverse = lax.rsqrt(jnp.mean(x * x, axis=-1, keepdims=True) + EPSILON)
+    inverse = lax.rsqrt(jnp.mean(x * x, axis=0, keepdims=True) + EPSILON)
     u1 = x * inverse
-    gain_attn = gain_ref[0:1, :]
-    h1t = narrow(jnp.transpose(u1 * gain_attn))
+    gain_attn = gain_ref[:, 0:1]
+    h1t = narrow(u1 * gain_attn)
     gx = narrow(dx2_ref[...])
     cosine, sine = cos_ref[...], sin_ref[...]
-    bias_ref[...] = mask_bias(col_ref[...], row_ref[...])
-    do = narrow(dot(w_ref[:, CHUNK : CHUNK + width], gx, 1, 1))
+    bias_ref[...] = mask_bias(row_ref[...])
+    do = narrow(dot(w_ref[:, CHUNK : CHUNK + width], gx))
     for g in range(GROUPS):
         for r in range(SHARE):
             at = (g * SHARE + r) * HEAD_WIDTH
@@ -781,12 +780,14 @@
     zeros = jnp.zeros((HEAD_WIDTH, TOKENS), jnp.bfloat16)
     dq_padded = jnp.concatenate([zeros] + dq, axis=0)
     dq = jnp.concatenate(dq, axis=0)
-    dh1 = jnp.transpose(dot(w_ref[:, :CHUNK], dkv) + dot(w_ref[:, 896:], dq_padded))
-    gain_grad = jnp.sum(dh1 * u1, axis=0, keepdims=True)
+    dh1 = dot(w_ref[:, :CHUNK], dkv) + dot(w_ref[:, 896:], dq_padded)
+    gain_grad = jnp.sum(dh1 * u1, axis=1, keepdims=True)
+    lane = lax.broadcasted_iota(jnp.int32, gain_grad_ref.shape, 1)
+    both = jnp.transpose(jnp.where(lane == 0, gain_grad, gain_grad_ref[...]))
+    gain_grad, gain_mlp_grad = both[0:1], both[1:2]
     n1 = dh1 * gain_attn
-    mean = jnp.mean(n1 * u1, axis=-1, keepdims=True)
+    mean = jnp.mean(n1 * u1, axis=0, keepdims=True)
     dx_ref[...] = dx2_ref[...] + inverse * (n1 - u1 * mean)
-    gain_mlp_grad = gain_grad_ref[0:1, :]
     tail = width - CHUNK
     blank = jnp.zeros((1, CHUNK - tail), jnp.float32)
     extra = jnp.concatenate(
@@ -804,10 +805,10 @@
         if c == 0:
             grad = dot(h1t, dkv, 1, 1)
         elif c == 1:
-            grad = dot(o, gx[:, :CHUNK])
+            grad = dot(o, gx[:CHUNK], 1, 1)
         elif c == 2:
             grad = jnp.concatenate(
-                [dot(o, gx[:, CHUNK:]), dot(h1t, dq[: CHUNK - tail], 1, 1)], axis=1
+                [dot(o, gx[CHUNK:], 1, 1), dot(h1t, dq[: CHUNK - tail], 1, 1)], axis=1
             )
         else:
             grad = dot(h1t, dq[CHUNK - tail :], 1, 1)
@@ -824,7 +825,7 @@
 
 def attention_backward(at, args, shards, copies):
     x = args[0]
-    width = x.shape[1]
+    width = x.shape[0]
     half = width // shards // 2
     cells = SHARE * TOKENS
     bf16, f32 = jnp.bfloat16, jnp.float32
@@ -849,7 +850,7 @@
             ],
         ),
         out_shape=[
-            jax.ShapeDtypeStruct((TOKENS, width), f32),
+            jax.ShapeDtypeStruct((width, TOKENS), f32),
             jax.ShapeDtypeStruct((copies // 2, shards, half + 8, CHUNK), bf16),
             jax.ShapeDtypeStruct((copies // 2, shards, half + 8, CHUNK), bf16),
         ],
@@ -884,7 +885,7 @@
     )(pieces)
 
 
-def unpack_mlp_kernel(piece_ref, gate_ref, up_ref, down_ref):
+def unpack_mlp_kernel(piece_ref, gate_ref, up_ref, tall_ref):
     half = piece_ref.shape[2]
     for c in range(piece_ref.shape[0] // 2):
         for h in range(2):
@@ -892,8 +893,8 @@
                 ref[h * half : (h + 1) * half, c * CHUNK : (c + 1) * CHUNK] = widen(
                     piece_ref[2 * c + h, m]
                 )
-    tall = [widen(piece_ref[r, 2]) for r in range(piece_ref.shape[0])]
-    down_ref[...] = jnp.transpose(jnp.concatenate(tall, axis=0))
+    for r in range(piece_ref.shape[0]):
+        tall_ref[r * half : (r + 1) * half, :] = widen(piece_ref[r, 2])
 
 
 def unpack_mlp(pieces, shapes):
@@ -931,7 +932,7 @@
     return narrow(widen(left) + widen(right))
 
 
-def sum_in_plane(keep, came):
+def exchange_one(keep, came):
     tail = keep.shape[1:]
     mid = tail[0] // 2
     keep = keep.reshape((2, 2) + tail)
@@ -940,20 +941,29 @@
     b_came = swapped(plus(keep[1, :, mid:], came[1, :, mid:]), 4)
     a_keep = plus(keep[:, 0, :mid], came[:, 0, :mid])
     b_keep = plus(keep[0, :, mid:], came[0, :, mid:])
+    return a_keep, b_keep, a_came, b_came
+
+
+def exchange_two(a_keep, b_keep, a_came, b_came):
     a_last = swapped(plus(a_keep[1], a_came[1]), 4)
     b_last = swapped(plus(b_keep[1], b_came[1]), 2)
+    return a_last, b_last
+
+
+def own_blocks(a_keep, b_keep, a_came, b_came, a_last, b_last):
     a = widen(a_keep[0]) + widen(a_came[0]) + widen(a_last)
     b = widen(b_keep[0]) + widen(b_came[0]) + widen(b_last)
-    return a, b
-
-
-def sum_along_shard(a, b):
-    blocks = [a[i] for i in range(a.shape[0])] + [b[i] for i in range(b.shape[0])]
-    came = [shifted(narrow(blocks[k]), k) for k in range(1, len(blocks))]
-    total = blocks[0]
+    return [a[i] for i in range(a.shape[0])] + [b[i] for i in range(b.shape[0])]
+
+
+def exchange_shards(blocks):
+    return [shifted(narrow(blocks[k]), k) for k in range(1, len(blocks))]
+
+
+def added(block, came):
     for value in came:
-        total = total + widen(value)
-    return total
+        block = block + widen(value)
+    return block
 
 
 def on_device(
@@ -992,28 +1002,28 @@
     at = jnp.stack([lax.axis_index("shard"), rank // 2, rank % 2]).astype(jnp.int32)
     tall = jnp.transpose(down_weight)
     wide = jnp.stack([piece_of(gate_weight), piece_of(up_weight), row_piece_of(tall)])
-    wide_others = fetch_others(wide)
-    wide_pieces = lax.all_gather(wide_others, "rep")
+    wide_came = [shifted(wide, k) for k in range(1, shards)]
+    wide_pieces = lax.all_gather(jnp.stack(wide_came), "rep")
+    half_dim = HEAD_WIDTH // 2
+    frequency = ROPE_BASE ** (-(jnp.arange(half_dim, dtype=jnp.float32) * 2.0 / HEAD_WIDTH))
+    angles = frequency[:, None] * positions.astype(jnp.float32)
+    cosine, sine = jnp.cos(angles), jnp.sin(angles)
+    row = segment_ids
+    x = jnp.transpose(block_input[0])
+    ct = jnp.transpose(layer_output_cotangent[0])
     own = jnp.concatenate([key_weight, value_weight, output_weight, query_weight], axis=1)
     gains_own = gain_rows(gain_attn, gain_mlp, own.shape[1])
     rows = own.shape[0]
     own_half = lax.dynamic_slice_in_dim(own, (rank % 2) * (rows // 2), rows // 2, 0)
     own_half = jnp.concatenate([own_half, gains_own])
-    own_half, _ = lax.optimization_barrier((own_half, wide_others))
+    own_half, own, gains_own, cosine, sine, at, _ = lax.optimization_barrier(
+        (own_half, own, gains_own, cosine, sine, at, wide_came[0])
+    )
     mine = fetch_others(own_half)
     pair = swapped(mine, 1)
 
-    half_dim = HEAD_WIDTH // 2
-    frequency = ROPE_BASE ** (-(jnp.arange(half_dim, dtype=jnp.float32) * 2.0 / HEAD_WIDTH))
-    angles = frequency[:, None] * positions.astype(jnp.float32)
-    cosine, sine = jnp.cos(angles), jnp.sin(angles)
-    row = segment_ids
-    col = segment_ids.reshape(-1, 1)
-    x = block_input[0]
-    ct = layer_output_cotangent[0]
-
     w, gains, x2, q, k, v, o, lse = attention_forward(
-        at, x, col, row, cosine, sine, own, gains_own, mine, pair, shards
+        at, x, row, cosine, sine, own, gains_own, mine, pair, shards
     )
     out, dx2, gain_mlp_grad, wide_keep, wide_send = mlp(
         at, x2, ct, gains, gate_weight, up_weight, tall, wide_pieces, shards
@@ -1021,16 +1031,28 @@
     wide_came = swapped(wide_send, 1)
     dx, attn_keep, attn_send = attention_backward(
         at,
-        (x, dx2, col, row, cosine, sine, w, gains, q, k, v, o, lse, gain_mlp_grad),
+        (x, dx2, row, cosine, sine, w, gains, q, k, v, o, lse, gain_mlp_grad),
         shards,
         copies,
     )
-    wide_total = narrow(sum_along_shard(*sum_in_plane(wide_keep, wide_came)))
-    gate_grad, up_grad, down_grad = unpack_mlp(
+    barrier = lax.optimization_barrier
+    wide_one = exchange_one(wide_keep, wide_came)
+    wide_one, attn_send = barrier((wide_one, attn_send))
+    attn_came = swapped(attn_send, 1)
+    wide_two = exchange_two(*wide_one)
+    wide_two, attn_came = barrier((wide_two, attn_came))
+    wide_blocks = own_blocks(*wide_one, *wide_two)
+    attn_one = exchange_one(attn_keep, attn_came)
+    wide_last = exchange_shards(wide_blocks)
+    wide_last, attn_one = barrier((wide_last, attn_one))
+    wide_total = narrow(added(wide_blocks[0], wide_last))
+    attn_two = exchange_two(*attn_one)
+    attn_blocks = own_blocks(*attn_one, *attn_two)
+    attn_total = added(attn_blocks[0], exchange_shards(attn_blocks))
+    gate_grad, up_grad, tall_grad = unpack_mlp(
         lax.all_gather(wide_total, "rep"),
-        (gate_weight.shape, up_weight.shape, down_weight.shape),
-    )
-    attn_total = sum_along_shard(*sum_in_plane(attn_keep, swapped(attn_send, 1)))
+        (gate_weight.shape, up_weight.shape, tall.shape),
+    )
     half = rows // 2
     q_grad, k_grad, v_grad, o_grad = unpack_attn(
         lax.all_gather(narrow(attn_total[:half]), "rep"),
@@ -1039,15 +1061,15 @@
     both = attn_total[half : half + 4].reshape(2, 2 * CHUNK)
     both = lax.dynamic_slice(both, (0, lax.axis_index("shard") * rows), (2, rows))
     return (
-        out[None],
-        dx[None],
+        jnp.transpose(out)[None],
+        jnp.transpose(dx)[None],
         q_grad,
         k_grad,
         v_grad,
         o_grad,
         gate_grad,
         up_grad,
-        down_grad,
+        jnp.transpose(tall_grad),
         both[0],
         both[1],
     )

time: 192 us -> 180 us (0.938)
  waiting for transfers between devices: 79.2 us -> 71.5 us
  local copies, waits for them, and re-layouts: 11.6 us -> 4.47 us
    ppermute x11, waiting for transfers between devices: 36 us -> 21.6 us  [swapped(): return lax.ppermute(values, 'rep', [(i, i ^ bit) for i in range(size)])]
    ppermute x12, waiting for transfers between devices: 43.2 us -> 49.8 us  [shifted(): lax.ppermute(values, 'shard', [(i, (i + steps) % size) for i in range(siz...]
    unnamed x41 -> x26, local copies, waits for them, and re-layouts: 7.59 us -> 1.27 us
    ppermute x12, starting transfers between devices: 15.4 us -> 17.3 us  [shifted(): lax.ppermute(values, 'shard', [(i, (i + steps) % size) for i in range(siz...]
  transfers between devices with their start and end apart: 25 -> 25, of which waited for: 15 -> 17; matrix products, arithmetic and copies ran while one was open for 5% -> 2% of each run, Pallas kernels for 12% -> 13%
where the time goes in v2:
time: 180 us
  waiting for transfers between devices  71.5 us (40%)
  Pallas kernels  44.5 us (25%)
  starting transfers between devices  26.7 us (15%)
  between operations  14.5 us (8%)
  blocking collectives  12 us (7%)
  other arithmetic  6.36 us (4%)
  local copies, waits for them, and re-layouts  4.47 us (2%)
    ppermute x12, waiting for transfers between devices, shifted(): lax.ppermute(values, 'shard', [(i, (i + steps) % size) for i in range(siz...  49.8 us
    ppermute x11, waiting for transfers between devices, swapped(): return lax.ppermute(values, 'rep', [(i, i ^ bit) for i in range(size)])  21.6 us
    pallas_call x1, Pallas kernels, mlp(): pl.pallas_call(kernel, grid_spec=pltpu.PrefetchScalarGridSpec(num_scalar_...  18.9 us
    ppermute x12, starting transfers between devices, shifted(): lax.ppermute(values, 'shard', [(i, (i + steps) % size) for i in range(siz...  17.3 us
    pallas_call x1, Pallas kernels, attention_backward(): pl.pallas_call(kernel, grid_spec=pltpu.PrefetchScalarGridSpec(num_scalar_...  12.3 us
    all_gather x1, blocking collectives, on_device(): lax.all_gather(narrow(attn_total[:half]), 'rep')  12 us
    ppermute x11, starting transfers between devices, swapped(): return lax.ppermute(values, 'rep', [(i, i ^ bit) for i in range(size)])  9.31 us
    pallas_call x1, Pallas kernels, attention_forward(): pl.pallas_call(kernel, grid_spec=pltpu.PrefetchScalarGridSpec(num_scalar_...  8.33 us
  transfers between devices with their start and end apart: 25, of which 17 were waited for; matrix products, arithmetic and copies ran while one was open for 2% of the time, Pallas kernels for 13%

profile of v2, /device:TPU:0, one launch (start us, length us, event | category | flops | bytes accessed | tf_op | source)
XLA Modules:
  0.0 180.0 jit_solution(15456271907346580943)
XLA Ops:
  9.2 5.1 %collective-permute-start.6 = (bf16[3,72,384]{2,1,0:T(8,128)(2,1)S(1)}, bf16[3,72,384]{2,1,0:T(8,128)(2,1)S(1)}, u32[]{:S(2)}, u32[]{:S(2)}) collective-permute-start(bf16[3,72,384]{2,1,0:T(8,128)(2,1)S(1)} %pad_maximum_fusion.3), channel_id=1, source_target_pairs={{0,3},{1,0},{2,1},{3,2},{4,7},{5,4},{6,5},{7,6},{8,11},{9,8},{10,9... | collective-permute-start | bytes 497672 | tf_op jit(solution)/shard_map/ppermute | solution.py:257
  15.3 3.7 %collective-permute-done.6 = bf16[3,72,384]{2,1,0:T(8,128)(2,1)S(1)} collective-permute-done((bf16[3,72,384]{2,1,0:T(8,128)(2,1)S(1)}, bf16[3,72,384]{2,1,0:T(8,128)(2,1)S(1)}, u32[]{:S(2)}, u32[]{:S(2)}) %collective-permute-start.6) | collective-permute-done | bytes 165920 | tf_op jit(solution)/shard_map/ppermute | solution.py:257
  19.0 9.4 %collective-permute-done.5 = bf16[3,72,384]{2,1,0:T(8,128)(2,1)S(1)} collective-permute-done((bf16[3,72,384]{2,1,0:T(8,128)(2,1)S(1)}, bf16[3,72,384]{2,1,0:T(8,128)(2,1)S(1)}, u32[]{:S(2)}, u32[]{:S(2)}) %collective-permute-start.5) | collective-permute-done | bytes 165920 | tf_op jit(solution)/shard_map/ppermute | solution.py:257
  33.0 1.9 %collective-permute-start.2 = (bf16[80,1536]{1,0:T(8,128)(2,1)S(1)}, bf16[80,1536]{1,0:T(8,128)(2,1)S(1)}, u32[]{:S(2)}, u32[]{:S(2)}) collective-permute-start(bf16[80,1536]{1,0:T(8,128)(2,1)S(1)} %pad_maximum_fusion.2), channel_id=1, source_target_pairs={{0,2},{1,3},{2,0},{3,1},{4,6},{5,7},{6,4},{7,5},{8,10},{9,11},{10,... | collective-permute-start | bytes 737288 | tf_op jit(solution)/shard_map/ppermute | solution.py:257
  34.9 1.9 %collective-permute-start.1 = (bf16[80,1536]{1,0:T(8,128)(2,1)S(1)}, bf16[80,1536]{1,0:T(8,128)(2,1)S(1)}, u32[]{:S(2)}, u32[]{:S(2)}) collective-permute-start(bf16[80,1536]{1,0:T(8,128)(2,1)S(1)} %pad_maximum_fusion.2), channel_id=1, source_target_pairs={{0,1},{1,2},{2,3},{3,0},{4,5},{5,6},{6,7},{7,4},{8,9},{9,10},{10,1... | collective-permute-start | bytes 737288 | tf_op jit(solution)/shard_map/ppermute | solution.py:257
  36.8 2.8 %collective-permute-done.3 = bf16[80,1536]{1,0:T(8,128)(2,1)S(1)} collective-permute-done((bf16[80,1536]{1,0:T(8,128)(2,1)S(1)}, bf16[80,1536]{1,0:T(8,128)(2,1)S(1)}, u32[]{:S(2)}, u32[]{:S(2)}) %collective-permute-start.3) | collective-permute-done | bytes 245792 | tf_op jit(solution)/shard_map/ppermute | solution.py:257
  39.7 16.3 %collective-permute-done.2 = bf16[80,1536]{1,0:T(8,128)(2,1)S(1)} collective-permute-done((bf16[80,1536]{1,0:T(8,128)(2,1)S(1)}, bf16[80,1536]{1,0:T(8,128)(2,1)S(1)}, u32[]{:S(2)}, u32[]{:S(2)}) %collective-permute-start.2) | collective-permute-done | bytes 245792 | tf_op jit(solution)/shard_map/ppermute | solution.py:257
  56.2 2.2 %collective-permute-done.4.refs_8_ = bf16[3,80,1536]{2,1,0:T(8,128)(2,1)S(1)} collective-permute-done((bf16[3,80,1536]{2,1,0:T(8,128)(2,1)S(1)}, bf16[3,80,1536]{2,1,0:T(8,128)(2,1)S(1)}, u32[]{:S(2)}, u32[]{:S(2)}) %collective-permute-start.4) | collective-permute-done | bytes 737312 | tf_op jit(solution)/shard_map/ppermute | solution.py:928
  59.2 8.3 %attention_forward.1 = (bf16[576,1536]{1,0:T(8,128)(2,1)}, f32[576,128]{1,0:T(8,128)}, f32[576,384]{1,0:T(8,128)}, bf16[3,64,1152]{2,1,0:T(8,128)(2,1)}, bf16[3,...) custom-call(s32[3]{0:T(128)} %pad_add_fusion.refs_0_, ...), custom_call_target="tpu_custom_call" | custom-call | flops 1500000000 | bytes 8000000 | tf_op jit(solution)/shard_map/attention_forward/pallas_call | solution.py:559
  67.6 18.9 %mlp.1 = (bf16[576,384]{1,0:T(8,128)(2,1)}, f32[576,384]{1,0:T(8,128)}, f32[576,128]{1,0:T(8,128)}, bf16[4,4,3,72,384]{4,3,2,1,0:T(8,128)(2,1)}, bf16[4,4,3,72,384]{4,3,2,1,0:T(8,128)(2,1)}) custom-call(s32[3]{0:T(128)} %pad_add_fusion.refs_0_, f32[576,384]{1,0:T(8,128)} %get-tuple-element.61.refs_1_, bf16[576,384]{1,0:T(8,128)(2,1)} %bitcast.160, ...), custom_call_target="tpu_custom_call" | custom-call | flops 6200000000 | bytes 14000000 | tf_op jit(solution)/shard_map/mlp/pallas_call | solution.py:681
  86.6 5.0 %collective-permute-done.7 = bf16[4,4,3,72,384]{4,3,2,1,0:T(8,128)(2,1)S(1)} collective-permute-done((bf16[4,4,3,72,384]{4,3,2,1,0:T(8,128)(2,1)}, bf16[4,4,3,72,384]{4,3,2,1,0:T(8,128)(2,1)S(1)}, u32[]{:S(2)}, u32[]{:S(2)}) %collective-permute-start.7) | collective-permute-done | bytes 2654240 | tf_op jit(solution)/shard_map/ppermute | solution.py:928
  91.7 1.8 fusion.3
  97.3 12.3 %attention_backward.1 = (f32[576,384]{1,0:T(8,128)}, bf16[4,4,80,384]{3,2,1,0:T(8,128)(2,1)}, bf16[4,4,80,384]{3,2,1,0:T(8,128)(2,1)}) custom-call(s32[3]{0:T(128)} %pad_add_fusion.refs_0_, bf16[576,384]{1,0:T(8,128)(2,1)} %bitcast.162, f32[576,384]{1,0:T(8,128)} %get-tuple-element.64.refs_2_, s32[1,384]{1,0:T(1,128)} %refs_3_.1, ...), custom_call_target="tpu_custom_call" | custom-call | flops 3000000000 | bytes 9000000 | tf_op jit(solution)/shard_map/attention_backward/pallas_call | solution.py:836
  109.6 1.6 collective-permute-done.9
  114.8 8.1 %collective-permute-done.11 = bf16[2,3,72,384]{3,2,1,0:T(8,128)(2,1)S(1)} collective-permute-done((bf16[2,3,72,384]{3,2,1,0:T(8,128)(2,1)S(1)}, bf16[2,3,72,384]{3,2,1,0:T(8,128)(2,1)S(1)}, u32[]{:S(2)}, u32[]{:S(2)}) %collective-permute-start.11) | collective-permute-done | bytes 331808 | tf_op jit(solution)/shard_map/ppermute | solution.py:928
  126.0 3.8 %collective-permute-start.15 = (bf16[3,72,384]{2,1,0:T(8,128)(2,1)S(1)}, bf16[3,72,384]{2,1,0:T(8,128)(2,1)S(1)}, u32[]{:S(2)}, u32[]{:S(2)}) collective-permute-start(bf16[3,72,384]{2,1,0:T(8,128)(2,1)S(1)} %get-tuple-element.107), channel_id=1, source_target_pairs={{0,3},{1,0},{2,1},{3,2},{4,7},{5,4},{6,5},{7,6},{8,11},{9,8},{10,9... | collective-permute-start | bytes 497672 | tf_op jit(solution)/shard_map/ppermute | solution.py:257
  129.8 5.2 %collective-permute-done.13 = bf16[3,72,384]{2,1,0:T(8,128)(2,1)S(1)} collective-permute-done((bf16[3,72,384]{2,1,0:T(8,128)(2,1)S(1)}, bf16[3,72,384]{2,1,0:T(8,128)(2,1)S(1)}, u32[]{:S(2)}, u32[]{:S(2)}) %collective-permute-start.13) | collective-permute-done | bytes 165920 | tf_op jit(solution)/shard_map/ppermute | solution.py:257
  135.4 6.5 %collective-permute-done.14 = bf16[3,72,384]{2,1,0:T(8,128)(2,1)S(1)} collective-permute-done((bf16[3,72,384]{2,1,0:T(8,128)(2,1)S(1)}, bf16[3,72,384]{2,1,0:T(8,128)(2,1)S(1)}, u32[]{:S(2)}, u32[]{:S(2)}) %collective-permute-start.14) | collective-permute-done | bytes 165920 | tf_op jit(solution)/shard_map/ppermute | solution.py:257
  145.7 2.0 %collective-permute-done.20 = bf16[2,80,384]{2,1,0:T(8,128)(2,1)S(1)} collective-permute-done((bf16[2,80,384]{2,1,0:T(8,128)(2,1)S(1)}, bf16[2,80,384]{2,1,0:T(8,128)(2,1)S(1)}, u32[]{:S(2)}, u32[]{:S(2)}) %collective-permute-start.20) | collective-permute-done | bytes 122912 | tf_op jit(solution)/shard_map/ppermute | solution.py:928
  150.1 3.0 %collective-permute-done.21 = bf16[80,384]{1,0:T(8,128)(2,1)S(1)} collective-permute-done((bf16[80,384]{1,0:T(8,128)(2,1)S(1)}, bf16[80,384]{1,0:T(8,128)(2,1)S(1)}, u32[]{:S(2)}, u32[]{:S(2)}) %collective-permute-start.21) | collective-permute-done | bytes 61472 | tf_op jit(solution)/shard_map/ppermute | solution.py:257
  153.5 2.1 %collective-permute-done.19 = bf16[80,384]{1,0:T(8,128)(2,1)S(1)} collective-permute-done((bf16[80,384]{1,0:T(8,128)(2,1)S(1)}, bf16[80,384]{1,0:T(8,128)(2,1)S(1)}, u32[]{:S(2)}, u32[]{:S(2)}) %collective-permute-start.19) | collective-permute-done | bytes 61472 | tf_op jit(solution)/shard_map/ppermute | solution.py:257
  155.7 12.0 %all-gather.1 = bf16[576,384]{1,0:T(8,128)(2,1)} all-gather(bf16[72,384]{1,0:T(8,128)(2,1)S(1)} %slice.284), channel_id=3, replica_groups=mesh['rep'=8,'shard'=4] {'rep'}, dimensions={0}, use_global_device_ids=true | all-gather | bytes 497664 | tf_op jit(solution)/shard_map/all_gather | solution.py:1058
  167.6 2.0 %unpack_attn.1 = (f32[144,576]{1,0:T(8,128)}, f32[144,192]{1,0:T(8,128)}, f32[144,192]{1,0:T(8,128)}, f32[144,576]{1,0:T(8,128)}) custom-call(bf16[8,72,384]{2,1,0:T(8,128)(2,1)} %bitcast.142), custom_call_target="tpu_custom_call" | custom-call | tf_op jit(solution)/shard_map/unpack_attn/pallas_call | solution.py:881
  170.3 2.9 %unpack_mlp.1 = (f32[144,1536]{1,0:T(8,128)}, f32[144,1536]{1,0:T(8,128)}, f32[576,384]{1,0:T(8,128)}) custom-call(bf16[8,3,72,384]{3,2,1,0:T(8,128)(2,1)} %bitcast.143), custom_call_target="tpu_custom_call" | custom-call | tf_op jit(solution)/shard_map/unpack_mlp/pallas_call | solution.py:901
  (99 shorter events, 26.6 us)
Async XLA Ops:
  7.2 60.3 %all-gather.6.cloned.1.call-start = ((), (), s32[]{:S(2)}) async-start(), calls=%async_computation | async-start | bytes 4478976 | tf_op jit(solution)/shard_map/all_gather | solution.py:1006
  9.2 9.8 %collective-permute-start.6 = (bf16[3,72,384]{2,1,0:T(8,128)(2,1)S(1)}, bf16[3,72,384]{2,1,0:T(8,128)(2,1)S(1)}, u32[]{:S(2)}, u32[]{:S(2)}) collective-permute-start(bf16[3,72,384]{2,1,0:T(8,128)(2,1)S(1)} %pad_maximum_fusion.3), channel_id=1, source_target_pairs={{0,3},{1,0},{2,1},{3,2},{4,7},{5,4},{6,5},{7,6},{8,11},{9,8},{10,9... | collective-permute-start | bytes 497672 | tf_op jit(solution)/shard_map/ppermute | solution.py:257
  14.3 14.1 %collective-permute-start.5 = (bf16[3,72,384]{2,1,0:T(8,128)(2,1)S(1)}, bf16[3,72,384]{2,1,0:T(8,128)(2,1)S(1)}, u32[]{:S(2)}, u32[]{:S(2)}) collective-permute-start(bf16[3,72,384]{2,1,0:T(8,128)(2,1)S(1)} %pad_maximum_fusion.3), channel_id=1, source_target_pairs={{0,2},{1,3},{2,0},{3,1},{4,6},{5,7},{6,4},{7,5},{8,10},{9,11},{10,... | collective-permute-start | bytes 497672 | tf_op jit(solution)/shard_map/ppermute | solution.py:257
  14.3 14.1 %collective-permute-start = (bf16[3,72,384]{2,1,0:T(8,128)(2,1)S(1)}, bf16[3,72,384]{2,1,0:T(8,128)(2,1)S(1)}, u32[]{:S(2)}, u32[]{:S(2)}) collective-permute-start(bf16[3,72,384]{2,1,0:T(8,128)(2,1)S(1)} %pad_maximum_fusion.3), channel_id=1, source_target_pairs={{0,1},{1,2},{2,3},{3,0},{4,5},{5,6},{6,7},{7,4},{8,9},{9,10},{10,1... | collective-permute-start | bytes 497672 | tf_op jit(solution)/shard_map/ppermute | solution.py:257
  29.2 141.0 %all-gather.8.cloned.1.call-start = ((), (), s32[]{:S(2)}) async-start(), calls=%async_computation.1 | async-start | bytes 1492992 | tf_op jit(solution)/shard_map/all_gather | solution.py:1053
  31.7 8.0 %collective-permute-start.3 = (bf16[80,1536]{1,0:T(8,128)(2,1)S(1)}, bf16[80,1536]{1,0:T(8,128)(2,1)S(1)}, u32[]{:S(2)}, u32[]{:S(2)}) collective-permute-start(bf16[80,1536]{1,0:T(8,128)(2,1)S(1)} %pad_maximum_fusion.2), channel_id=1, source_target_pairs={{0,3},{1,0},{2,1},{3,2},{4,7},{5,4},{6,5},{7,6},{8,11},{9,8},{10,9... | collective-permute-start | bytes 737288 | tf_op jit(solution)/shard_map/ppermute | solution.py:257
  33.0 22.9 %collective-permute-start.2 = (bf16[80,1536]{1,0:T(8,128)(2,1)S(1)}, bf16[80,1536]{1,0:T(8,128)(2,1)S(1)}, u32[]{:S(2)}, u32[]{:S(2)}) collective-permute-start(bf16[80,1536]{1,0:T(8,128)(2,1)S(1)} %pad_maximum_fusion.2), channel_id=1, source_target_pairs={{0,2},{1,3},{2,0},{3,1},{4,6},{5,7},{6,4},{7,5},{8,10},{9,11},{10,... | collective-permute-start | bytes 737288 | tf_op jit(solution)/shard_map/ppermute | solution.py:257
  34.9 21.1 %collective-permute-start.1 = (bf16[80,1536]{1,0:T(8,128)(2,1)S(1)}, bf16[80,1536]{1,0:T(8,128)(2,1)S(1)}, u32[]{:S(2)}, u32[]{:S(2)}) collective-permute-start(bf16[80,1536]{1,0:T(8,128)(2,1)S(1)} %pad_maximum_fusion.2), channel_id=1, source_target_pairs={{0,1},{1,2},{2,3},{3,0},{4,5},{5,6},{6,7},{7,4},{8,9},{9,10},{10,1... | collective-permute-start | bytes 737288 | tf_op jit(solution)/shard_map/ppermute | solution.py:257
  86.5 5.2 %collective-permute-start.7 = (bf16[4,4,3,72,384]{4,3,2,1,0:T(8,128)(2,1)}, bf16[4,4,3,72,384]{4,3,2,1,0:T(8,128)(2,1)S(1)}, u32[]{:S(2)}, u32[]{:S(2)}) collective-permute-start(bf16[4,4,3,72,384]{4,3,2,1,0:T(8,128)(2,1)} %get-tuple-element.74), channel_id=1, source_target_pairs={{0,4},{4,0},{8,12},{12,8},{16,20},{20,16},{24,28},{28,24},{1,5},{5... | collective-permute-start | bytes 7962632 | tf_op jit(solution)/shard_map/ppermute | solution.py:928
  94.2 17.0 %collective-permute-start.9 = (bf16[2,2,3,72,384]{4,3,2,1,0:T(8,128)(2,1)S(1)}, bf16[2,2,3,72,384]{4,3,2,1,0:T(8,128)(2,1)S(1)}, u32[]{:S(2)}, u32[]{:S(2)}) collective-permute-start(bf16[2,2,3,72,384]{4,3,2,1,0:T(8,128)(2,1)S(1)} %get-tuple-element.99), channel_id=1, source_target_pairs={{0,16},{4,20},{8,24},{12,28},{16,0},{20,4},{24,8},{28,12},{1,17},{... | collective-permute-start | bytes 1990664 | tf_op jit(solution)/shard_map/ppermute | solution.py:928
  95.8 16.7 %collective-permute-start.8 = (bf16[2,2,3,72,384]{4,3,2,1,0:T(8,128)(2,1)S(1)}, bf16[2,2,3,72,384]{4,3,2,1,0:T(8,128)(2,1)S(1)}, u32[]{:S(2)}, u32[]{:S(2)}) collective-permute-start(bf16[2,2,3,72,384]{4,3,2,1,0:T(8,128)(2,1)S(1)} %get-tuple-element.101), channel_id=1, source_target_pairs={{0,8},{4,12},{8,0},{12,4},{16,24},{20,28},{24,16},{28,20},{1,9},{5... | collective-permute-start | bytes 1990664 | tf_op jit(solution)/shard_map/ppermute | solution.py:928
  112.5 11.7 %collective-permute-start.12 = (bf16[4,4,80,384]{3,2,1,0:T(8,128)(2,1)}, bf16[4,4,80,384]{3,2,1,0:T(8,128)(2,1)S(1)}, u32[]{:S(2)}, u32[]{:S(2)}) collective-permute-start(bf16[4,4,80,384]{3,2,1,0:T(8,128)(2,1)} %get-tuple-element.80), channel_id=1, source_target_pairs={{0,4},{4,0},{8,12},{12,8},{16,20},{20,16},{24,28},{28,24},{1,5},{5... | collective-permute-start | bytes 2949128 | tf_op jit(solution)/shard_map/ppermute | solution.py:928
  112.6 10.3 %collective-permute-start.11 = (bf16[2,3,72,384]{3,2,1,0:T(8,128)(2,1)S(1)}, bf16[2,3,72,384]{3,2,1,0:T(8,128)(2,1)S(1)}, u32[]{:S(2)}, u32[]{:S(2)}) collective-permute-start(bf16[2,3,72,384]{3,2,1,0:T(8,128)(2,1)S(1)} %fusion.6), channel_id=1, source_target_pairs={{0,8},{4,12},{8,0},{12,4},{16,24},{20,28},{24,16},{28,20},{1,9},{5... | collective-permute-start | bytes 995336 | tf_op jit(solution)/shard_map/ppermute | solution.py:928
  114.2 10.0 %collective-permute-start.10 = (bf16[2,3,72,384]{3,2,1,0:T(8,128)(2,1)S(1)}, bf16[2,3,72,384]{3,2,1,0:T(8,128)(2,1)S(1)}, u32[]{:S(2)}, u32[]{:S(2)}) collective-permute-start(bf16[2,3,72,384]{3,2,1,0:T(8,128)(2,1)S(1)} %fusion.5), channel_id=1, source_target_pairs={{0,16},{4,20},{8,24},{12,28},{16,0},{20,4},{24,8},{28,12},{1,17},{... | collective-permute-start | bytes 995336 | tf_op jit(solution)/shard_map/ppermute | solution.py:928
  124.8 17.1 %collective-permute-start.17 = (bf16[2,2,80,384]{3,2,1,0:T(8,128)(2,1)S(1)}, bf16[2,2,80,384]{3,2,1,0:T(8,128)(2,1)S(1)}, u32[]{:S(2)}, u32[]{:S(2)}) collective-permute-start(bf16[2,2,80,384]{3,2,1,0:T(8,128)(2,1)S(1)} %get-tuple-element.103), channel_id=1, source_target_pairs={{0,16},{4,20},{8,24},{12,28},{16,0},{20,4},{24,8},{28,12},{1,17},{... | collective-permute-start | bytes 737288 | tf_op jit(solution)/shard_map/ppermute | solution.py:928
  125.3 16.6 %collective-permute-start.16 = (bf16[2,2,80,384]{3,2,1,0:T(8,128)(2,1)S(1)}, bf16[2,2,80,384]{3,2,1,0:T(8,128)(2,1)S(1)}, u32[]{:S(2)}, u32[]{:S(2)}) collective-permute-start(bf16[2,2,80,384]{3,2,1,0:T(8,128)(2,1)S(1)} %get-tuple-element.105), channel_id=1, source_target_pairs={{0,8},{4,12},{8,0},{12,4},{16,24},{20,28},{24,16},{28,20},{1,9},{5... | collective-permute-start | bytes 737288 | tf_op jit(solution)/shard_map/ppermute | solution.py:928
  125.9 9.0 %collective-permute-start.13 = (bf16[3,72,384]{2,1,0:T(8,128)(2,1)S(1)}, bf16[3,72,384]{2,1,0:T(8,128)(2,1)S(1)}, u32[]{:S(2)}, u32[]{:S(2)}) collective-permute-start(bf16[3,72,384]{2,1,0:T(8,128)(2,1)S(1)} %fusion.16), channel_id=1, source_target_pairs={{0,1},{1,2},{2,3},{3,0},{4,5},{5,6},{6,7},{7,4},{8,9},{9,10},{10,1... | collective-permute-start | bytes 497672 | tf_op jit(solution)/shard_map/ppermute | solution.py:257
  126.0 9.4 %collective-permute-start.15 = (bf16[3,72,384]{2,1,0:T(8,128)(2,1)S(1)}, bf16[3,72,384]{2,1,0:T(8,128)(2,1)S(1)}, u32[]{:S(2)}, u32[]{:S(2)}) collective-permute-start(bf16[3,72,384]{2,1,0:T(8,128)(2,1)S(1)} %get-tuple-element.107), channel_id=1, source_target_pairs={{0,3},{1,0},{2,1},{3,2},{4,7},{5,4},{6,5},{7,6},{8,11},{9,8},{10,9... | collective-permute-start | bytes 497672 | tf_op jit(solution)/shard_map/ppermute | solution.py:257
  129.8 12.2 %collective-permute-start.14 = (bf16[3,72,384]{2,1,0:T(8,128)(2,1)S(1)}, bf16[3,72,384]{2,1,0:T(8,128)(2,1)S(1)}, u32[]{:S(2)}, u32[]{:S(2)}) collective-permute-start(bf16[3,72,384]{2,1,0:T(8,128)(2,1)S(1)} %get-tuple-element.108), channel_id=1, source_target_pairs={{0,2},{1,3},{2,0},{3,1},{4,6},{5,7},{6,4},{7,5},{8,10},{9,11},{10,... | collective-permute-start | bytes 497672 | tf_op jit(solution)/shard_map/ppermute | solution.py:257
  142.8 4.9 %collective-permute-start.20 = (bf16[2,80,384]{2,1,0:T(8,128)(2,1)S(1)}, bf16[2,80,384]{2,1,0:T(8,128)(2,1)S(1)}, u32[]{:S(2)}, u32[]{:S(2)}) collective-permute-start(bf16[2,80,384]{2,1,0:T(8,128)(2,1)S(1)} %fusion.18), channel_id=1, source_target_pairs={{0,8},{4,12},{8,0},{12,4},{16,24},{20,28},{24,16},{28,20},{1,9},{5... | collective-permute-start | bytes 368648 | tf_op jit(solution)/shard_map/ppermute | solution.py:928
  144.3 5.1 %collective-permute-start.18 = (bf16[2,80,384]{2,1,0:T(8,128)(2,1)S(1)}, bf16[2,80,384]{2,1,0:T(8,128)(2,1)S(1)}, u32[]{:S(2)}, u32[]{:S(2)}) collective-permute-start(bf16[2,80,384]{2,1,0:T(8,128)(2,1)S(1)} %fusion.17), channel_id=1, source_target_pairs={{0,16},{4,20},{8,24},{12,28},{16,0},{20,4},{24,8},{28,12},{1,17},{... | collective-permute-start | bytes 368648 | tf_op jit(solution)/shard_map/ppermute | solution.py:928
  147.8 5.3 %collective-permute-start.21 = (bf16[80,384]{1,0:T(8,128)(2,1)S(1)}, bf16[80,384]{1,0:T(8,128)(2,1)S(1)}, u32[]{:S(2)}, u32[]{:S(2)}) collective-permute-start(bf16[80,384]{1,0:T(8,128)(2,1)S(1)} %get-tuple-element.109), channel_id=1, source_target_pairs={{0,2},{1,3},{2,0},{3,1},{4,6},{5,7},{6,4},{7,5},{8,10},{9,11},{10,... | collective-permute-start | bytes 184328 | tf_op jit(solution)/shard_map/ppermute | solution.py:257
  147.9 5.6 %collective-permute-start.22 = (bf16[80,384]{1,0:T(8,128)(2,1)S(1)}, bf16[80,384]{1,0:T(8,128)(2,1)S(1)}, u32[]{:S(2)}, u32[]{:S(2)}) collective-permute-start(bf16[80,384]{1,0:T(8,128)(2,1)S(1)} %get-tuple-element.110), channel_id=1, source_target_pairs={{0,3},{1,0},{2,1},{3,2},{4,7},{5,4},{6,5},{7,6},{8,11},{9,8},{10,9... | collective-permute-start | bytes 184328 | tf_op jit(solution)/shard_map/ppermute | solution.py:257
  149.5 6.1 %collective-permute-start.19 = (bf16[80,384]{1,0:T(8,128)(2,1)S(1)}, bf16[80,384]{1,0:T(8,128)(2,1)S(1)}, u32[]{:S(2)}, u32[]{:S(2)}) collective-permute-start(bf16[80,384]{1,0:T(8,128)(2,1)S(1)} %fusion.22), channel_id=1, source_target_pairs={{0,1},{1,2},{2,3},{3,0},{4,5},{5,6},{6,7},{7,4},{8,9},{9,10},{10,1... | collective-permute-start | bytes 184328 | tf_op jit(solution)/shard_map/ppermute | solution.py:257
  (14 other events, 232.8 us)
Sparse Core Ops, SparseCore 0:
  29.4 36.2 all-gather.5
  142.8 24.9 all-gather.7

commit v3 on v2

--- a/solution.py
+++ b/solution.py
@@ -482,12 +482,18 @@
     )
 
 
+def in_core_order(core, mine, pair):
+    mine, pair = widen(mine), widen(pair)
+    upper = jnp.where(core == 0, mine, pair)
+    lower = jnp.where(core == 0, pair, mine)
+    return narrow(jnp.concatenate([upper, lower], axis=0))
+
+
 def attention_forward_kernel(
     shards, at_ref, x_ref, row_ref, cos_ref, sin_ref, own_ref, gain_own_ref, mine_ref,
     pair_ref, w_ref, gain_ref, x2_ref, q_ref, k_ref, v_ref, o_ref, lse_ref, bias_ref,
 ):
     z = at_ref[0]
-    first_core = at_ref[2] == 0
     rows = own_ref.shape[0]
     half = rows // 2
     width = x_ref.shape[0]
@@ -496,12 +502,22 @@
     gains = widen(gain_own_ref[...])
     for k in range(1, shards):
         at = pl.multiple_of(lax.rem(z + shards - k, shards) * rows, 16)
-        gains = gains + widen(mine_ref[k - 1, half:])
-        mine, pair = widen(mine_ref[k - 1, :half]), widen(pair_ref[k - 1, :half])
-        upper = jnp.where(first_core, mine, pair)
-        lower = jnp.where(first_core, pair, mine)
-        w_ref[pl.ds(at, rows), :] = narrow(jnp.concatenate([upper, lower], axis=0))
-    turned = jnp.transpose(jnp.concatenate([gains[:, : 5 * LANES]] * (LANES // 8), axis=0))
+        gains = gains + widen(mine_ref[0, k - 1, half:])
+        for c in range(mine_ref.shape[0]):
+            to = lax.bitwise_xor(at_ref[1], c)
+            w_ref[pl.ds(at, rows), c * CHUNK : (c + 1) * CHUNK] = in_core_order(
+                at_ref[2], mine_ref[to, k - 1, :half], pair_ref[to, k - 1, :half]
+            )
+    spare = 5 * LANES - CHUNK
+    gains = jnp.concatenate(
+        [
+            jnp.concatenate([gains[0:1], gains[1:2, :spare]], axis=1),
+            jnp.concatenate([gains[2:3], gains[3:4, :spare]], axis=1),
+            jnp.zeros((6, 5 * LANES), jnp.float32),
+        ],
+        axis=0,
+    )
+    turned = jnp.transpose(jnp.concatenate([gains] * (LANES // 8), axis=0))
     gain_ref[...] = turned[:width]
     x = widen(x_ref[...])
     inverse = lax.rsqrt(jnp.mean(x * x, axis=0, keepdims=True) + EPSILON)
@@ -584,7 +600,8 @@
 
 
 def mlp_kernel(
-    shards, at_ref, x2_ref, ctt_ref, gain_ref, gate_ref, up_ref, tall_ref, wide_ref, tall_other_ref,
+    shards, at_ref, x2_ref, ctt_ref, gain_ref, gate_ref, up_ref, tall_ref, mine_ref,
+    pair_ref, tall_mine_ref, tall_pair_ref,
     out_ref, dx2_ref, gain_grad_ref, keep_ref, send_ref,
     h2_ref, h2t_ref, ct_ref, acc_ref, dh2_ref, wg_ref, wu_ref, wd_ref,
     gg_ref, gu_ref, gd_ref,
@@ -611,8 +628,9 @@
     for k in range(1, shards):
         at = pl.multiple_of(lax.rem(z + shards - k, shards) * rows, 16)
         for m, ref in ((0, wg_ref), (1, wu_ref)):
-            pieces = [widen(wide_ref[h, k - 1, m]) for h in range(2)]
-            ref[pl.ds(at, rows), :] = narrow(jnp.concatenate(pieces, axis=0))
+            ref[pl.ds(at, rows), :] = in_core_order(
+                core, mine_ref[0, k - 1, m], pair_ref[0, k - 1, m]
+            )
 
     @pl.when(j == z)
     def _():
@@ -620,8 +638,11 @@
 
     @pl.when(j != z)
     def _():
-        pieces = [widen(tall_other_ref[r, 0, 0]) for r in range(tall_other_ref.shape[0])]
-        wd_ref[...] = narrow(jnp.concatenate(pieces, axis=0))
+        for c in range(tall_mine_ref.shape[0]):
+            to = lax.bitwise_xor(chip, c)
+            wd_ref[c * rows : (c + 1) * rows, :] = in_core_order(
+                core, tall_mine_ref[to, 0, 0], tall_pair_ref[to, 0, 0]
+            )
 
     h2, ct = h2_ref[...], ct_ref[...]
     wg, wu, wd = wg_ref[...], wu_ref[...], wd_ref[...]
@@ -664,15 +685,18 @@
         dx2_ref[...] = widen(ctt_ref[...]) + inverse * (n2 - u2 * mean)
 
 
-def mlp(at, x2, ct, gains, gate, up, tall, gathered, shards):
+def mlp(at, x2, ct, gains, gate, up, tall, mine, pair, shards):
     width = x2.shape[0]
-    copies = gathered.shape[0]
+    copies = 2 * mine.shape[0]
     rows, ff = gate.shape
     half = rows // 2
     bf16, f32 = jnp.bfloat16, jnp.float32
 
     def kernel(*refs):
         mlp_kernel(shards, *refs)
+
+    def wide_block(j, at_ref):
+        return (lax.bitwise_xor(j, at_ref[1]), 0, 0, 0, 0)
 
     def tall_block(j, at_ref):
         return (0, jnp.maximum(lax.rem(at_ref[0] + shards - j, shards) - 1, 0), 2, 0, 0)
@@ -690,8 +714,10 @@
                 pl.BlockSpec((rows, CHUNK), lambda j, at_ref: (0, j)),
                 pl.BlockSpec((rows, CHUNK), lambda j, at_ref: (0, j)),
                 whole((width, CHUNK)),
-                pl.BlockSpec((2, shards - 1, 2, half, CHUNK), lambda j, at_ref: (j, 0, 0, 0, 0)),
-                pl.BlockSpec((copies, 1, 1, half, CHUNK), tall_block),
+                pl.BlockSpec((1, shards - 1, 2, half, CHUNK), wide_block),
+                pl.BlockSpec((1, shards - 1, 2, half, CHUNK), wide_block),
+                pl.BlockSpec((copies // 2, 1, 1, half, CHUNK), tall_block),
+                pl.BlockSpec((copies // 2, 1, 1, half, CHUNK), tall_block),
             ],
             out_specs=[
                 whole((width, TOKENS)),
@@ -728,7 +754,7 @@
             flops=int(6.2e9), bytes_accessed=14000000, transcendentals=1200000
         ),
         name="mlp",
-    )(at, x2, ct, gains, gate, up, tall, gathered, gathered)
+    )(at, x2, ct, gains, gate, up, tall, mine, pair, mine, pair)
 
 
 def attention_backward_kernel(
@@ -885,24 +911,36 @@
     )(pieces)
 
 
-def unpack_mlp_kernel(piece_ref, gate_ref, up_ref, tall_ref):
-    half = piece_ref.shape[2]
-    for c in range(piece_ref.shape[0] // 2):
-        for h in range(2):
-            for m, ref in ((0, gate_ref), (1, up_ref)):
-                ref[h * half : (h + 1) * half, c * CHUNK : (c + 1) * CHUNK] = widen(
-                    piece_ref[2 * c + h, m]
-                )
-    for r in range(piece_ref.shape[0]):
-        tall_ref[r * half : (r + 1) * half, :] = widen(piece_ref[r, 2])
-
-
-def unpack_mlp(pieces, shapes):
+def unpack_mlp_kernel(at_ref, mine_ref, pair_ref, gate_ref, up_ref, tall_ref):
+    chip, core = at_ref[1], at_ref[2]
+    half = mine_ref.shape[2]
+    for c in range(mine_ref.shape[0]):
+        to = lax.bitwise_xor(chip, c)
+        for m in range(3):
+            mine, pair = widen(mine_ref[to, m]), widen(pair_ref[to, m])
+            upper = jnp.where(core == 0, mine, pair)
+            lower = jnp.where(core == 0, pair, mine)
+            if m < 2:
+                ref = (gate_ref, up_ref)[m]
+                ref[:half, c * CHUNK : (c + 1) * CHUNK] = upper
+                ref[half:, c * CHUNK : (c + 1) * CHUNK] = lower
+            else:
+                tall_ref[2 * c * half : (2 * c + 1) * half, :] = upper
+                tall_ref[(2 * c + 1) * half : (2 * c + 2) * half, :] = lower
+
+
+def unpack_mlp(at, mine, pair, shapes):
     return pl.pallas_call(
         unpack_mlp_kernel,
+        grid_spec=pltpu.PrefetchScalarGridSpec(
+            num_scalar_prefetch=1,
+            grid=(),
+            in_specs=[pl.BlockSpec(memory_space=pltpu.VMEM)] * 2,
+            out_specs=[pl.BlockSpec(memory_space=pltpu.VMEM)] * 3,
+        ),
         out_shape=[jax.ShapeDtypeStruct(shape, jnp.float32) for shape in shapes],
         name="unpack_mlp",
-    )(pieces)
+    )(at, mine, pair)
 
 
 def fits_kernels(block_input, query_weight, key_weight, gate_weight, down_weight):
@@ -917,15 +955,22 @@
     )
 
 
-def gain_rows(gain_attn, gain_mlp, columns):
-    both = jnp.zeros((8, columns), jnp.bfloat16)
+def gain_rows(gain_attn, gain_mlp):
+    both = jnp.zeros((2, 2 * CHUNK), jnp.bfloat16)
     at = lax.axis_index("shard") * gain_attn.shape[0]
-    return lax.dynamic_update_slice(both, jnp.stack([gain_attn, gain_mlp]), (0, at))
+    both = lax.dynamic_update_slice(both, jnp.stack([gain_attn, gain_mlp]), (0, at))
+    return jnp.pad(both.reshape(4, CHUNK), ((0, 4), (0, 0)))
 
 
 def swapped(values, bit):
     size = lax.axis_size("rep")
     return lax.ppermute(values, "rep", [(i, i ^ bit) for i in range(size)])
+
+
+def plane_gather(own):
+    from_x, from_y = swapped(own, 2), swapped(own, 4)
+    mine = jnp.stack([own, from_x, from_y, swapped(from_y, 2)])
+    return mine, swapped(mine, 1)
 
 
 def plus(left, right):
@@ -1000,10 +1045,15 @@
     shards, copies = lax.axis_size("shard"), lax.axis_size("rep")
     rank = lax.axis_index("rep")
     at = jnp.stack([lax.axis_index("shard"), rank // 2, rank % 2]).astype(jnp.int32)
+    barrier = lax.optimization_barrier
+    own = jnp.concatenate([key_weight, value_weight, output_weight, query_weight], axis=1)
+    rows = own.shape[0]
+    gains_own = gain_rows(gain_attn, gain_mlp)
+    attn_piece = jnp.concatenate([piece_of(own), gains_own])
+    attn_came = [shifted(attn_piece, k) for k in range(1, shards)]
     tall = jnp.transpose(down_weight)
     wide = jnp.stack([piece_of(gate_weight), piece_of(up_weight), row_piece_of(tall)])
     wide_came = [shifted(wide, k) for k in range(1, shards)]
-    wide_pieces = lax.all_gather(jnp.stack(wide_came), "rep")
     half_dim = HEAD_WIDTH // 2
     frequency = ROPE_BASE ** (-(jnp.arange(half_dim, dtype=jnp.float32) * 2.0 / HEAD_WIDTH))
     angles = frequency[:, None] * positions.astype(jnp.float32)
@@ -1011,22 +1061,26 @@
     row = segment_ids
     x = jnp.transpose(block_input[0])
     ct = jnp.transpose(layer_output_cotangent[0])
-    own = jnp.concatenate([key_weight, value_weight, output_weight, query_weight], axis=1)
-    gains_own = gain_rows(gain_attn, gain_mlp, own.shape[1])
-    rows = own.shape[0]
-    own_half = lax.dynamic_slice_in_dim(own, (rank % 2) * (rows // 2), rows // 2, 0)
-    own_half = jnp.concatenate([own_half, gains_own])
-    own_half, own, gains_own, cosine, sine, at, _ = lax.optimization_barrier(
-        (own_half, own, gains_own, cosine, sine, at, wide_came[0])
-    )
-    mine = fetch_others(own_half)
+    attn_own = jnp.stack(attn_came)
+    attn_x, attn_y = swapped(attn_own, 2), swapped(attn_own, 4)
+    mine = jnp.stack([attn_own, attn_x, attn_y, swapped(attn_y, 2)])
+    mine, wide_came, cosine, sine, at = barrier((mine, wide_came, cosine, sine, at))
     pair = swapped(mine, 1)
+    wide_own = jnp.concatenate(wide_came)
+    wide_x, wide_y = swapped(wide_own, 2), swapped(wide_own, 4)
 
     w, gains, x2, q, k, v, o, lse = attention_forward(
         at, x, row, cosine, sine, own, gains_own, mine, pair, shards
     )
+    wide_x, wide_y, x2 = barrier((wide_x, wide_y, x2))
+    mid = wide_own.shape[0] // 2
+    across = jnp.concatenate([swapped(wide_y[:mid], 2), swapped(wide_x[mid:], 4)])
+    wide_mine = jnp.stack([wide_own, wide_x, wide_y, across])
+    wide_pair = swapped(wide_mine, 1)
+    blocks = (-1, shards - 1, 3) + wide.shape[1:]
+    wide_mine, wide_pair = wide_mine.reshape(blocks), wide_pair.reshape(blocks)
     out, dx2, gain_mlp_grad, wide_keep, wide_send = mlp(
-        at, x2, ct, gains, gate_weight, up_weight, tall, wide_pieces, shards
+        at, x2, ct, gains, gate_weight, up_weight, tall, wide_mine, wide_pair, shards
     )
     wide_came = swapped(wide_send, 1)
     dx, attn_keep, attn_send = attention_backward(
@@ -1035,7 +1089,6 @@
         shards,
         copies,
     )
-    barrier = lax.optimization_barrier
     wide_one = exchange_one(wide_keep, wide_came)
     wide_one, attn_send = barrier((wide_one, attn_send))
     attn_came = swapped(attn_send, 1)
@@ -1049,14 +1102,19 @@
     attn_two = exchange_two(*attn_one)
     attn_blocks = own_blocks(*attn_one, *attn_two)
     attn_total = added(attn_blocks[0], exchange_shards(attn_blocks))
+    half = rows // 2
+    total_mine, total_pair = plane_gather(wide_total)
+    attn_pieces = lax.all_gather(narrow(attn_total[:half]), "rep")
+    total_pair, attn_pieces = barrier((total_pair, attn_pieces))
+    q_grad, k_grad, v_grad, o_grad = unpack_attn(
+        attn_pieces,
+        (query_weight.shape, key_weight.shape, value_weight.shape, output_weight.shape),
+    )
     gate_grad, up_grad, tall_grad = unpack_mlp(
-        lax.all_gather(wide_total, "rep"),
+        at,
+        total_mine,
+        total_pair,
         (gate_weight.shape, up_weight.shape, tall.shape),
-    )
-    half = rows // 2
-    q_grad, k_grad, v_grad, o_grad = unpack_attn(
-        lax.all_gather(narrow(attn_total[:half]), "rep"),
-        (query_weight.shape, key_weight.shape, value_weight.shape, output_weight.shape),
     )
     both = attn_total[half : half + 4].reshape(2, 2 * CHUNK)
     both = lax.dynamic_slice(both, (0, lax.axis_index("shard") * rows), (2, rows))

time: 180 us -> 175 us (0.972)
  starting transfers between devices: 26.7 us -> 44.6 us
  waiting for transfers between devices: 71.5 us -> 56.6 us
  between operations: 14.5 us -> 1.06 us
  local copies, waits for them, and re-layouts: 4.47 us -> 8.92 us
    ppermute x12, waiting for transfers between devices: 49.8 us -> 14.5 us  [shifted(): lax.ppermute(values, 'shard', [(i, (i + steps) % size) for i in range(siz...]
    ppermute x11 -> x23, waiting for transfers between devices: 21.6 us -> 42.1 us  [swapped(): return lax.ppermute(values, 'rep', [(i, i ^ bit) for i in range(size)])]
    ppermute x11 -> x23, starting transfers between devices: 9.31 us -> 21.2 us  [swapped(): return lax.ppermute(values, 'rep', [(i, i ^ bit) for i in range(size)])]
    ppermute x12, starting transfers between devices: 17.3 us -> 23.3 us  [shifted(): lax.ppermute(values, 'shard', [(i, (i + steps) % size) for i in range(siz...]
    unnamed x26 -> x23, local copies, waits for them, and re-layouts: 1.27 us -> 3.53 us
  transfers between devices with their start and end apart: 25 -> 35, of which waited for: 17 -> 18; matrix products, arithmetic and copies ran while one was open for 2% -> 4% of each run, Pallas kernels for 13% -> 12%
where the time goes in v3:
time: 175 us
  waiting for transfers between devices  56.6 us (32%)
  Pallas kernels  46 us (26%)
  starting transfers between devices  44.6 us (25%)
  blocking collectives  10.6 us (6%)
  local copies, waits for them, and re-layouts  8.92 us (5%)
  other arithmetic  6.9 us (4%)
    ppermute x23, waiting for transfers between devices, swapped(): return lax.ppermute(values, 'rep', [(i, i ^ bit) for i in range(size)])  42.1 us
    ppermute x12, starting transfers between devices, shifted(): lax.ppermute(values, 'shard', [(i, (i + steps) % size) for i in range(siz...  23.3 us
    ppermute x23, starting transfers between devices, swapped(): return lax.ppermute(values, 'rep', [(i, i ^ bit) for i in range(size)])  21.2 us
    pallas_call x1, Pallas kernels, mlp(): pl.pallas_call(kernel, grid_spec=pltpu.PrefetchScalarGridSpec(num_scalar_...  19.5 us
    ppermute x12, waiting for transfers between devices, shifted(): lax.ppermute(values, 'shard', [(i, (i + steps) % size) for i in range(siz...  14.5 us
    pallas_call x1, Pallas kernels, attention_backward(): pl.pallas_call(kernel, grid_spec=pltpu.PrefetchScalarGridSpec(num_scalar_...  12.5 us
    all_gather x1, blocking collectives, on_device(): attn_pieces = lax.all_gather(narrow(attn_total[:half]), 'rep')  10.6 us
    pallas_call x1, Pallas kernels, attention_forward(): pl.pallas_call(kernel, grid_spec=pltpu.PrefetchScalarGridSpec(num_scalar_...  8.39 us
  transfers between devices with their start and end apart: 35, of which 18 were waited for; matrix products, arithmetic and copies ran while one was open for 4% of the time, Pallas kernels for 12%

profile of v3, /device:TPU:0, one launch (start us, length us, event | category | flops | bytes accessed | tf_op | source)
XLA Modules:
  0.0 174.7 jit_solution(1062102887345305925)
XLA Ops:
  3.6 3.2 %collective-permute-start = (bf16[80,384]{1,0:T(8,128)(2,1)S(1)}, bf16[80,384]{1,0:T(8,128)(2,1)S(1)}, u32[]{:S(2)}, u32[]{:S(2)}) collective-permute-start(bf16[80,384]{1,0:T(8,128)(2,1)S(1)} %pad_maximum_fusion.6), channel_id=1, source_target_pairs={{0,1},{1,2},{2,3},{3,0},{4,5},{5,6},{6,7},{7,4},{8,9},{9,10},{10,1... | collective-permute-start | bytes 184328 | tf_op jit(solution)/shard_map/ppermute | solution.py:257
  6.8 2.6 %collective-permute-start.1 = (bf16[80,384]{1,0:T(8,128)(2,1)S(1)}, bf16[80,384]{1,0:T(8,128)(2,1)S(1)}, u32[]{:S(2)}, u32[]{:S(2)}) collective-permute-start(bf16[80,384]{1,0:T(8,128)(2,1)S(1)} %pad_maximum_fusion.6), channel_id=1, source_target_pairs={{0,2},{1,3},{2,0},{3,1},{4,6},{5,7},{6,4},{7,5},{8,10},{9,11},{10,... | collective-permute-start | bytes 184328 | tf_op jit(solution)/shard_map/ppermute | solution.py:257
  13.5 2.8 %collective-permute-start.8 = (bf16[3,72,384]{2,1,0:T(8,128)(2,1)S(1)}, bf16[3,72,384]{2,1,0:T(8,128)(2,1)S(1)}, u32[]{:S(2)}, u32[]{:S(2)}) collective-permute-start(bf16[3,72,384]{2,1,0:T(8,128)(2,1)S(1)} %pad_maximum_fusion.5), channel_id=1, source_target_pairs={{0,3},{1,0},{2,1},{3,2},{4,7},{5,4},{6,5},{7,6},{8,11},{9,8},{10,9... | collective-permute-start | bytes 497672 | tf_op jit(solution)/shard_map/ppermute | solution.py:257
  19.6 2.4 %collective-permute-done.4 = bf16[3,80,384]{2,1,0:T(8,128)(2,1)S(1)} collective-permute-done((bf16[3,80,384]{2,1,0:T(8,128)(2,1)S(1)}, bf16[3,80,384]{2,1,0:T(8,128)(2,1)S(1)}, u32[]{:S(2)}, u32[]{:S(2)}) %collective-permute-start.4) | collective-permute-done | bytes 184352 | tf_op jit(solution)/shard_map/ppermute | solution.py:967
  25.1 2.4 %collective-permute-done.5 = bf16[3,80,384]{2,1,0:T(8,128)(2,1)S(1)} collective-permute-done((bf16[3,80,384]{2,1,0:T(8,128)(2,1)S(1)}, bf16[3,80,384]{2,1,0:T(8,128)(2,1)S(1)}, u32[]{:S(2)}, u32[]{:S(2)}) %collective-permute-start.5) | collective-permute-done | bytes 184352 | tf_op jit(solution)/shard_map/ppermute | solution.py:967
  31.9 8.4 %attention_forward.1 = (bf16[576,1536]{1,0:T(8,128)(2,1)}, f32[576,128]{1,0:T(8,128)}, f32[576,384]{1,0:T(8,128)}, bf16[3,64,1152]{2,1,0:T(8,128)(2,1)}, bf16[3,...) custom-call(s32[3]{0:T(128)} %pad_add_fusion.refs_0_.at_ref, ...), custom_call_target="tpu_custom_call" | custom-call | flops 1500000000 | bytes 8000000 | tf_op jit(solution)/shard_map/attention_forward/pallas_call | solution.py:575
  45.2 4.6 %collective-permute-done.12 = bf16[4,72,384]{2,1,0:T(8,128)(2,1)S(1)} collective-permute-done((bf16[4,72,384]{2,1,0:T(8,128)(2,1)S(1)}, bf16[4,72,384]{2,1,0:T(8,128)(2,1)S(1)}, u32[]{:S(2)}, u32[]{:S(2)}) %collective-permute-start.12) | collective-permute-done | bytes 221216 | tf_op jit(solution)/shard_map/ppermute | solution.py:967
  49.8 2.5 %collective-permute-done.13 = bf16[5,72,384]{2,1,0:T(8,128)(2,1)S(1)} collective-permute-done((bf16[5,72,384]{2,1,0:T(8,128)(2,1)S(1)}, bf16[5,72,384]{2,1,0:T(8,128)(2,1)S(1)}, u32[]{:S(2)}, u32[]{:S(2)}) %collective-permute-start.13) | collective-permute-done | bytes 276512 | tf_op jit(solution)/shard_map/ppermute | solution.py:967
  54.3 2.4 %collective-permute-done.14 = bf16[4,9,72,384]{3,2,1,0:T(8,128)(2,1)S(1)} collective-permute-done((bf16[4,9,72,384]{3,2,1,0:T(8,128)(2,1)S(1)}, bf16[4,9,72,384]{3,2,1,0:T(8,128)(2,1)S(1)}, u32[]{:S(2)}, u32[]{:S(2)}) %collective-permute-start.14) | collective-permute-done | bytes 1990688 | tf_op jit(solution)/shard_map/ppermute | solution.py:967
  58.1 19.5 %mlp.1 = (bf16[576,384]{1,0:T(8,128)(2,1)}, f32[576,384]{1,0:T(8,128)}, f32[576,128]{1,0:T(8,128)}, bf16[4,4,3,72,384]{4,3,2,1,0:T(8,128)(2,1)}, bf16[4,4,3,72,384]{4,3,2,1,0:T(8,128)(2,1)}) custom-call(s32[3]{0:T(128)} %pad_add_fusion.refs_0_.at_ref, f32[576,384]{1,0:T(8,128)} %get-tuple-element.69.refs_1_, bf16[576,384]{1,0:T(8,128)(2,1)} %bitcast.184, ...), custom_call_target="tpu_custom_call" | custom-call | flops 6200000000 | bytes 14000000 | tf_op jit(solution)/shard_map/mlp/pallas_call | solution.py:705
  77.7 5.0 %collective-permute-done.15 = bf16[4,4,3,72,384]{4,3,2,1,0:T(8,128)(2,1)S(1)} collective-permute-done((bf16[4,4,3,72,384]{4,3,2,1,0:T(8,128)(2,1)}, bf16[4,4,3,72,384]{4,3,2,1,0:T(8,128)(2,1)S(1)}, u32[]{:S(2)}, u32[]{:S(2)}) %collective-permute-start.15) | collective-permute-done | bytes 2654240 | tf_op jit(solution)/shard_map/ppermute | solution.py:967
  86.5 12.5 %attention_backward.1 = (f32[576,384]{1,0:T(8,128)}, bf16[4,4,80,384]{3,2,1,0:T(8,128)(2,1)}, bf16[4,4,80,384]{3,2,1,0:T(8,128)(2,1)}) custom-call(s32[3]{0:T(128)} %pad_add_fusion.refs_0_.at_ref, bf16[576,384]{1,0:T(8,128)(2,1)} %bitcast.186, f32[576,384]{1,0:T(8,128)} %get-tuple-element.74.refs_2_, s32[1,384]{1,0:T(1,128)} %refs_3_.1, ...), custom_call_target="tpu_custom_call" | custom-call | flops 3000000000 | bytes 9000000 | tf_op jit(solution)/shard_map/attention_backward/pallas_call | solution.py:862
  99.1 3.3 %collective-permute-done.17 = bf16[2,2,3,72,384]{4,3,2,1,0:T(8,128)(2,1)S(1)} collective-permute-done((bf16[2,2,3,72,384]{4,3,2,1,0:T(8,128)(2,1)S(1)}, bf16[2,2,3,72,384]{4,3,2,1,0:T(8,128)(2,1)S(1)}, u32[]{:S(2)}, u32[]{:S(2)}) %collective-permute-start.17) | collective-permute-done | bytes 663584 | tf_op jit(solution)/shard_map/ppermute | solution.py:967
  104.9 8.1 %collective-permute-done.19 = bf16[2,3,72,384]{3,2,1,0:T(8,128)(2,1)S(1)} collective-permute-done((bf16[2,3,72,384]{3,2,1,0:T(8,128)(2,1)S(1)}, bf16[2,3,72,384]{3,2,1,0:T(8,128)(2,1)S(1)}, u32[]{:S(2)}, u32[]{:S(2)}) %collective-permute-start.19) | collective-permute-done | bytes 331808 | tf_op jit(solution)/shard_map/ppermute | solution.py:967
  116.9 2.1 %collective-permute-start.22 = (bf16[3,72,384]{2,1,0:T(8,128)(2,1)S(1)}, bf16[3,72,384]{2,1,0:T(8,128)(2,1)S(1)}, u32[]{:S(2)}, u32[]{:S(2)}) collective-permute-start(bf16[3,72,384]{2,1,0:T(8,128)(2,1)S(1)} %get-tuple-element.120), channel_id=1, source_target_pairs={{0,2},{1,3},{2,0},{3,1},{4,6},{5,7},{6,4},{7,5},{8,10},{9,11},{10,... | collective-permute-start | bytes 497672 | tf_op jit(solution)/shard_map/ppermute | solution.py:257
  118.9 2.8 %collective-permute-start.23 = (bf16[3,72,384]{2,1,0:T(8,128)(2,1)S(1)}, bf16[3,72,384]{2,1,0:T(8,128)(2,1)S(1)}, u32[]{:S(2)}, u32[]{:S(2)}) collective-permute-start(bf16[3,72,384]{2,1,0:T(8,128)(2,1)S(1)} %get-tuple-element.119), channel_id=1, source_target_pairs={{0,3},{1,0},{2,1},{3,2},{4,7},{5,4},{6,5},{7,6},{8,11},{9,8},{10,9... | collective-permute-start | bytes 497672 | tf_op jit(solution)/shard_map/ppermute | solution.py:257
  122.0 8.0 %collective-permute-done.22 = bf16[3,72,384]{2,1,0:T(8,128)(2,1)S(1)} collective-permute-done((bf16[3,72,384]{2,1,0:T(8,128)(2,1)S(1)}, bf16[3,72,384]{2,1,0:T(8,128)(2,1)S(1)}, u32[]{:S(2)}, u32[]{:S(2)}) %collective-permute-start.22) | collective-permute-done | bytes 165920 | tf_op jit(solution)/shard_map/ppermute | solution.py:257
  136.3 3.0 %collective-permute-done.32 = bf16[2,80,384]{2,1,0:T(8,128)(2,1)S(1)} collective-permute-done((bf16[2,80,384]{2,1,0:T(8,128)(2,1)S(1)}, bf16[2,80,384]{2,1,0:T(8,128)(2,1)S(1)}, u32[]{:S(2)}, u32[]{:S(2)}) %collective-permute-start.32) | collective-permute-done | bytes 122912 | tf_op jit(solution)/shard_map/ppermute | solution.py:967
  139.4 5.3 %collective-permute-start.33 = (bf16[80,384]{1,0:T(8,128)(2,1)S(1)}, bf16[80,384]{1,0:T(8,128)(2,1)S(1)}, u32[]{:S(2)}, u32[]{:S(2)}) collective-permute-start(bf16[80,384]{1,0:T(8,128)(2,1)S(1)} %get-tuple-element.123), channel_id=1, source_target_pairs={{0,2},{1,3},{2,0},{3,1},{4,6},{5,7},{6,4},{7,5},{8,10},{9,11},{10,... | collective-permute-start | bytes 184328 | tf_op jit(solution)/shard_map/ppermute | solution.py:257
  145.7 4.7 %collective-permute-done.28 = bf16[3,72,384]{2,1,0:T(8,128)(2,1)S(1)} collective-permute-done((bf16[3,72,384]{2,1,0:T(8,128)(2,1)S(1)}, bf16[3,72,384]{2,1,0:T(8,128)(2,1)S(1)}, u32[]{:S(2)}, u32[]{:S(2)}) %collective-permute-start.28) | collective-permute-done | bytes 165920 | tf_op jit(solution)/shard_map/ppermute | solution.py:967
  152.3 4.6 %collective-permute-done.31 = bf16[80,384]{1,0:T(8,128)(2,1)S(1)} collective-permute-done((bf16[80,384]{1,0:T(8,128)(2,1)S(1)}, bf16[80,384]{1,0:T(8,128)(2,1)S(1)}, u32[]{:S(2)}, u32[]{:S(2)}) %collective-permute-start.31) | collective-permute-done | bytes 61472 | tf_op jit(solution)/shard_map/ppermute | solution.py:257
  157.0 10.6 %all-gather = bf16[576,384]{1,0:T(8,128)(2,1)} all-gather(bf16[72,384]{1,0:T(8,128)(2,1)S(1)} %slice.292), channel_id=2, replica_groups=mesh['rep'=8,'shard'=4] {'rep'}, dimensions={0}, use_global_device_ids=true | all-gather | bytes 497664 | tf_op jit(solution)/shard_map/all_gather | solution.py:1107
  169.1 3.5 %unpack_mlp.1 = (f32[144,1536]{1,0:T(8,128)}, f32[144,1536]{1,0:T(8,128)}, f32[576,384]{1,0:T(8,128)}) custom-call(s32[3]{0:T(128)} %pad_add_fusion.refs_0_.at_ref, bf16[4,3,72,384]{3,2,1,0:T(8,128)(2,1)} %copy-done, bf16[4,3,72,384]{3,2,1,0:T(8,128)(2,1)} %copy-done.4), custom_call_target="tpu_custom_call" | custom-call | tf_op jit(solution)/shard_map/unpack_mlp/pallas_call | solution.py:933
  172.7 2.0 %unpack_attn.1 = (f32[144,576]{1,0:T(8,128)}, f32[144,192]{1,0:T(8,128)}, f32[144,192]{1,0:T(8,128)}, f32[144,576]{1,0:T(8,128)}) custom-call(bf16[8,72,384]{2,1,0:T(8,128)(2,1)} %bitcast.163), custom_call_target="tpu_custom_call" | custom-call | tf_op jit(solution)/shard_map/unpack_attn/pallas_call | solution.py:907
  (123 shorter events, 47.0 us)
Async XLA Ops:
  3.6 9.9 %collective-permute-start = (bf16[80,384]{1,0:T(8,128)(2,1)S(1)}, bf16[80,384]{1,0:T(8,128)(2,1)S(1)}, u32[]{:S(2)}, u32[]{:S(2)}) collective-permute-start(bf16[80,384]{1,0:T(8,128)(2,1)S(1)} %pad_maximum_fusion.6), channel_id=1, source_target_pairs={{0,1},{1,2},{2,3},{3,0},{4,5},{5,6},{6,7},{7,4},{8,9},{9,10},{10,1... | collective-permute-start | bytes 184328 | tf_op jit(solution)/shard_map/ppermute | solution.py:257
  6.8 9.5 %collective-permute-start.1 = (bf16[80,384]{1,0:T(8,128)(2,1)S(1)}, bf16[80,384]{1,0:T(8,128)(2,1)S(1)}, u32[]{:S(2)}, u32[]{:S(2)}) collective-permute-start(bf16[80,384]{1,0:T(8,128)(2,1)S(1)} %pad_maximum_fusion.6), channel_id=1, source_target_pairs={{0,2},{1,3},{2,0},{3,1},{4,6},{5,7},{6,4},{7,5},{8,10},{9,11},{10,... | collective-permute-start | bytes 184328 | tf_op jit(solution)/shard_map/ppermute | solution.py:257
  12.5 15.3 %collective-permute-start.6 = (bf16[3,72,384]{2,1,0:T(8,128)(2,1)S(1)}, bf16[3,72,384]{2,1,0:T(8,128)(2,1)S(1)}, u32[]{:S(2)}, u32[]{:S(2)}) collective-permute-start(bf16[3,72,384]{2,1,0:T(8,128)(2,1)S(1)} %pad_maximum_fusion.5), channel_id=1, source_target_pairs={{0,1},{1,2},{2,3},{3,0},{4,5},{5,6},{6,7},{7,4},{8,9},{9,10},{10,1... | collective-permute-start | bytes 497672 | tf_op jit(solution)/shard_map/ppermute | solution.py:257
  13.2 14.5 %collective-permute-start.7 = (bf16[3,72,384]{2,1,0:T(8,128)(2,1)S(1)}, bf16[3,72,384]{2,1,0:T(8,128)(2,1)S(1)}, u32[]{:S(2)}, u32[]{:S(2)}) collective-permute-start(bf16[3,72,384]{2,1,0:T(8,128)(2,1)S(1)} %pad_maximum_fusion.5), channel_id=1, source_target_pairs={{0,2},{1,3},{2,0},{3,1},{4,6},{5,7},{6,4},{7,5},{8,10},{9,11},{10,... | collective-permute-start | bytes 497672 | tf_op jit(solution)/shard_map/ppermute | solution.py:257
  13.5 14.2 %collective-permute-start.8 = (bf16[3,72,384]{2,1,0:T(8,128)(2,1)S(1)}, bf16[3,72,384]{2,1,0:T(8,128)(2,1)S(1)}, u32[]{:S(2)}, u32[]{:S(2)}) collective-permute-start(bf16[3,72,384]{2,1,0:T(8,128)(2,1)S(1)} %pad_maximum_fusion.5), channel_id=1, source_target_pairs={{0,3},{1,0},{2,1},{3,2},{4,7},{5,4},{6,5},{7,6},{8,11},{9,8},{10,9... | collective-permute-start | bytes 497672 | tf_op jit(solution)/shard_map/ppermute | solution.py:257
  27.9 13.8 %collective-permute-start.10 = (bf16[9,72,384]{2,1,0:T(8,128)(2,1)S(1)}, bf16[9,72,384]{2,1,0:T(8,128)(2,1)S(1)}, u32[]{:S(2)}, u32[]{:S(2)}) collective-permute-start(bf16[9,72,384]{2,1,0:T(8,128)(2,1)S(1)} %constant_dynamic-update-slice_fusion), channel_id=1, source_target_pairs={{0,16},{4,20},{8,24},{12,28},{16,0},{20,4},{24,8},{28,12},{1,17},{... | collective-permute-start | bytes 1493000 | tf_op jit(solution)/shard_map/ppermute | solution.py:967
  29.5 13.5 %collective-permute-start.9 = (bf16[9,72,384]{2,1,0:T(8,128)(2,1)S(1)}, bf16[9,72,384]{2,1,0:T(8,128)(2,1)S(1)}, u32[]{:S(2)}, u32[]{:S(2)}) collective-permute-start(bf16[9,72,384]{2,1,0:T(8,128)(2,1)S(1)} %constant_dynamic-update-slice_fusion), channel_id=1, source_target_pairs={{0,8},{4,12},{8,0},{12,4},{16,24},{20,28},{24,16},{28,20},{1,9},{5... | collective-permute-start | bytes 1493000 | tf_op jit(solution)/shard_map/ppermute | solution.py:967
  44.6 7.7 %collective-permute-start.13 = (bf16[5,72,384]{2,1,0:T(8,128)(2,1)S(1)}, bf16[5,72,384]{2,1,0:T(8,128)(2,1)S(1)}, u32[]{:S(2)}, u32[]{:S(2)}) collective-permute-start(bf16[5,72,384]{2,1,0:T(8,128)(2,1)S(1)} %slice.146), channel_id=1, source_target_pairs={{0,16},{4,20},{8,24},{12,28},{16,0},{20,4},{24,8},{28,12},{1,17},{... | collective-permute-start | bytes 829448 | tf_op jit(solution)/shard_map/ppermute | solution.py:967
  85.3 17.0 %collective-permute-start.17 = (bf16[2,2,3,72,384]{4,3,2,1,0:T(8,128)(2,1)S(1)}, bf16[2,2,3,72,384]{4,3,2,1,0:T(8,128)(2,1)S(1)}, u32[]{:S(2)}, u32[]{:S(2)}) collective-permute-start(bf16[2,2,3,72,384]{4,3,2,1,0:T(8,128)(2,1)S(1)} %get-tuple-element.111), channel_id=1, source_target_pairs={{0,16},{4,20},{8,24},{12,28},{16,0},{20,4},{24,8},{28,12},{1,17},{... | collective-permute-start | bytes 1990664 | tf_op jit(solution)/shard_map/ppermute | solution.py:967
  86.0 16.7 %collective-permute-start.16 = (bf16[2,2,3,72,384]{4,3,2,1,0:T(8,128)(2,1)S(1)}, bf16[2,2,3,72,384]{4,3,2,1,0:T(8,128)(2,1)S(1)}, u32[]{:S(2)}, u32[]{:S(2)}) collective-permute-start(bf16[2,2,3,72,384]{4,3,2,1,0:T(8,128)(2,1)S(1)} %get-tuple-element.113), channel_id=1, source_target_pairs={{0,8},{4,12},{8,0},{12,4},{16,24},{20,28},{24,16},{28,20},{1,9},{5... | collective-permute-start | bytes 1990664 | tf_op jit(solution)/shard_map/ppermute | solution.py:967
  102.7 10.8 %collective-permute-start.20 = (bf16[4,4,80,384]{3,2,1,0:T(8,128)(2,1)}, bf16[4,4,80,384]{3,2,1,0:T(8,128)(2,1)S(1)}, u32[]{:S(2)}, u32[]{:S(2)}) collective-permute-start(bf16[4,4,80,384]{3,2,1,0:T(8,128)(2,1)} %get-tuple-element.90), channel_id=1, source_target_pairs={{0,4},{4,0},{8,12},{12,8},{16,20},{20,16},{24,28},{28,24},{1,5},{5... | collective-permute-start | bytes 2949128 | tf_op jit(solution)/shard_map/ppermute | solution.py:967
  102.7 10.3 %collective-permute-start.19 = (bf16[2,3,72,384]{3,2,1,0:T(8,128)(2,1)S(1)}, bf16[2,3,72,384]{3,2,1,0:T(8,128)(2,1)S(1)}, u32[]{:S(2)}, u32[]{:S(2)}) collective-permute-start(bf16[2,3,72,384]{3,2,1,0:T(8,128)(2,1)S(1)} %fusion.6), channel_id=1, source_target_pairs={{0,8},{4,12},{8,0},{12,4},{16,24},{20,28},{24,16},{28,20},{1,9},{5... | collective-permute-start | bytes 995336 | tf_op jit(solution)/shard_map/ppermute | solution.py:967
  103.4 10.0 %collective-permute-start.18 = (bf16[2,3,72,384]{3,2,1,0:T(8,128)(2,1)S(1)}, bf16[2,3,72,384]{3,2,1,0:T(8,128)(2,1)S(1)}, u32[]{:S(2)}, u32[]{:S(2)}) collective-permute-start(bf16[2,3,72,384]{3,2,1,0:T(8,128)(2,1)S(1)} %fusion.5), channel_id=1, source_target_pairs={{0,16},{4,20},{8,24},{12,28},{16,0},{20,4},{24,8},{28,12},{1,17},{... | collective-permute-start | bytes 995336 | tf_op jit(solution)/shard_map/ppermute | solution.py:967
  113.7 18.2 %collective-permute-start.25 = (bf16[2,2,80,384]{3,2,1,0:T(8,128)(2,1)S(1)}, bf16[2,2,80,384]{3,2,1,0:T(8,128)(2,1)S(1)}, u32[]{:S(2)}, u32[]{:S(2)}) collective-permute-start(bf16[2,2,80,384]{3,2,1,0:T(8,128)(2,1)S(1)} %get-tuple-element.115), channel_id=1, source_target_pairs={{0,16},{4,20},{8,24},{12,28},{16,0},{20,4},{24,8},{28,12},{1,17},{... | collective-permute-start | bytes 737288 | tf_op jit(solution)/shard_map/ppermute | solution.py:967
  115.2 16.7 %collective-permute-start.24 = (bf16[2,2,80,384]{3,2,1,0:T(8,128)(2,1)S(1)}, bf16[2,2,80,384]{3,2,1,0:T(8,128)(2,1)S(1)}, u32[]{:S(2)}, u32[]{:S(2)}) collective-permute-start(bf16[2,2,80,384]{3,2,1,0:T(8,128)(2,1)S(1)} %get-tuple-element.117), channel_id=1, source_target_pairs={{0,8},{4,12},{8,0},{12,4},{16,24},{20,28},{24,16},{28,20},{1,9},{5... | collective-permute-start | bytes 737288 | tf_op jit(solution)/shard_map/ppermute | solution.py:967
  116.9 13.2 %collective-permute-start.22 = (bf16[3,72,384]{2,1,0:T(8,128)(2,1)S(1)}, bf16[3,72,384]{2,1,0:T(8,128)(2,1)S(1)}, u32[]{:S(2)}, u32[]{:S(2)}) collective-permute-start(bf16[3,72,384]{2,1,0:T(8,128)(2,1)S(1)} %get-tuple-element.120), channel_id=1, source_target_pairs={{0,2},{1,3},{2,0},{3,1},{4,6},{5,7},{6,4},{7,5},{8,10},{9,11},{10,... | collective-permute-start | bytes 497672 | tf_op jit(solution)/shard_map/ppermute | solution.py:257
  118.9 11.1 %collective-permute-start.23 = (bf16[3,72,384]{2,1,0:T(8,128)(2,1)S(1)}, bf16[3,72,384]{2,1,0:T(8,128)(2,1)S(1)}, u32[]{:S(2)}, u32[]{:S(2)}) collective-permute-start(bf16[3,72,384]{2,1,0:T(8,128)(2,1)S(1)} %get-tuple-element.119), channel_id=1, source_target_pairs={{0,3},{1,0},{2,1},{3,2},{4,7},{5,4},{6,5},{7,6},{8,11},{9,8},{10,9... | collective-permute-start | bytes 497672 | tf_op jit(solution)/shard_map/ppermute | solution.py:257
  121.9 10.0 %collective-permute-start.21 = (bf16[3,72,384]{2,1,0:T(8,128)(2,1)S(1)}, bf16[3,72,384]{2,1,0:T(8,128)(2,1)S(1)}, u32[]{:S(2)}, u32[]{:S(2)}) collective-permute-start(bf16[3,72,384]{2,1,0:T(8,128)(2,1)S(1)} %fusion.16), channel_id=1, source_target_pairs={{0,1},{1,2},{2,3},{3,0},{4,5},{5,6},{6,7},{7,4},{8,9},{9,10},{10,1... | collective-permute-start | bytes 497672 | tf_op jit(solution)/shard_map/ppermute | solution.py:257
  132.0 13.2 %collective-permute-start.27 = (bf16[3,72,384]{2,1,0:T(8,128)(2,1)S(1)}, bf16[3,72,384]{2,1,0:T(8,128)(2,1)S(1)}, u32[]{:S(2)}, u32[]{:S(2)}) collective-permute-start(bf16[3,72,384]{2,1,0:T(8,128)(2,1)S(1)} %fusion.10), channel_id=1, source_target_pairs={{0,16},{4,20},{8,24},{12,28},{16,0},{20,4},{24,8},{28,12},{1,17},{... | collective-permute-start | bytes 497672 | tf_op jit(solution)/shard_map/ppermute | solution.py:967
  132.6 13.1 %collective-permute-start.26 = (bf16[3,72,384]{2,1,0:T(8,128)(2,1)S(1)}, bf16[3,72,384]{2,1,0:T(8,128)(2,1)S(1)}, u32[]{:S(2)}, u32[]{:S(2)}) collective-permute-start(bf16[3,72,384]{2,1,0:T(8,128)(2,1)S(1)} %fusion.10), channel_id=1, source_target_pairs={{0,8},{4,12},{8,0},{12,4},{16,24},{20,28},{24,16},{28,20},{1,9},{5... | collective-permute-start | bytes 497672 | tf_op jit(solution)/shard_map/ppermute | solution.py:967
  134.8 10.9 %collective-permute-start.30 = (bf16[2,80,384]{2,1,0:T(8,128)(2,1)S(1)}, bf16[2,80,384]{2,1,0:T(8,128)(2,1)S(1)}, u32[]{:S(2)}, u32[]{:S(2)}) collective-permute-start(bf16[2,80,384]{2,1,0:T(8,128)(2,1)S(1)} %fusion.17), channel_id=1, source_target_pairs={{0,16},{4,20},{8,24},{12,28},{16,0},{20,4},{24,8},{28,12},{1,17},{... | collective-permute-start | bytes 368648 | tf_op jit(solution)/shard_map/ppermute | solution.py:967
  139.4 13.0 %collective-permute-start.33 = (bf16[80,384]{1,0:T(8,128)(2,1)S(1)}, bf16[80,384]{1,0:T(8,128)(2,1)S(1)}, u32[]{:S(2)}, u32[]{:S(2)}) collective-permute-start(bf16[80,384]{1,0:T(8,128)(2,1)S(1)} %get-tuple-element.123), channel_id=1, source_target_pairs={{0,2},{1,3},{2,0},{3,1},{4,6},{5,7},{6,4},{7,5},{8,10},{9,11},{10,... | collective-permute-start | bytes 184328 | tf_op jit(solution)/shard_map/ppermute | solution.py:257
  144.7 7.6 %collective-permute-start.34 = (bf16[80,384]{1,0:T(8,128)(2,1)S(1)}, bf16[80,384]{1,0:T(8,128)(2,1)S(1)}, u32[]{:S(2)}, u32[]{:S(2)}) collective-permute-start(bf16[80,384]{1,0:T(8,128)(2,1)S(1)} %get-tuple-element.124), channel_id=1, source_target_pairs={{0,3},{1,0},{2,1},{3,2},{4,7},{5,4},{6,5},{7,6},{8,11},{9,8},{10,9... | collective-permute-start | bytes 184328 | tf_op jit(solution)/shard_map/ppermute | solution.py:257
  150.6 17.7 %collective-permute-start.29 = (bf16[4,3,72,384]{3,2,1,0:T(8,128)(2,1)S(1)}, bf16[4,3,72,384]{3,2,1,0:T(8,128)(2,1)S(1)}, u32[]{:S(2)}, u32[]{:S(2)}) collective-permute-start(bf16[4,3,72,384]{3,2,1,0:T(8,128)(2,1)S(1)} %pad_maximum_fusion.3.mine_ref), channel_id=1, source_target_pairs={{0,4},{4,0},{8,12},{12,8},{16,20},{20,16},{24,28},{28,24},{1,5},{5... | collective-permute-start | bytes 1990664 | tf_op jit(solution)/shard_map/ppermute | solution.py:967
  (21 other events, 170.0 us)

commit v4 on v3

--- a/solution.py
+++ b/solution.py
@@ -888,35 +888,15 @@
     )(at, *args)
 
 
-def unpack_attn_kernel(piece_ref, q_ref, k_ref, v_ref, o_ref):
-    half = piece_ref.shape[1]
-    columns = []
-    for c in range(piece_ref.shape[0] // 2):
-        columns.append(
-            jnp.concatenate([widen(piece_ref[2 * c]), widen(piece_ref[2 * c + 1])], axis=0)
-        )
-    full = jnp.concatenate(columns, axis=1)
-    kvw, width = k_ref.shape[1], o_ref.shape[1]
-    k_ref[...] = full[:, :kvw]
-    v_ref[...] = full[:, kvw : 2 * kvw]
-    o_ref[...] = full[:, 2 * kvw : 2 * kvw + width]
-    q_ref[...] = full[:, 2 * kvw + width :]
-
-
-def unpack_attn(pieces, shapes):
-    return pl.pallas_call(
-        unpack_attn_kernel,
-        out_shape=[jax.ShapeDtypeStruct(shape, jnp.float32) for shape in shapes],
-        name="unpack_attn",
-    )(pieces)
-
-
-def unpack_mlp_kernel(at_ref, mine_ref, pair_ref, gate_ref, up_ref, tall_ref):
+def unpack_kernel(
+    at_ref, mine_ref, pair_ref, gate_ref, up_ref, tall_ref, q_ref, k_ref, v_ref, o_ref
+):
     chip, core = at_ref[1], at_ref[2]
     half = mine_ref.shape[2]
+    columns = []
     for c in range(mine_ref.shape[0]):
         to = lax.bitwise_xor(chip, c)
-        for m in range(3):
+        for m in range(4):
             mine, pair = widen(mine_ref[to, m]), widen(pair_ref[to, m])
             upper = jnp.where(core == 0, mine, pair)
             lower = jnp.where(core == 0, pair, mine)
@@ -924,22 +904,30 @@
                 ref = (gate_ref, up_ref)[m]
                 ref[:half, c * CHUNK : (c + 1) * CHUNK] = upper
                 ref[half:, c * CHUNK : (c + 1) * CHUNK] = lower
-            else:
+            elif m == 2:
                 tall_ref[2 * c * half : (2 * c + 1) * half, :] = upper
                 tall_ref[(2 * c + 1) * half : (2 * c + 2) * half, :] = lower
-
-
-def unpack_mlp(at, mine, pair, shapes):
+            else:
+                columns.append(jnp.concatenate([upper, lower], axis=0))
+    full = jnp.concatenate(columns, axis=1)
+    kvw, width = k_ref.shape[1], o_ref.shape[1]
+    k_ref[...] = full[:, :kvw]
+    v_ref[...] = full[:, kvw : 2 * kvw]
+    o_ref[...] = full[:, 2 * kvw : 2 * kvw + width]
+    q_ref[...] = full[:, 2 * kvw + width :]
+
+
+def unpack(at, mine, pair, shapes):
     return pl.pallas_call(
-        unpack_mlp_kernel,
+        unpack_kernel,
         grid_spec=pltpu.PrefetchScalarGridSpec(
             num_scalar_prefetch=1,
             grid=(),
             in_specs=[pl.BlockSpec(memory_space=pltpu.VMEM)] * 2,
-            out_specs=[pl.BlockSpec(memory_space=pltpu.VMEM)] * 3,
+            out_specs=[pl.BlockSpec(memory_space=pltpu.VMEM)] * len(shapes),
         ),
         out_shape=[jax.ShapeDtypeStruct(shape, jnp.float32) for shape in shapes],
-        name="unpack_mlp",
+        name="unpack",
     )(at, mine, pair)
 
 
@@ -969,7 +957,9 @@
 
 def plane_gather(own):
     from_x, from_y = swapped(own, 2), swapped(own, 4)
-    mine = jnp.stack([own, from_x, from_y, swapped(from_y, 2)])
+    mid = own.shape[0] // 2
+    across = jnp.concatenate([swapped(from_y[:mid], 2), swapped(from_x[mid:], 4)])
+    mine = jnp.stack([own, from_x, from_y, across])
     return mine, swapped(mine, 1)
 
 
@@ -1103,18 +1093,19 @@
     attn_blocks = own_blocks(*attn_one, *attn_two)
     attn_total = added(attn_blocks[0], exchange_shards(attn_blocks))
     half = rows // 2
-    total_mine, total_pair = plane_gather(wide_total)
-    attn_pieces = lax.all_gather(narrow(attn_total[:half]), "rep")
-    total_pair, attn_pieces = barrier((total_pair, attn_pieces))
-    q_grad, k_grad, v_grad, o_grad = unpack_attn(
-        attn_pieces,
-        (query_weight.shape, key_weight.shape, value_weight.shape, output_weight.shape),
-    )
-    gate_grad, up_grad, tall_grad = unpack_mlp(
+    totals = jnp.concatenate([wide_total, narrow(attn_total[:half])[None]])
+    gate_grad, up_grad, tall_grad, q_grad, k_grad, v_grad, o_grad = unpack(
         at,
-        total_mine,
-        total_pair,
-        (gate_weight.shape, up_weight.shape, tall.shape),
+        *plane_gather(totals),
+        (
+            gate_weight.shape,
+            up_weight.shape,
+            tall.shape,
+            query_weight.shape,
+            key_weight.shape,
+            value_weight.shape,
+            output_weight.shape,
+        ),
     )
     both = attn_total[half : half + 4].reshape(2, 2 * CHUNK)
     both = lax.dynamic_slice(both, (0, lax.axis_index("shard") * rows), (2, rows))

time: 175 us -> 169 us (0.966)
  blocking collectives: 10.6 us -> 0 us
  waiting for transfers between devices: 56.6 us -> 64.5 us
  starting transfers between devices: 44.6 us -> 42 us
    all_gather x1 -> x0, blocking collectives: 10.6 us -> none  [on_device(): attn_pieces = lax.all_gather(narrow(attn_total[:half]), 'rep')]
    ppermute x23 -> x24, waiting for transfers between devices: 42.1 us -> 49.8 us  [swapped(): return lax.ppermute(values, 'rep', [(i, i ^ bit) for i in range(size)])]
    pallas_call x2 -> x1, Pallas kernels: 5.52 us -> 4.04 us  [unpack(): pl.pallas_call(unpack_kernel, grid_spec=pltpu.PrefetchScalarGridSpec(num_...]
    ppermute x23 -> x24, starting transfers between devices: 21.2 us -> 20.1 us  [swapped(): return lax.ppermute(values, 'rep', [(i, i ^ bit) for i in range(size)])]
  transfers between devices with their start and end apart: 35 -> 36, of which waited for: 18 -> 24; matrix products, arithmetic and copies ran while one was open for 4% -> 4% of each run, Pallas kernels for 12% -> 12%
where the time goes in v4:
time: 169 us; the launch traced here: 168 us
  waiting for transfers between devices  64.5 us (38%)
  Pallas kernels  44.5 us (26%)
  starting transfers between devices  42 us (25%)
  local copies, waits for them, and re-layouts  9.13 us (5%)
  other arithmetic  6.98 us (4%)
    ppermute x24, waiting for transfers between devices, swapped(): return lax.ppermute(values, 'rep', [(i, i ^ bit) for i in range(size)])  49.8 us
    ppermute x12, starting transfers between devices, shifted(): lax.ppermute(values, 'shard', [(i, (i + steps) % size) for i in range(siz...  21.8 us
    ppermute x24, starting transfers between devices, swapped(): return lax.ppermute(values, 'rep', [(i, i ^ bit) for i in range(size)])  20.1 us
    pallas_call x1, Pallas kernels, mlp(): pl.pallas_call(kernel, grid_spec=pltpu.PrefetchScalarGridSpec(num_scalar_...  19.5 us
    ppermute x12, waiting for transfers between devices, shifted(): lax.ppermute(values, 'shard', [(i, (i + steps) % size) for i in range(siz...  14.7 us
    pallas_call x1, Pallas kernels, attention_backward(): pl.pallas_call(kernel, grid_spec=pltpu.PrefetchScalarGridSpec(num_scalar_...  12.5 us
    pallas_call x1, Pallas kernels, attention_forward(): pl.pallas_call(kernel, grid_spec=pltpu.PrefetchScalarGridSpec(num_scalar_...  8.39 us
    pallas_call x1, Pallas kernels, unpack(): pl.pallas_call(unpack_kernel, grid_spec=pltpu.PrefetchScalarGridSpec(num_...  4.04 us
  transfers between devices with their start and end apart: 36, of which 24 were waited for; matrix products, arithmetic and copies ran while one was open for 4% of the time, Pallas kernels for 12%

profile of v4, /device:TPU:0, one launch (start us, length us, event | category | flops | bytes accessed | tf_op | source)
XLA Modules:
  0.0 168.2 jit_solution(11496138311824435096)
XLA Ops:
  3.6 3.2 %collective-permute-start = (bf16[80,384]{1,0:T(8,128)(2,1)S(1)}, bf16[80,384]{1,0:T(8,128)(2,1)S(1)}, u32[]{:S(2)}, u32[]{:S(2)}) collective-permute-start(bf16[80,384]{1,0:T(8,128)(2,1)S(1)} %pad_maximum_fusion.7), channel_id=1, source_target_pairs={{0,1},{1,2},{2,3},{3,0},{4,5},{5,6},{6,7},{7,4},{8,9},{9,10},{10,1... | collective-permute-start | bytes 184328 | tf_op jit(solution)/shard_map/ppermute | solution.py:257
  6.8 2.6 %collective-permute-start.1 = (bf16[80,384]{1,0:T(8,128)(2,1)S(1)}, bf16[80,384]{1,0:T(8,128)(2,1)S(1)}, u32[]{:S(2)}, u32[]{:S(2)}) collective-permute-start(bf16[80,384]{1,0:T(8,128)(2,1)S(1)} %pad_maximum_fusion.7), channel_id=1, source_target_pairs={{0,2},{1,3},{2,0},{3,1},{4,6},{5,7},{6,4},{7,5},{8,10},{9,11},{10,... | collective-permute-start | bytes 184328 | tf_op jit(solution)/shard_map/ppermute | solution.py:257
  13.5 2.8 %collective-permute-start.8 = (bf16[3,72,384]{2,1,0:T(8,128)(2,1)S(1)}, bf16[3,72,384]{2,1,0:T(8,128)(2,1)S(1)}, u32[]{:S(2)}, u32[]{:S(2)}) collective-permute-start(bf16[3,72,384]{2,1,0:T(8,128)(2,1)S(1)} %pad_maximum_fusion.6), channel_id=1, source_target_pairs={{0,3},{1,0},{2,1},{3,2},{4,7},{5,4},{6,5},{7,6},{8,11},{9,8},{10,9... | collective-permute-start | bytes 497672 | tf_op jit(solution)/shard_map/ppermute | solution.py:257
  19.6 2.4 %collective-permute-done.4 = bf16[3,80,384]{2,1,0:T(8,128)(2,1)S(1)} collective-permute-done((bf16[3,80,384]{2,1,0:T(8,128)(2,1)S(1)}, bf16[3,80,384]{2,1,0:T(8,128)(2,1)S(1)}, u32[]{:S(2)}, u32[]{:S(2)}) %collective-permute-start.4) | collective-permute-done | bytes 184352 | tf_op jit(solution)/shard_map/ppermute | solution.py:955
  25.1 2.4 %collective-permute-done.5 = bf16[3,80,384]{2,1,0:T(8,128)(2,1)S(1)} collective-permute-done((bf16[3,80,384]{2,1,0:T(8,128)(2,1)S(1)}, bf16[3,80,384]{2,1,0:T(8,128)(2,1)S(1)}, u32[]{:S(2)}, u32[]{:S(2)}) %collective-permute-start.5) | collective-permute-done | bytes 184352 | tf_op jit(solution)/shard_map/ppermute | solution.py:955
  31.9 8.4 %attention_forward.1 = (bf16[576,1536]{1,0:T(8,128)(2,1)}, f32[576,128]{1,0:T(8,128)}, f32[576,384]{1,0:T(8,128)}, bf16[3,64,1152]{2,1,0:T(8,128)(2,1)}, bf16[3,...) custom-call(s32[3]{0:T(128)} %pad_add_fusion.refs_0_.at_ref, ...), custom_call_target="tpu_custom_call" | custom-call | flops 1500000000 | bytes 8000000 | tf_op jit(solution)/shard_map/attention_forward/pallas_call | solution.py:575
  45.2 4.6 %collective-permute-done.12 = bf16[4,72,384]{2,1,0:T(8,128)(2,1)S(1)} collective-permute-done((bf16[4,72,384]{2,1,0:T(8,128)(2,1)S(1)}, bf16[4,72,384]{2,1,0:T(8,128)(2,1)S(1)}, u32[]{:S(2)}, u32[]{:S(2)}) %collective-permute-start.12) | collective-permute-done | bytes 221216 | tf_op jit(solution)/shard_map/ppermute | solution.py:955
  49.8 2.5 %collective-permute-done.13 = bf16[5,72,384]{2,1,0:T(8,128)(2,1)S(1)} collective-permute-done((bf16[5,72,384]{2,1,0:T(8,128)(2,1)S(1)}, bf16[5,72,384]{2,1,0:T(8,128)(2,1)S(1)}, u32[]{:S(2)}, u32[]{:S(2)}) %collective-permute-start.13) | collective-permute-done | bytes 276512 | tf_op jit(solution)/shard_map/ppermute | solution.py:955
  54.3 2.4 %collective-permute-done.14 = bf16[4,9,72,384]{3,2,1,0:T(8,128)(2,1)S(1)} collective-permute-done((bf16[4,9,72,384]{3,2,1,0:T(8,128)(2,1)S(1)}, bf16[4,9,72,384]{3,2,1,0:T(8,128)(2,1)S(1)}, u32[]{:S(2)}, u32[]{:S(2)}) %collective-permute-start.14) | collective-permute-done | bytes 1990688 | tf_op jit(solution)/shard_map/ppermute | solution.py:955
  58.1 19.5 %mlp.1 = (bf16[576,384]{1,0:T(8,128)(2,1)}, f32[576,384]{1,0:T(8,128)}, f32[576,128]{1,0:T(8,128)}, bf16[4,4,3,72,384]{4,3,2,1,0:T(8,128)(2,1)}, bf16[4,4,3,72,384]{4,3,2,1,0:T(8,128)(2,1)}) custom-call(s32[3]{0:T(128)} %pad_add_fusion.refs_0_.at_ref, f32[576,384]{1,0:T(8,128)} %get-tuple-element.67.refs_1_, bf16[576,384]{1,0:T(8,128)(2,1)} %bitcast.184, ...), custom_call_target="tpu_custom_call" | custom-call | flops 6200000000 | bytes 14000000 | tf_op jit(solution)/shard_map/mlp/pallas_call | solution.py:705
  77.7 5.1 %collective-permute-done.15 = bf16[4,4,3,72,384]{4,3,2,1,0:T(8,128)(2,1)S(1)} collective-permute-done((bf16[4,4,3,72,384]{4,3,2,1,0:T(8,128)(2,1)}, bf16[4,4,3,72,384]{4,3,2,1,0:T(8,128)(2,1)S(1)}, u32[]{:S(2)}, u32[]{:S(2)}) %collective-permute-start.15) | collective-permute-done | bytes 2654240 | tf_op jit(solution)/shard_map/ppermute | solution.py:955
  86.5 12.5 %attention_backward.1 = (f32[576,384]{1,0:T(8,128)}, bf16[4,4,80,384]{3,2,1,0:T(8,128)(2,1)}, bf16[4,4,80,384]{3,2,1,0:T(8,128)(2,1)}) custom-call(s32[3]{0:T(128)} %pad_add_fusion.refs_0_.at_ref, bf16[576,384]{1,0:T(8,128)(2,1)} %bitcast.186, f32[576,384]{1,0:T(8,128)} %get-tuple-element.72.refs_2_, s32[1,384]{1,0:T(1,128)} %refs_3_.1, ...), custom_call_target="tpu_custom_call" | custom-call | flops 3000000000 | bytes 9000000 | tf_op jit(solution)/shard_map/attention_backward/pallas_call | solution.py:862
  99.1 3.3 %collective-permute-done.17 = bf16[2,2,3,72,384]{4,3,2,1,0:T(8,128)(2,1)S(1)} collective-permute-done((bf16[2,2,3,72,384]{4,3,2,1,0:T(8,128)(2,1)S(1)}, bf16[2,2,3,72,384]{4,3,2,1,0:T(8,128)(2,1)S(1)}, u32[]{:S(2)}, u32[]{:S(2)}) %collective-permute-start.17) | collective-permute-done | bytes 663584 | tf_op jit(solution)/shard_map/ppermute | solution.py:955
  104.9 8.1 %collective-permute-done.19 = bf16[2,3,72,384]{3,2,1,0:T(8,128)(2,1)S(1)} collective-permute-done((bf16[2,3,72,384]{3,2,1,0:T(8,128)(2,1)S(1)}, bf16[2,3,72,384]{3,2,1,0:T(8,128)(2,1)S(1)}, u32[]{:S(2)}, u32[]{:S(2)}) %collective-permute-start.19) | collective-permute-done | bytes 331808 | tf_op jit(solution)/shard_map/ppermute | solution.py:955
  116.9 2.1 %collective-permute-start.22 = (bf16[3,72,384]{2,1,0:T(8,128)(2,1)S(1)}, bf16[3,72,384]{2,1,0:T(8,128)(2,1)S(1)}, u32[]{:S(2)}, u32[]{:S(2)}) collective-permute-start(bf16[3,72,384]{2,1,0:T(8,128)(2,1)S(1)} %get-tuple-element.116), channel_id=1, source_target_pairs={{0,2},{1,3},{2,0},{3,1},{4,6},{5,7},{6,4},{7,5},{8,10},{9,11},{10,... | collective-permute-start | bytes 497672 | tf_op jit(solution)/shard_map/ppermute | solution.py:257
  118.9 2.8 %collective-permute-start.23 = (bf16[3,72,384]{2,1,0:T(8,128)(2,1)S(1)}, bf16[3,72,384]{2,1,0:T(8,128)(2,1)S(1)}, u32[]{:S(2)}, u32[]{:S(2)}) collective-permute-start(bf16[3,72,384]{2,1,0:T(8,128)(2,1)S(1)} %get-tuple-element.115), channel_id=1, source_target_pairs={{0,3},{1,0},{2,1},{3,2},{4,7},{5,4},{6,5},{7,6},{8,11},{9,8},{10,9... | collective-permute-start | bytes 497672 | tf_op jit(solution)/shard_map/ppermute | solution.py:257
  122.0 8.0 %collective-permute-done.22 = bf16[3,72,384]{2,1,0:T(8,128)(2,1)S(1)} collective-permute-done((bf16[3,72,384]{2,1,0:T(8,128)(2,1)S(1)}, bf16[3,72,384]{2,1,0:T(8,128)(2,1)S(1)}, u32[]{:S(2)}, u32[]{:S(2)}) %collective-permute-start.22) | collective-permute-done | bytes 165920 | tf_op jit(solution)/shard_map/ppermute | solution.py:257
  133.2 3.6 %collective-permute-done.28 = bf16[2,80,384]{2,1,0:T(8,128)(2,1)S(1)} collective-permute-done((bf16[2,80,384]{2,1,0:T(8,128)(2,1)S(1)}, bf16[2,80,384]{2,1,0:T(8,128)(2,1)S(1)}, u32[]{:S(2)}, u32[]{:S(2)}) %collective-permute-start.28) | collective-permute-done | bytes 122912 | tf_op jit(solution)/shard_map/ppermute | solution.py:955
  136.9 3.8 %collective-permute-start.29 = (bf16[80,384]{1,0:T(8,128)(2,1)S(1)}, bf16[80,384]{1,0:T(8,128)(2,1)S(1)}, u32[]{:S(2)}, u32[]{:S(2)}) collective-permute-start(bf16[80,384]{1,0:T(8,128)(2,1)S(1)} %get-tuple-element.121), channel_id=1, source_target_pairs={{0,2},{1,3},{2,0},{3,1},{4,6},{5,7},{6,4},{7,5},{8,10},{9,11},{10,... | collective-permute-start | bytes 184328 | tf_op jit(solution)/shard_map/ppermute | solution.py:257
  143.1 2.3 %collective-permute-done.30 = bf16[80,384]{1,0:T(8,128)(2,1)S(1)} collective-permute-done((bf16[80,384]{1,0:T(8,128)(2,1)S(1)}, bf16[80,384]{1,0:T(8,128)(2,1)S(1)}, u32[]{:S(2)}, u32[]{:S(2)}) %collective-permute-start.30) | collective-permute-done | bytes 61472 | tf_op jit(solution)/shard_map/ppermute | solution.py:257
  145.4 2.4 %collective-permute-done.27 = bf16[80,384]{1,0:T(8,128)(2,1)S(1)} collective-permute-done((bf16[80,384]{1,0:T(8,128)(2,1)S(1)}, bf16[80,384]{1,0:T(8,128)(2,1)S(1)}, u32[]{:S(2)}, u32[]{:S(2)}) %collective-permute-start.27) | collective-permute-done | bytes 61472 | tf_op jit(solution)/shard_map/ppermute | solution.py:257
  149.1 5.7 %collective-permute-done.32 = bf16[4,72,384]{2,1,0:T(8,128)(2,1)S(1)} collective-permute-done((bf16[4,72,384]{2,1,0:T(8,128)(2,1)S(1)}, bf16[4,72,384]{2,1,0:T(8,128)(2,1)S(1)}, u32[]{:S(2)}, u32[]{:S(2)}) %collective-permute-start.32) | collective-permute-done | bytes 221216 | tf_op jit(solution)/shard_map/ppermute | solution.py:955
  156.8 2.8 %collective-permute-done.33 = bf16[2,72,384]{2,1,0:T(8,128)(2,1)S(1)} collective-permute-done((bf16[2,72,384]{2,1,0:T(8,128)(2,1)S(1)}, bf16[2,72,384]{2,1,0:T(8,128)(2,1)S(1)}, u32[]{:S(2)}, u32[]{:S(2)}) %collective-permute-start.33) | collective-permute-done | bytes 110624 | tf_op jit(solution)/shard_map/ppermute | solution.py:955
  164.1 4.0 %unpack.1 = (f32[144,1536]{1,0:T(8,128)}, f32[144,1536]{1,0:T(8,128)}, f32[576,384]{1,0:T(8,128)}, f32[144,576]{1,0:T(8,128)}, f32[144,192]{1,0:T(8,128)}, /*index=5*/f32[144,192]{1,0:T(8,128)}, f32[144,576]{1,0:T(8,128)}) custom-call(s32[3]{0:T(128)} %pad_add_fusion.refs_0_.at_ref, bf16[4,4,72,384]{3,2,1,0:T(8,128)(2,1)} %copy-done, ...), custom_call_target="tpu_custom_call" | custom-call | tf_op jit(solution)/shard_map/unpack/pallas_call | solution.py:921
  (127 shorter events, 49.7 us)
Async XLA Ops:
  3.6 9.9 %collective-permute-start = (bf16[80,384]{1,0:T(8,128)(2,1)S(1)}, bf16[80,384]{1,0:T(8,128)(2,1)S(1)}, u32[]{:S(2)}, u32[]{:S(2)}) collective-permute-start(bf16[80,384]{1,0:T(8,128)(2,1)S(1)} %pad_maximum_fusion.7), channel_id=1, source_target_pairs={{0,1},{1,2},{2,3},{3,0},{4,5},{5,6},{6,7},{7,4},{8,9},{9,10},{10,1... | collective-permute-start | bytes 184328 | tf_op jit(solution)/shard_map/ppermute | solution.py:257
  6.8 9.5 %collective-permute-start.1 = (bf16[80,384]{1,0:T(8,128)(2,1)S(1)}, bf16[80,384]{1,0:T(8,128)(2,1)S(1)}, u32[]{:S(2)}, u32[]{:S(2)}) collective-permute-start(bf16[80,384]{1,0:T(8,128)(2,1)S(1)} %pad_maximum_fusion.7), channel_id=1, source_target_pairs={{0,2},{1,3},{2,0},{3,1},{4,6},{5,7},{6,4},{7,5},{8,10},{9,11},{10,... | collective-permute-start | bytes 184328 | tf_op jit(solution)/shard_map/ppermute | solution.py:257
  9.4 7.0 %collective-permute-start.2 = (bf16[80,384]{1,0:T(8,128)(2,1)S(1)}, bf16[80,384]{1,0:T(8,128)(2,1)S(1)}, u32[]{:S(2)}, u32[]{:S(2)}) collective-permute-start(bf16[80,384]{1,0:T(8,128)(2,1)S(1)} %pad_maximum_fusion.7), channel_id=1, source_target_pairs={{0,3},{1,0},{2,1},{3,2},{4,7},{5,4},{6,5},{7,6},{8,11},{9,8},{10,9... | collective-permute-start | bytes 184328 | tf_op jit(solution)/shard_map/ppermute | solution.py:257
  12.5 15.3 %collective-permute-start.6 = (bf16[3,72,384]{2,1,0:T(8,128)(2,1)S(1)}, bf16[3,72,384]{2,1,0:T(8,128)(2,1)S(1)}, u32[]{:S(2)}, u32[]{:S(2)}) collective-permute-start(bf16[3,72,384]{2,1,0:T(8,128)(2,1)S(1)} %pad_maximum_fusion.6), channel_id=1, source_target_pairs={{0,1},{1,2},{2,3},{3,0},{4,5},{5,6},{6,7},{7,4},{8,9},{9,10},{10,1... | collective-permute-start | bytes 497672 | tf_op jit(solution)/shard_map/ppermute | solution.py:257
  13.2 14.5 %collective-permute-start.7 = (bf16[3,72,384]{2,1,0:T(8,128)(2,1)S(1)}, bf16[3,72,384]{2,1,0:T(8,128)(2,1)S(1)}, u32[]{:S(2)}, u32[]{:S(2)}) collective-permute-start(bf16[3,72,384]{2,1,0:T(8,128)(2,1)S(1)} %pad_maximum_fusion.6), channel_id=1, source_target_pairs={{0,2},{1,3},{2,0},{3,1},{4,6},{5,7},{6,4},{7,5},{8,10},{9,11},{10,... | collective-permute-start | bytes 497672 | tf_op jit(solution)/shard_map/ppermute | solution.py:257
  13.5 14.2 %collective-permute-start.8 = (bf16[3,72,384]{2,1,0:T(8,128)(2,1)S(1)}, bf16[3,72,384]{2,1,0:T(8,128)(2,1)S(1)}, u32[]{:S(2)}, u32[]{:S(2)}) collective-permute-start(bf16[3,72,384]{2,1,0:T(8,128)(2,1)S(1)} %pad_maximum_fusion.6), channel_id=1, source_target_pairs={{0,3},{1,0},{2,1},{3,2},{4,7},{5,4},{6,5},{7,6},{8,11},{9,8},{10,9... | collective-permute-start | bytes 497672 | tf_op jit(solution)/shard_map/ppermute | solution.py:257
  18.0 7.1 %collective-permute-start.3 = (bf16[3,80,384]{2,1,0:T(8,128)(2,1)S(1)}, bf16[3,80,384]{2,1,0:T(8,128)(2,1)S(1)}, u32[]{:S(2)}, u32[]{:S(2)}) collective-permute-start(bf16[3,80,384]{2,1,0:T(8,128)(2,1)S(1)} %get-tuple-element.120), channel_id=1, source_target_pairs={{0,8},{4,12},{8,0},{12,4},{16,24},{20,28},{24,16},{28,20},{1,9},{5... | collective-permute-start | bytes 552968 | tf_op jit(solution)/shard_map/ppermute | solution.py:955
  27.9 13.8 %collective-permute-start.10 = (bf16[9,72,384]{2,1,0:T(8,128)(2,1)S(1)}, bf16[9,72,384]{2,1,0:T(8,128)(2,1)S(1)}, u32[]{:S(2)}, u32[]{:S(2)}) collective-permute-start(bf16[9,72,384]{2,1,0:T(8,128)(2,1)S(1)} %constant_dynamic-update-slice_fusion), channel_id=1, source_target_pairs={{0,16},{4,20},{8,24},{12,28},{16,0},{20,4},{24,8},{28,12},{1,17},{... | collective-permute-start | bytes 1493000 | tf_op jit(solution)/shard_map/ppermute | solution.py:955
  29.5 13.5 %collective-permute-start.9 = (bf16[9,72,384]{2,1,0:T(8,128)(2,1)S(1)}, bf16[9,72,384]{2,1,0:T(8,128)(2,1)S(1)}, u32[]{:S(2)}, u32[]{:S(2)}) collective-permute-start(bf16[9,72,384]{2,1,0:T(8,128)(2,1)S(1)} %constant_dynamic-update-slice_fusion), channel_id=1, source_target_pairs={{0,8},{4,12},{8,0},{12,4},{16,24},{20,28},{24,16},{28,20},{1,9},{5... | collective-permute-start | bytes 1493000 | tf_op jit(solution)/shard_map/ppermute | solution.py:955
  43.0 6.8 %collective-permute-start.12 = (bf16[4,72,384]{2,1,0:T(8,128)(2,1)S(1)}, bf16[4,72,384]{2,1,0:T(8,128)(2,1)S(1)}, u32[]{:S(2)}, u32[]{:S(2)}) collective-permute-start(bf16[4,72,384]{2,1,0:T(8,128)(2,1)S(1)} %slice.151), channel_id=1, source_target_pairs={{0,8},{4,12},{8,0},{12,4},{16,24},{20,28},{24,16},{28,20},{1,9},{5... | collective-permute-start | bytes 663560 | tf_op jit(solution)/shard_map/ppermute | solution.py:955
  44.6 7.7 %collective-permute-start.13 = (bf16[5,72,384]{2,1,0:T(8,128)(2,1)S(1)}, bf16[5,72,384]{2,1,0:T(8,128)(2,1)S(1)}, u32[]{:S(2)}, u32[]{:S(2)}) collective-permute-start(bf16[5,72,384]{2,1,0:T(8,128)(2,1)S(1)} %slice.152), channel_id=1, source_target_pairs={{0,16},{4,20},{8,24},{12,28},{16,0},{20,4},{24,8},{28,12},{1,17},{... | collective-permute-start | bytes 829448 | tf_op jit(solution)/shard_map/ppermute | solution.py:955
  85.3 17.0 %collective-permute-start.17 = (bf16[2,2,3,72,384]{4,3,2,1,0:T(8,128)(2,1)S(1)}, bf16[2,2,3,72,384]{4,3,2,1,0:T(8,128)(2,1)S(1)}, u32[]{:S(2)}, u32[]{:S(2)}) collective-permute-start(bf16[2,2,3,72,384]{4,3,2,1,0:T(8,128)(2,1)S(1)} %get-tuple-element.107), channel_id=1, source_target_pairs={{0,16},{4,20},{8,24},{12,28},{16,0},{20,4},{24,8},{28,12},{1,17},{... | collective-permute-start | bytes 1990664 | tf_op jit(solution)/shard_map/ppermute | solution.py:955
  86.0 16.7 %collective-permute-start.16 = (bf16[2,2,3,72,384]{4,3,2,1,0:T(8,128)(2,1)S(1)}, bf16[2,2,3,72,384]{4,3,2,1,0:T(8,128)(2,1)S(1)}, u32[]{:S(2)}, u32[]{:S(2)}) collective-permute-start(bf16[2,2,3,72,384]{4,3,2,1,0:T(8,128)(2,1)S(1)} %get-tuple-element.109), channel_id=1, source_target_pairs={{0,8},{4,12},{8,0},{12,4},{16,24},{20,28},{24,16},{28,20},{1,9},{5... | collective-permute-start | bytes 1990664 | tf_op jit(solution)/shard_map/ppermute | solution.py:955
  102.7 10.8 %collective-permute-start.20 = (bf16[4,4,80,384]{3,2,1,0:T(8,128)(2,1)}, bf16[4,4,80,384]{3,2,1,0:T(8,128)(2,1)S(1)}, u32[]{:S(2)}, u32[]{:S(2)}) collective-permute-start(bf16[4,4,80,384]{3,2,1,0:T(8,128)(2,1)} %get-tuple-element.88), channel_id=1, source_target_pairs={{0,4},{4,0},{8,12},{12,8},{16,20},{20,16},{24,28},{28,24},{1,5},{5... | collective-permute-start | bytes 2949128 | tf_op jit(solution)/shard_map/ppermute | solution.py:955
  102.7 10.3 %collective-permute-start.19 = (bf16[2,3,72,384]{3,2,1,0:T(8,128)(2,1)S(1)}, bf16[2,3,72,384]{3,2,1,0:T(8,128)(2,1)S(1)}, u32[]{:S(2)}, u32[]{:S(2)}) collective-permute-start(bf16[2,3,72,384]{3,2,1,0:T(8,128)(2,1)S(1)} %fusion.6), channel_id=1, source_target_pairs={{0,8},{4,12},{8,0},{12,4},{16,24},{20,28},{24,16},{28,20},{1,9},{5... | collective-permute-start | bytes 995336 | tf_op jit(solution)/shard_map/ppermute | solution.py:955
  103.4 10.0 %collective-permute-start.18 = (bf16[2,3,72,384]{3,2,1,0:T(8,128)(2,1)S(1)}, bf16[2,3,72,384]{3,2,1,0:T(8,128)(2,1)S(1)}, u32[]{:S(2)}, u32[]{:S(2)}) collective-permute-start(bf16[2,3,72,384]{3,2,1,0:T(8,128)(2,1)S(1)} %fusion.5), channel_id=1, source_target_pairs={{0,16},{4,20},{8,24},{12,28},{16,0},{20,4},{24,8},{28,12},{1,17},{... | collective-permute-start | bytes 995336 | tf_op jit(solution)/shard_map/ppermute | solution.py:955
  113.7 18.2 %collective-permute-start.25 = (bf16[2,2,80,384]{3,2,1,0:T(8,128)(2,1)S(1)}, bf16[2,2,80,384]{3,2,1,0:T(8,128)(2,1)S(1)}, u32[]{:S(2)}, u32[]{:S(2)}) collective-permute-start(bf16[2,2,80,384]{3,2,1,0:T(8,128)(2,1)S(1)} %get-tuple-element.111), channel_id=1, source_target_pairs={{0,16},{4,20},{8,24},{12,28},{16,0},{20,4},{24,8},{28,12},{1,17},{... | collective-permute-start | bytes 737288 | tf_op jit(solution)/shard_map/ppermute | solution.py:955
  115.2 16.7 %collective-permute-start.24 = (bf16[2,2,80,384]{3,2,1,0:T(8,128)(2,1)S(1)}, bf16[2,2,80,384]{3,2,1,0:T(8,128)(2,1)S(1)}, u32[]{:S(2)}, u32[]{:S(2)}) collective-permute-start(bf16[2,2,80,384]{3,2,1,0:T(8,128)(2,1)S(1)} %get-tuple-element.113), channel_id=1, source_target_pairs={{0,8},{4,12},{8,0},{12,4},{16,24},{20,28},{24,16},{28,20},{1,9},{5... | collective-permute-start | bytes 737288 | tf_op jit(solution)/shard_map/ppermute | solution.py:955
  116.9 13.2 %collective-permute-start.22 = (bf16[3,72,384]{2,1,0:T(8,128)(2,1)S(1)}, bf16[3,72,384]{2,1,0:T(8,128)(2,1)S(1)}, u32[]{:S(2)}, u32[]{:S(2)}) collective-permute-start(bf16[3,72,384]{2,1,0:T(8,128)(2,1)S(1)} %get-tuple-element.116), channel_id=1, source_target_pairs={{0,2},{1,3},{2,0},{3,1},{4,6},{5,7},{6,4},{7,5},{8,10},{9,11},{10,... | collective-permute-start | bytes 497672 | tf_op jit(solution)/shard_map/ppermute | solution.py:257
  118.9 11.1 %collective-permute-start.23 = (bf16[3,72,384]{2,1,0:T(8,128)(2,1)S(1)}, bf16[3,72,384]{2,1,0:T(8,128)(2,1)S(1)}, u32[]{:S(2)}, u32[]{:S(2)}) collective-permute-start(bf16[3,72,384]{2,1,0:T(8,128)(2,1)S(1)} %get-tuple-element.115), channel_id=1, source_target_pairs={{0,3},{1,0},{2,1},{3,2},{4,7},{5,4},{6,5},{7,6},{8,11},{9,8},{10,9... | collective-permute-start | bytes 497672 | tf_op jit(solution)/shard_map/ppermute | solution.py:257
  121.9 10.0 %collective-permute-start.21 = (bf16[3,72,384]{2,1,0:T(8,128)(2,1)S(1)}, bf16[3,72,384]{2,1,0:T(8,128)(2,1)S(1)}, u32[]{:S(2)}, u32[]{:S(2)}) collective-permute-start(bf16[3,72,384]{2,1,0:T(8,128)(2,1)S(1)} %fusion.16), channel_id=1, source_target_pairs={{0,1},{1,2},{2,3},{3,0},{4,5},{5,6},{6,7},{7,4},{8,9},{9,10},{10,1... | collective-permute-start | bytes 497672 | tf_op jit(solution)/shard_map/ppermute | solution.py:257
  132.5 9.1 %collective-permute-start.26 = (bf16[2,80,384]{2,1,0:T(8,128)(2,1)S(1)}, bf16[2,80,384]{2,1,0:T(8,128)(2,1)S(1)}, u32[]{:S(2)}, u32[]{:S(2)}) collective-permute-start(bf16[2,80,384]{2,1,0:T(8,128)(2,1)S(1)} %fusion.17), channel_id=1, source_target_pairs={{0,16},{4,20},{8,24},{12,28},{16,0},{20,4},{24,8},{28,12},{1,17},{... | collective-permute-start | bytes 368648 | tf_op jit(solution)/shard_map/ppermute | solution.py:955
  147.9 6.9 %collective-permute-start.32 = (bf16[4,72,384]{2,1,0:T(8,128)(2,1)S(1)}, bf16[4,72,384]{2,1,0:T(8,128)(2,1)S(1)}, u32[]{:S(2)}, u32[]{:S(2)}) collective-permute-start(bf16[4,72,384]{2,1,0:T(8,128)(2,1)S(1)} %get-tuple-element.118), channel_id=1, source_target_pairs={{0,16},{4,20},{8,24},{12,28},{16,0},{20,4},{24,8},{28,12},{1,17},{... | collective-permute-start | bytes 663560 | tf_op jit(solution)/shard_map/ppermute | solution.py:955
  148.6 7.1 %collective-permute-start.31 = (bf16[4,72,384]{2,1,0:T(8,128)(2,1)S(1)}, bf16[4,72,384]{2,1,0:T(8,128)(2,1)S(1)}, u32[]{:S(2)}, u32[]{:S(2)}) collective-permute-start(bf16[4,72,384]{2,1,0:T(8,128)(2,1)S(1)} %get-tuple-element.118), channel_id=1, source_target_pairs={{0,8},{4,12},{8,0},{12,4},{16,24},{20,28},{24,16},{28,20},{1,9},{5... | collective-permute-start | bytes 663560 | tf_op jit(solution)/shard_map/ppermute | solution.py:955
  (22 other events, 150.2 us)

commit v5 on v4

--- a/solution.py
+++ b/solution.py
@@ -1087,7 +1087,6 @@
     wide_blocks = own_blocks(*wide_one, *wide_two)
     attn_one = exchange_one(attn_keep, attn_came)
     wide_last = exchange_shards(wide_blocks)
-    wide_last, attn_one = barrier((wide_last, attn_one))
     wide_total = narrow(added(wide_blocks[0], wide_last))
     attn_two = exchange_two(*attn_one)
     attn_blocks = own_blocks(*attn_one, *attn_two)

time: 169 us -> 160 us (0.947)
  waiting for transfers between devices: 64.5 us -> 54.3 us
  starting transfers between devices: 42 us -> 44 us
    ppermute x12, waiting for transfers between devices: 14.7 us -> 3.92 us  [shifted(): lax.ppermute(values, 'shard', [(i, (i + steps) % size) for i in range(siz...]
    ppermute x24, starting transfers between devices: 20.1 us -> 25.4 us  [swapped(): return lax.ppermute(values, 'rep', [(i, i ^ bit) for i in range(size)])]
    ppermute x12, starting transfers between devices: 21.8 us -> 18.6 us  [shifted(): lax.ppermute(values, 'shard', [(i, (i + steps) % size) for i in range(siz...]
  transfers between devices with their start and end apart: 36 -> 36, of which waited for: 24 -> 24; matrix products, arithmetic and copies ran while one was open for 4% -> 4% of each run, Pallas kernels for 12% -> 13%
where the time goes in v5:
time: 160 us
  waiting for transfers between devices  54.3 us (34%)
  Pallas kernels  44.5 us (28%)
  starting transfers between devices  44 us (28%)
  local copies, waits for them, and re-layouts  9.13 us (6%)
  other arithmetic  6.98 us (4%)
    ppermute x24, waiting for transfers between devices, swapped(): return lax.ppermute(values, 'rep', [(i, i ^ bit) for i in range(size)])  50.4 us
    ppermute x24, starting transfers between devices, swapped(): return lax.ppermute(values, 'rep', [(i, i ^ bit) for i in range(size)])  25.4 us
    pallas_call x1, Pallas kernels, mlp(): pl.pallas_call(kernel, grid_spec=pltpu.PrefetchScalarGridSpec(num_scalar_...  19.5 us
    ppermute x12, starting transfers between devices, shifted(): lax.ppermute(values, 'shard', [(i, (i + steps) % size) for i in range(siz...  18.6 us
    pallas_call x1, Pallas kernels, attention_backward(): pl.pallas_call(kernel, grid_spec=pltpu.PrefetchScalarGridSpec(num_scalar_...  12.5 us
    pallas_call x1, Pallas kernels, attention_forward(): pl.pallas_call(kernel, grid_spec=pltpu.PrefetchScalarGridSpec(num_scalar_...  8.39 us
    pallas_call x1, Pallas kernels, unpack(): pl.pallas_call(unpack_kernel, grid_spec=pltpu.PrefetchScalarGridSpec(num_...  4.04 us
    ppermute x12, waiting for transfers between devices, shifted(): lax.ppermute(values, 'shard', [(i, (i + steps) % size) for i in range(siz...  3.92 us
  transfers between devices with their start and end apart: 36, of which 24 were waited for; matrix products, arithmetic and copies ran while one was open for 4% of the time, Pallas kernels for 13%

profile of v5, /device:TPU:0, one launch (start us, length us, event | category | flops | bytes accessed | tf_op | source)
XLA Modules:
  0.0 160.0 jit_solution(15951588970793286831)
XLA Ops:
  3.6 3.2 %collective-permute-start = (bf16[80,384]{1,0:T(8,128)(2,1)S(1)}, bf16[80,384]{1,0:T(8,128)(2,1)S(1)}, u32[]{:S(2)}, u32[]{:S(2)}) collective-permute-start(bf16[80,384]{1,0:T(8,128)(2,1)S(1)} %pad_maximum_fusion.7), channel_id=1, source_target_pairs={{0,1},{1,2},{2,3},{3,0},{4,5},{5,6},{6,7},{7,4},{8,9},{9,10},{10,1... | collective-permute-start | bytes 184328 | tf_op jit(solution)/shard_map/ppermute | solution.py:257
  6.8 2.6 %collective-permute-start.1 = (bf16[80,384]{1,0:T(8,128)(2,1)S(1)}, bf16[80,384]{1,0:T(8,128)(2,1)S(1)}, u32[]{:S(2)}, u32[]{:S(2)}) collective-permute-start(bf16[80,384]{1,0:T(8,128)(2,1)S(1)} %pad_maximum_fusion.7), channel_id=1, source_target_pairs={{0,2},{1,3},{2,0},{3,1},{4,6},{5,7},{6,4},{7,5},{8,10},{9,11},{10,... | collective-permute-start | bytes 184328 | tf_op jit(solution)/shard_map/ppermute | solution.py:257
  13.5 2.8 %collective-permute-start.8 = (bf16[3,72,384]{2,1,0:T(8,128)(2,1)S(1)}, bf16[3,72,384]{2,1,0:T(8,128)(2,1)S(1)}, u32[]{:S(2)}, u32[]{:S(2)}) collective-permute-start(bf16[3,72,384]{2,1,0:T(8,128)(2,1)S(1)} %pad_maximum_fusion.6), channel_id=1, source_target_pairs={{0,3},{1,0},{2,1},{3,2},{4,7},{5,4},{6,5},{7,6},{8,11},{9,8},{10,9... | collective-permute-start | bytes 497672 | tf_op jit(solution)/shard_map/ppermute | solution.py:257
  19.6 2.4 %collective-permute-done.4 = bf16[3,80,384]{2,1,0:T(8,128)(2,1)S(1)} collective-permute-done((bf16[3,80,384]{2,1,0:T(8,128)(2,1)S(1)}, bf16[3,80,384]{2,1,0:T(8,128)(2,1)S(1)}, u32[]{:S(2)}, u32[]{:S(2)}) %collective-permute-start.4) | collective-permute-done | bytes 184352 | tf_op jit(solution)/shard_map/ppermute | solution.py:955
  25.1 2.4 %collective-permute-done.5 = bf16[3,80,384]{2,1,0:T(8,128)(2,1)S(1)} collective-permute-done((bf16[3,80,384]{2,1,0:T(8,128)(2,1)S(1)}, bf16[3,80,384]{2,1,0:T(8,128)(2,1)S(1)}, u32[]{:S(2)}, u32[]{:S(2)}) %collective-permute-start.5) | collective-permute-done | bytes 184352 | tf_op jit(solution)/shard_map/ppermute | solution.py:955
  31.9 8.4 %attention_forward.1 = (bf16[576,1536]{1,0:T(8,128)(2,1)}, f32[576,128]{1,0:T(8,128)}, f32[576,384]{1,0:T(8,128)}, bf16[3,64,1152]{2,1,0:T(8,128)(2,1)}, bf16[3,...) custom-call(s32[3]{0:T(128)} %pad_add_fusion.refs_0_.at_ref, ...), custom_call_target="tpu_custom_call" | custom-call | flops 1500000000 | bytes 8000000 | tf_op jit(solution)/shard_map/attention_forward/pallas_call | solution.py:575
  45.2 4.6 %collective-permute-done.12 = bf16[4,72,384]{2,1,0:T(8,128)(2,1)S(1)} collective-permute-done((bf16[4,72,384]{2,1,0:T(8,128)(2,1)S(1)}, bf16[4,72,384]{2,1,0:T(8,128)(2,1)S(1)}, u32[]{:S(2)}, u32[]{:S(2)}) %collective-permute-start.12) | collective-permute-done | bytes 221216 | tf_op jit(solution)/shard_map/ppermute | solution.py:955
  49.8 2.5 %collective-permute-done.13 = bf16[5,72,384]{2,1,0:T(8,128)(2,1)S(1)} collective-permute-done((bf16[5,72,384]{2,1,0:T(8,128)(2,1)S(1)}, bf16[5,72,384]{2,1,0:T(8,128)(2,1)S(1)}, u32[]{:S(2)}, u32[]{:S(2)}) %collective-permute-start.13) | collective-permute-done | bytes 276512 | tf_op jit(solution)/shard_map/ppermute | solution.py:955
  54.3 2.4 %collective-permute-done.14 = bf16[4,9,72,384]{3,2,1,0:T(8,128)(2,1)S(1)} collective-permute-done((bf16[4,9,72,384]{3,2,1,0:T(8,128)(2,1)S(1)}, bf16[4,9,72,384]{3,2,1,0:T(8,128)(2,1)S(1)}, u32[]{:S(2)}, u32[]{:S(2)}) %collective-permute-start.14) | collective-permute-done | bytes 1990688 | tf_op jit(solution)/shard_map/ppermute | solution.py:955
  58.1 19.5 %mlp.1 = (bf16[576,384]{1,0:T(8,128)(2,1)}, f32[576,384]{1,0:T(8,128)}, f32[576,128]{1,0:T(8,128)}, bf16[4,4,3,72,384]{4,3,2,1,0:T(8,128)(2,1)}, bf16[4,4,3,72,384]{4,3,2,1,0:T(8,128)(2,1)}) custom-call(s32[3]{0:T(128)} %pad_add_fusion.refs_0_.at_ref, f32[576,384]{1,0:T(8,128)} %get-tuple-element.60.refs_1_, bf16[576,384]{1,0:T(8,128)(2,1)} %bitcast.188, ...), custom_call_target="tpu_custom_call" | custom-call | flops 6200000000 | bytes 14000000 | tf_op jit(solution)/shard_map/mlp/pallas_call | solution.py:705
  77.7 5.1 %collective-permute-done.15 = bf16[4,4,3,72,384]{4,3,2,1,0:T(8,128)(2,1)S(1)} collective-permute-done((bf16[4,4,3,72,384]{4,3,2,1,0:T(8,128)(2,1)}, bf16[4,4,3,72,384]{4,3,2,1,0:T(8,128)(2,1)S(1)}, u32[]{:S(2)}, u32[]{:S(2)}) %collective-permute-start.15) | collective-permute-done | bytes 2654240 | tf_op jit(solution)/shard_map/ppermute | solution.py:955
  86.5 12.5 %attention_backward.1 = (f32[576,384]{1,0:T(8,128)}, bf16[4,4,80,384]{3,2,1,0:T(8,128)(2,1)}, bf16[4,4,80,384]{3,2,1,0:T(8,128)(2,1)}) custom-call(s32[3]{0:T(128)} %pad_add_fusion.refs_0_.at_ref, bf16[576,384]{1,0:T(8,128)(2,1)} %bitcast.190, f32[576,384]{1,0:T(8,128)} %get-tuple-element.65.refs_2_, s32[1,384]{1,0:T(1,128)} %refs_3_.1, ...), custom_call_target="tpu_custom_call" | custom-call | flops 3000000000 | bytes 9000000 | tf_op jit(solution)/shard_map/attention_backward/pallas_call | solution.py:862
  99.1 3.3 %collective-permute-done.17 = bf16[2,2,3,72,384]{4,3,2,1,0:T(8,128)(2,1)S(1)} collective-permute-done((bf16[2,2,3,72,384]{4,3,2,1,0:T(8,128)(2,1)S(1)}, bf16[2,2,3,72,384]{4,3,2,1,0:T(8,128)(2,1)S(1)}, u32[]{:S(2)}, u32[]{:S(2)}) %collective-permute-start.17) | collective-permute-done | bytes 663584 | tf_op jit(solution)/shard_map/ppermute | solution.py:955
  104.9 8.1 %collective-permute-done.19 = bf16[2,3,72,384]{3,2,1,0:T(8,128)(2,1)S(1)} collective-permute-done((bf16[2,3,72,384]{3,2,1,0:T(8,128)(2,1)S(1)}, bf16[2,3,72,384]{3,2,1,0:T(8,128)(2,1)S(1)}, u32[]{:S(2)}, u32[]{:S(2)}) %collective-permute-start.19) | collective-permute-done | bytes 331808 | tf_op jit(solution)/shard_map/ppermute | solution.py:955
  113.6 2.1 %collective-permute-start.22 = (bf16[3,72,384]{2,1,0:T(8,128)(2,1)S(1)}, bf16[3,72,384]{2,1,0:T(8,128)(2,1)S(1)}, u32[]{:S(2)}, u32[]{:S(2)}) collective-permute-start(bf16[3,72,384]{2,1,0:T(8,128)(2,1)S(1)} %get-tuple-element.101), channel_id=1, source_target_pairs={{0,2},{1,3},{2,0},{3,1},{4,6},{5,7},{6,4},{7,5},{8,10},{9,11},{10,... | collective-permute-start | bytes 497672 | tf_op jit(solution)/shard_map/ppermute | solution.py:257
  115.7 2.8 %collective-permute-start.23 = (bf16[3,72,384]{2,1,0:T(8,128)(2,1)S(1)}, bf16[3,72,384]{2,1,0:T(8,128)(2,1)S(1)}, u32[]{:S(2)}, u32[]{:S(2)}) collective-permute-start(bf16[3,72,384]{2,1,0:T(8,128)(2,1)S(1)} %get-tuple-element.102), channel_id=1, source_target_pairs={{0,3},{1,0},{2,1},{3,2},{4,7},{5,4},{6,5},{7,6},{8,11},{9,8},{10,9... | collective-permute-start | bytes 497672 | tf_op jit(solution)/shard_map/ppermute | solution.py:257
  122.0 3.5 %collective-permute-done.27 = bf16[2,2,80,384]{3,2,1,0:T(8,128)(2,1)S(1)} collective-permute-done((bf16[2,2,80,384]{3,2,1,0:T(8,128)(2,1)S(1)}, bf16[2,2,80,384]{3,2,1,0:T(8,128)(2,1)S(1)}, u32[]{:S(2)}, u32[]{:S(2)}) %collective-permute-start.27) | collective-permute-done | bytes 245792 | tf_op jit(solution)/shard_map/ppermute | solution.py:955
  128.7 1.9 %collective-permute-done.28 = bf16[2,80,384]{2,1,0:T(8,128)(2,1)S(1)} collective-permute-done((bf16[2,80,384]{2,1,0:T(8,128)(2,1)S(1)}, bf16[2,80,384]{2,1,0:T(8,128)(2,1)S(1)}, u32[]{:S(2)}, u32[]{:S(2)}) %collective-permute-start.28) | collective-permute-done | bytes 122912 | tf_op jit(solution)/shard_map/ppermute | solution.py:955
  132.6 2.1 %collective-permute-start.26 = (bf16[80,384]{1,0:T(8,128)(2,1)S(1)}, bf16[80,384]{1,0:T(8,128)(2,1)S(1)}, u32[]{:S(2)}, u32[]{:S(2)}) collective-permute-start(bf16[80,384]{1,0:T(8,128)(2,1)S(1)} %fusion.26), channel_id=1, source_target_pairs={{0,1},{1,2},{2,3},{3,0},{4,5},{5,6},{6,7},{7,4},{8,9},{9,10},{10,1... | collective-permute-start | bytes 184328 | tf_op jit(solution)/shard_map/ppermute | solution.py:257
  136.7 1.9 %collective-permute-done.26 = bf16[80,384]{1,0:T(8,128)(2,1)S(1)} collective-permute-done((bf16[80,384]{1,0:T(8,128)(2,1)S(1)}, bf16[80,384]{1,0:T(8,128)(2,1)S(1)}, u32[]{:S(2)}, u32[]{:S(2)}) %collective-permute-start.26) | collective-permute-done | bytes 61472 | tf_op jit(solution)/shard_map/ppermute | solution.py:257
  141.6 3.8 %collective-permute-done.32 = bf16[4,72,384]{2,1,0:T(8,128)(2,1)S(1)} collective-permute-done((bf16[4,72,384]{2,1,0:T(8,128)(2,1)S(1)}, bf16[4,72,384]{2,1,0:T(8,128)(2,1)S(1)}, u32[]{:S(2)}, u32[]{:S(2)}) %collective-permute-start.32) | collective-permute-done | bytes 221216 | tf_op jit(solution)/shard_map/ppermute | solution.py:955
  145.5 2.0 %collective-permute-start.33 = (bf16[2,72,384]{2,1,0:T(8,128)(2,1)S(1)}, bf16[2,72,384]{2,1,0:T(8,128)(2,1)S(1)}, u32[]{:S(2)}, u32[]{:S(2)}) collective-permute-start(bf16[2,72,384]{2,1,0:T(8,128)(2,1)S(1)} %slice.236), channel_id=1, source_target_pairs={{0,8},{4,12},{8,0},{12,4},{16,24},{20,28},{24,16},{28,20},{1,9},{5... | collective-permute-start | bytes 331784 | tf_op jit(solution)/shard_map/ppermute | solution.py:955
  150.3 2.1 %collective-permute-done.34 = bf16[2,72,384]{2,1,0:T(8,128)(2,1)S(1)} collective-permute-done((bf16[2,72,384]{2,1,0:T(8,128)(2,1)S(1)}, bf16[2,72,384]{2,1,0:T(8,128)(2,1)S(1)}, u32[]{:S(2)}, u32[]{:S(2)}) %collective-permute-start.34) | collective-permute-done | bytes 110624 | tf_op jit(solution)/shard_map/ppermute | solution.py:955
  156.0 4.0 %unpack.1 = (f32[144,1536]{1,0:T(8,128)}, f32[144,1536]{1,0:T(8,128)}, f32[576,384]{1,0:T(8,128)}, f32[144,576]{1,0:T(8,128)}, f32[144,192]{1,0:T(8,128)}, /*index=5*/f32[144,192]{1,0:T(8,128)}, f32[144,576]{1,0:T(8,128)}) custom-call(s32[3]{0:T(128)} %pad_add_fusion.refs_0_.at_ref, bf16[4,4,72,384]{3,2,1,0:T(8,128)(2,1)} %copy-done, ...), custom_call_target="tpu_custom_call" | custom-call | tf_op jit(solution)/shard_map/unpack/pallas_call | solution.py:921
  (127 shorter events, 52.9 us)
Async XLA Ops:
  3.6 9.9 %collective-permute-start = (bf16[80,384]{1,0:T(8,128)(2,1)S(1)}, bf16[80,384]{1,0:T(8,128)(2,1)S(1)}, u32[]{:S(2)}, u32[]{:S(2)}) collective-permute-start(bf16[80,384]{1,0:T(8,128)(2,1)S(1)} %pad_maximum_fusion.7), channel_id=1, source_target_pairs={{0,1},{1,2},{2,3},{3,0},{4,5},{5,6},{6,7},{7,4},{8,9},{9,10},{10,1... | collective-permute-start | bytes 184328 | tf_op jit(solution)/shard_map/ppermute | solution.py:257
  6.8 9.5 %collective-permute-start.1 = (bf16[80,384]{1,0:T(8,128)(2,1)S(1)}, bf16[80,384]{1,0:T(8,128)(2,1)S(1)}, u32[]{:S(2)}, u32[]{:S(2)}) collective-permute-start(bf16[80,384]{1,0:T(8,128)(2,1)S(1)} %pad_maximum_fusion.7), channel_id=1, source_target_pairs={{0,2},{1,3},{2,0},{3,1},{4,6},{5,7},{6,4},{7,5},{8,10},{9,11},{10,... | collective-permute-start | bytes 184328 | tf_op jit(solution)/shard_map/ppermute | solution.py:257
  9.4 7.0 %collective-permute-start.2 = (bf16[80,384]{1,0:T(8,128)(2,1)S(1)}, bf16[80,384]{1,0:T(8,128)(2,1)S(1)}, u32[]{:S(2)}, u32[]{:S(2)}) collective-permute-start(bf16[80,384]{1,0:T(8,128)(2,1)S(1)} %pad_maximum_fusion.7), channel_id=1, source_target_pairs={{0,3},{1,0},{2,1},{3,2},{4,7},{5,4},{6,5},{7,6},{8,11},{9,8},{10,9... | collective-permute-start | bytes 184328 | tf_op jit(solution)/shard_map/ppermute | solution.py:257
  12.5 15.3 %collective-permute-start.6 = (bf16[3,72,384]{2,1,0:T(8,128)(2,1)S(1)}, bf16[3,72,384]{2,1,0:T(8,128)(2,1)S(1)}, u32[]{:S(2)}, u32[]{:S(2)}) collective-permute-start(bf16[3,72,384]{2,1,0:T(8,128)(2,1)S(1)} %pad_maximum_fusion.6), channel_id=1, source_target_pairs={{0,1},{1,2},{2,3},{3,0},{4,5},{5,6},{6,7},{7,4},{8,9},{9,10},{10,1... | collective-permute-start | bytes 497672 | tf_op jit(solution)/shard_map/ppermute | solution.py:257
  13.2 14.5 %collective-permute-start.7 = (bf16[3,72,384]{2,1,0:T(8,128)(2,1)S(1)}, bf16[3,72,384]{2,1,0:T(8,128)(2,1)S(1)}, u32[]{:S(2)}, u32[]{:S(2)}) collective-permute-start(bf16[3,72,384]{2,1,0:T(8,128)(2,1)S(1)} %pad_maximum_fusion.6), channel_id=1, source_target_pairs={{0,2},{1,3},{2,0},{3,1},{4,6},{5,7},{6,4},{7,5},{8,10},{9,11},{10,... | collective-permute-start | bytes 497672 | tf_op jit(solution)/shard_map/ppermute | solution.py:257
  13.5 14.2 %collective-permute-start.8 = (bf16[3,72,384]{2,1,0:T(8,128)(2,1)S(1)}, bf16[3,72,384]{2,1,0:T(8,128)(2,1)S(1)}, u32[]{:S(2)}, u32[]{:S(2)}) collective-permute-start(bf16[3,72,384]{2,1,0:T(8,128)(2,1)S(1)} %pad_maximum_fusion.6), channel_id=1, source_target_pairs={{0,3},{1,0},{2,1},{3,2},{4,7},{5,4},{6,5},{7,6},{8,11},{9,8},{10,9... | collective-permute-start | bytes 497672 | tf_op jit(solution)/shard_map/ppermute | solution.py:257
  18.0 7.1 %collective-permute-start.3 = (bf16[3,80,384]{2,1,0:T(8,128)(2,1)S(1)}, bf16[3,80,384]{2,1,0:T(8,128)(2,1)S(1)}, u32[]{:S(2)}, u32[]{:S(2)}) collective-permute-start(bf16[3,80,384]{2,1,0:T(8,128)(2,1)S(1)} %get-tuple-element.106), channel_id=1, source_target_pairs={{0,8},{4,12},{8,0},{12,4},{16,24},{20,28},{24,16},{28,20},{1,9},{5... | collective-permute-start | bytes 552968 | tf_op jit(solution)/shard_map/ppermute | solution.py:955
  27.9 13.8 %collective-permute-start.10 = (bf16[9,72,384]{2,1,0:T(8,128)(2,1)S(1)}, bf16[9,72,384]{2,1,0:T(8,128)(2,1)S(1)}, u32[]{:S(2)}, u32[]{:S(2)}) collective-permute-start(bf16[9,72,384]{2,1,0:T(8,128)(2,1)S(1)} %constant_dynamic-update-slice_fusion), channel_id=1, source_target_pairs={{0,16},{4,20},{8,24},{12,28},{16,0},{20,4},{24,8},{28,12},{1,17},{... | collective-permute-start | bytes 1493000 | tf_op jit(solution)/shard_map/ppermute | solution.py:955
  29.5 13.5 %collective-permute-start.9 = (bf16[9,72,384]{2,1,0:T(8,128)(2,1)S(1)}, bf16[9,72,384]{2,1,0:T(8,128)(2,1)S(1)}, u32[]{:S(2)}, u32[]{:S(2)}) collective-permute-start(bf16[9,72,384]{2,1,0:T(8,128)(2,1)S(1)} %constant_dynamic-update-slice_fusion), channel_id=1, source_target_pairs={{0,8},{4,12},{8,0},{12,4},{16,24},{20,28},{24,16},{28,20},{1,9},{5... | collective-permute-start | bytes 1493000 | tf_op jit(solution)/shard_map/ppermute | solution.py:955
  43.0 6.8 %collective-permute-start.12 = (bf16[4,72,384]{2,1,0:T(8,128)(2,1)S(1)}, bf16[4,72,384]{2,1,0:T(8,128)(2,1)S(1)}, u32[]{:S(2)}, u32[]{:S(2)}) collective-permute-start(bf16[4,72,384]{2,1,0:T(8,128)(2,1)S(1)} %slice.155), channel_id=1, source_target_pairs={{0,8},{4,12},{8,0},{12,4},{16,24},{20,28},{24,16},{28,20},{1,9},{5... | collective-permute-start | bytes 663560 | tf_op jit(solution)/shard_map/ppermute | solution.py:955
  44.6 7.7 %collective-permute-start.13 = (bf16[5,72,384]{2,1,0:T(8,128)(2,1)S(1)}, bf16[5,72,384]{2,1,0:T(8,128)(2,1)S(1)}, u32[]{:S(2)}, u32[]{:S(2)}) collective-permute-start(bf16[5,72,384]{2,1,0:T(8,128)(2,1)S(1)} %slice.156), channel_id=1, source_target_pairs={{0,16},{4,20},{8,24},{12,28},{16,0},{20,4},{24,8},{28,12},{1,17},{... | collective-permute-start | bytes 829448 | tf_op jit(solution)/shard_map/ppermute | solution.py:955
  85.3 17.0 %collective-permute-start.17 = (bf16[2,2,3,72,384]{4,3,2,1,0:T(8,128)(2,1)S(1)}, bf16[2,2,3,72,384]{4,3,2,1,0:T(8,128)(2,1)S(1)}, u32[]{:S(2)}, u32[]{:S(2)}) collective-permute-start(bf16[2,2,3,72,384]{4,3,2,1,0:T(8,128)(2,1)S(1)} %get-tuple-element.93), channel_id=1, source_target_pairs={{0,16},{4,20},{8,24},{12,28},{16,0},{20,4},{24,8},{28,12},{1,17},{... | collective-permute-start | bytes 1990664 | tf_op jit(solution)/shard_map/ppermute | solution.py:955
  86.0 16.7 %collective-permute-start.16 = (bf16[2,2,3,72,384]{4,3,2,1,0:T(8,128)(2,1)S(1)}, bf16[2,2,3,72,384]{4,3,2,1,0:T(8,128)(2,1)S(1)}, u32[]{:S(2)}, u32[]{:S(2)}) collective-permute-start(bf16[2,2,3,72,384]{4,3,2,1,0:T(8,128)(2,1)S(1)} %get-tuple-element.95), channel_id=1, source_target_pairs={{0,8},{4,12},{8,0},{12,4},{16,24},{20,28},{24,16},{28,20},{1,9},{5... | collective-permute-start | bytes 1990664 | tf_op jit(solution)/shard_map/ppermute | solution.py:955
  102.7 10.8 %collective-permute-start.20 = (bf16[4,4,80,384]{3,2,1,0:T(8,128)(2,1)}, bf16[4,4,80,384]{3,2,1,0:T(8,128)(2,1)S(1)}, u32[]{:S(2)}, u32[]{:S(2)}) collective-permute-start(bf16[4,4,80,384]{3,2,1,0:T(8,128)(2,1)} %get-tuple-element.81), channel_id=1, source_target_pairs={{0,4},{4,0},{8,12},{12,8},{16,20},{20,16},{24,28},{28,24},{1,5},{5... | collective-permute-start | bytes 2949128 | tf_op jit(solution)/shard_map/ppermute | solution.py:955
  102.7 10.3 %collective-permute-start.19 = (bf16[2,3,72,384]{3,2,1,0:T(8,128)(2,1)S(1)}, bf16[2,3,72,384]{3,2,1,0:T(8,128)(2,1)S(1)}, u32[]{:S(2)}, u32[]{:S(2)}) collective-permute-start(bf16[2,3,72,384]{3,2,1,0:T(8,128)(2,1)S(1)} %fusion.6), channel_id=1, source_target_pairs={{0,8},{4,12},{8,0},{12,4},{16,24},{20,28},{24,16},{28,20},{1,9},{5... | collective-permute-start | bytes 995336 | tf_op jit(solution)/shard_map/ppermute | solution.py:955
  103.4 10.0 %collective-permute-start.18 = (bf16[2,3,72,384]{3,2,1,0:T(8,128)(2,1)S(1)}, bf16[2,3,72,384]{3,2,1,0:T(8,128)(2,1)S(1)}, u32[]{:S(2)}, u32[]{:S(2)}) collective-permute-start(bf16[2,3,72,384]{3,2,1,0:T(8,128)(2,1)S(1)} %fusion.5), channel_id=1, source_target_pairs={{0,16},{4,20},{8,24},{12,28},{16,0},{20,4},{24,8},{28,12},{1,17},{... | collective-permute-start | bytes 995336 | tf_op jit(solution)/shard_map/ppermute | solution.py:955
  113.6 19.0 %collective-permute-start.22 = (bf16[3,72,384]{2,1,0:T(8,128)(2,1)S(1)}, bf16[3,72,384]{2,1,0:T(8,128)(2,1)S(1)}, u32[]{:S(2)}, u32[]{:S(2)}) collective-permute-start(bf16[3,72,384]{2,1,0:T(8,128)(2,1)S(1)} %get-tuple-element.101), channel_id=1, source_target_pairs={{0,2},{1,3},{2,0},{3,1},{4,6},{5,7},{6,4},{7,5},{8,10},{9,11},{10,... | collective-permute-start | bytes 497672 | tf_op jit(solution)/shard_map/ppermute | solution.py:257
  115.7 19.0 %collective-permute-start.23 = (bf16[3,72,384]{2,1,0:T(8,128)(2,1)S(1)}, bf16[3,72,384]{2,1,0:T(8,128)(2,1)S(1)}, u32[]{:S(2)}, u32[]{:S(2)}) collective-permute-start(bf16[3,72,384]{2,1,0:T(8,128)(2,1)S(1)} %get-tuple-element.102), channel_id=1, source_target_pairs={{0,3},{1,0},{2,1},{3,2},{4,7},{5,4},{6,5},{7,6},{8,11},{9,8},{10,9... | collective-permute-start | bytes 497672 | tf_op jit(solution)/shard_map/ppermute | solution.py:257
  118.8 6.8 %collective-permute-start.27 = (bf16[2,2,80,384]{3,2,1,0:T(8,128)(2,1)S(1)}, bf16[2,2,80,384]{3,2,1,0:T(8,128)(2,1)S(1)}, u32[]{:S(2)}, u32[]{:S(2)}) collective-permute-start(bf16[2,2,80,384]{3,2,1,0:T(8,128)(2,1)S(1)} %get-tuple-element.98), channel_id=1, source_target_pairs={{0,16},{4,20},{8,24},{12,28},{16,0},{20,4},{24,8},{28,12},{1,17},{... | collective-permute-start | bytes 737288 | tf_op jit(solution)/shard_map/ppermute | solution.py:955
  120.4 7.1 %collective-permute-start.24 = (bf16[2,2,80,384]{3,2,1,0:T(8,128)(2,1)S(1)}, bf16[2,2,80,384]{3,2,1,0:T(8,128)(2,1)S(1)}, u32[]{:S(2)}, u32[]{:S(2)}) collective-permute-start(bf16[2,2,80,384]{3,2,1,0:T(8,128)(2,1)S(1)} %get-tuple-element.100), channel_id=1, source_target_pairs={{0,8},{4,12},{8,0},{12,4},{16,24},{20,28},{24,16},{28,20},{1,9},{5... | collective-permute-start | bytes 737288 | tf_op jit(solution)/shard_map/ppermute | solution.py:955
  122.0 12.7 %collective-permute-start.21 = (bf16[3,72,384]{2,1,0:T(8,128)(2,1)S(1)}, bf16[3,72,384]{2,1,0:T(8,128)(2,1)S(1)}, u32[]{:S(2)}, u32[]{:S(2)}) collective-permute-start(bf16[3,72,384]{2,1,0:T(8,128)(2,1)S(1)} %fusion.20), channel_id=1, source_target_pairs={{0,1},{1,2},{2,3},{3,0},{4,5},{5,6},{6,7},{7,4},{8,9},{9,10},{10,1... | collective-permute-start | bytes 497672 | tf_op jit(solution)/shard_map/ppermute | solution.py:257
  132.6 6.1 %collective-permute-start.26 = (bf16[80,384]{1,0:T(8,128)(2,1)S(1)}, bf16[80,384]{1,0:T(8,128)(2,1)S(1)}, u32[]{:S(2)}, u32[]{:S(2)}) collective-permute-start(bf16[80,384]{1,0:T(8,128)(2,1)S(1)} %fusion.26), channel_id=1, source_target_pairs={{0,1},{1,2},{2,3},{3,0},{4,5},{5,6},{6,7},{7,4},{8,9},{9,10},{10,1... | collective-permute-start | bytes 184328 | tf_op jit(solution)/shard_map/ppermute | solution.py:257
  138.8 6.7 %collective-permute-start.32 = (bf16[4,72,384]{2,1,0:T(8,128)(2,1)S(1)}, bf16[4,72,384]{2,1,0:T(8,128)(2,1)S(1)}, u32[]{:S(2)}, u32[]{:S(2)}) collective-permute-start(bf16[4,72,384]{2,1,0:T(8,128)(2,1)S(1)} %get-tuple-element.104), channel_id=1, source_target_pairs={{0,16},{4,20},{8,24},{12,28},{16,0},{20,4},{24,8},{28,12},{1,17},{... | collective-permute-start | bytes 663560 | tf_op jit(solution)/shard_map/ppermute | solution.py:955
  140.2 7.4 %collective-permute-start.31 = (bf16[4,72,384]{2,1,0:T(8,128)(2,1)S(1)}, bf16[4,72,384]{2,1,0:T(8,128)(2,1)S(1)}, u32[]{:S(2)}, u32[]{:S(2)}) collective-permute-start(bf16[4,72,384]{2,1,0:T(8,128)(2,1)S(1)} %get-tuple-element.104), channel_id=1, source_target_pairs={{0,8},{4,12},{8,0},{12,4},{16,24},{20,28},{24,16},{28,20},{1,9},{5... | collective-permute-start | bytes 663560 | tf_op jit(solution)/shard_map/ppermute | solution.py:955
  (22 other events, 148.7 us)
